TPU v7x, 256 devices: a whole 4x4x8 slice. The times are simulated.
256 devices in a mesh: grp: 4 (over x), pen: 64 (over y, z, core).
Axes of the slice: x: 4, y: 4, z: 8, core: 2. Of those that a mesh axis runs over, the one named last changes fastest.
Arguments:
- occupancy: int32 [256, 512, 256], P('grp', 'pen'), may hold values from 0 to 11, as said below
- embedding: float32 [12, 16], replicated, may hold values from -6 to 6
- spectral_weight: float32 [256, 16, 2, 16, 16], P(('grp', 'pen')), may hold values from -1.5 to 1.5
- point_weight: float32 [16, 16], replicated, may hold values from -1.5 to 1.5
- point_bias: float32 [16], replicated, may hold values from -3 to 3
- expand_weight: bfloat16 [16, 64], replicated, may hold values from -1.5 to 1.5
- expand_bias: float32 [64], replicated, may hold values from -3 to 3
- reduce_weight: bfloat16 [64, 16], replicated, may hold values from -0.75 to 0.75
- reduce_bias: float32 [16], replicated, may hold values from -3 to 3
Outputs:
- encoded: bfloat16 [16, 256, 512, 256], P(None, 'grp', 'pen')
Inputs may be any that keep to these rules, and one draw needn't show every extreme that they name: `occupancy`: each cell holds one of 12 class labels.
All inputs are finite; a program needn't handle non-finite values.
Results may differ from a plain program's by a relative error of at most 0.001.
The roundings to bfloat16 on the way count: a program that leaves them out, or rounds other values in their place, can miss the bound.
Values may be sent and summed in bfloat16 or wider, within the bound.
No kernel may reach another device: no remote copies, remote signals or barrier semaphores. Data moves between devices by JAX's collectives and lax.ppermute only.
A program may use at most 128 MiB of HBM per device.

v0:
```python
import functools
import math

import jax
import jax.numpy as jnp
import ml_dtypes
import numpy as np
from jax import lax
from jax.experimental import pallas as pl
from jax.experimental.pallas import tpu as pltpu
from jax.sharding import PartitionSpec as P

NZ = 256
NX = 512
NY = 256
CH = 16
MODES = 16
NCLASS = 12
HIDDEN = 64
LZ = 64
LX = 8
ROWS = LZ * LX

highest = lax.Precision.HIGHEST
f32 = jnp.float32
bf16 = jnp.bfloat16
FREQ = np.where(np.arange(MODES) < 8, np.arange(MODES), np.arange(MODES) - MODES)


def split(values):
    hi = values.astype(ml_dtypes.bfloat16)
    lo = (values - hi.astype(np.float64)).astype(ml_dtypes.bfloat16)
    return hi, lo


def y_tables():
    product = np.remainder(FREQ[:, None] * np.arange(NY)[None, :], NY)
    angles = product.astype(np.float32) * np.float32(2.0 * math.pi / NY)
    cos = np.cos(angles).astype(ml_dtypes.bfloat16)
    sin = np.sin(angles).astype(ml_dtypes.bfloat16)
    return np.stack([cos, -sin], axis=1).reshape(2 * MODES, NY)


def plane_tables():
    z = np.arange(LZ)
    x = np.arange(LX)
    turn = (
        2 * FREQ[None, :, None, None] * z[None, None, :, None]
        + FREQ[:, None, None, None] * x[None, None, None, :]
    )
    angles = 2.0 * np.pi * np.remainder(turn, NX) / NX
    table = np.stack([np.cos(angles), np.sin(angles)])
    return table.reshape(2 * MODES * MODES, ROWS)


def pen_phases():
    turn = np.remainder(np.arange(64)[:, None] * FREQ[None, :], 64)
    angles = 2.0 * np.pi * turn / 64
    return np.concatenate([np.cos(angles), np.sin(angles)], axis=1).astype(np.float32)


def iota(shape, axis):
    return lax.broadcasted_iota(jnp.int32, shape, axis)


def times_j(tile):
    imag_lane = (iota(tile.shape, 1) // 16) % 2 == 1
    return jnp.where(imag_lane, pltpu.roll(tile, 16, 1), -pltpu.roll(tile, 112, 1))


def swap_blocks(tile):
    row = iota(tile.shape, 0) % 4
    block = iota(tile.shape, 1) // 32
    out = tile
    for step in (-3, -2, -1, 1, 2, 3):
        moved = pltpu.roll(pltpu.roll(tile, (-step) % 16, 0), (32 * step) % 128, 1)
        out = jnp.where(block - row == step, moved, out)
    return out


def to_parts(values):
    hi = values.astype(bf16)
    lo = (values - hi.astype(f32)).astype(bf16)
    return hi, lo


def dot(left, right, dims=((1,), (0,)), precision=None):
    return lax.dot_general(
        left, right, (dims, ((), ())), precision=precision, preferred_element_type=f32
    )


def forward_kernel(occ_ref, ytab_ref, hi_ref, lo_ref, out_ref, rows_ref):
    rows_ref[...] = jnp.zeros_like(rows_ref)
    labels = occ_ref[...]
    for label in range(NCLASS):
        hot = jnp.where(labels == label, 1.0, 0.0).astype(bf16)
        part = dot(ytab_ref[...], hot, ((1,), (1,)))
        for quarter in range(4):
            rows_ref[quarter, pl.ds(label, 32, stride=16), :] = part[
                :, quarter * 128 : (quarter + 1) * 128
            ]
    for group in range(4):
        block = [rows_ref[quarter, pl.ds(group * 128, 128), :] for quarter in range(4)]
        block_hi, block_lo = to_parts(jnp.concatenate(block, axis=1))
        nt = ((1,), (1,))
        full = (
            dot(hi_ref[...], block_hi, nt)
            + dot(hi_ref[...], block_lo, nt)
            + dot(lo_ref[...], block_hi, nt)
        )
        out_ref[group] = full[:256] - times_j(full[256:])


def gather_groups_kernel(phase_ref, in_ref, out_ref, mid_ref):
    quarter = iota((16, 128), 0) % 4
    zero = jnp.zeros((16, 128), f32)
    for kx in range(MODES):
        tiles = [in_ref[g, pl.ds(kx * 16, 16), :] for g in range(4)]
        real = zero
        imag = zero
        for g in range(4):
            turn = (quarter * g) % 4
            real = real + jnp.where(turn == 0, tiles[g], jnp.where(turn == 2, -tiles[g], zero))
            imag = imag + jnp.where(turn == 3, tiles[g], jnp.where(turn == 1, -tiles[g], zero))
        cos = phase_ref[kx]
        sin = phase_ref[16 + kx]
        tile = (real * cos + imag * sin) + times_j(imag * cos - real * sin)
        mid_ref[pl.ds(kx * 16, 16), :] = swap_blocks(tile)
    for q in range(4):
        out_ref[pl.ds(q * 64, 64), :] = mid_ref[pl.ds(q, 64, stride=4), :]


def mix_kernel(in_ref, weight_ref, emb_ref, rep_ref, out_ref):
    total = in_ref[0:8, :]
    for step in range(1, 32):
        total = total + in_ref[pl.ds(step * 8, 8), :]
    total = total + pltpu.roll(total, 4, 0)
    left = jnp.where(iota((128, NCLASS), 0) % 16 == iota((128, NCLASS), 1), 1.0, 0.0).astype(f32)
    right = jnp.where(iota((16, 128), 1) % 16 == iota((16, 128), 0), 1.0, 0.0).astype(f32)
    wide = dot(dot(left, emb_ref[...], precision=highest), right, precision=highest)
    wide = jnp.where(iota((128, 128), 0) // 16 == iota((128, 128), 1) // 16, wide, 0.0)
    lifted = dot(total, wide, precision=highest)
    first = lifted.astype(bf16)
    rest = lifted - first.astype(f32)
    second = rest.astype(bf16)
    third = (rest - second.astype(f32)).astype(bf16)
    rep = rep_ref[...]
    spread = dot(first, rep) + dot(second, rep) + dot(third, rep)
    weight = jnp.concatenate([weight_ref[...], weight_ref[...]], axis=0)
    pieces = []
    for k in range(4):
        s_real = spread[:, k * 512 : k * 512 + 256]
        s_imag = spread[:, k * 512 + 256 : k * 512 + 512]
        w_real = weight[:, k * 512 : k * 512 + 256]
        w_imag = weight[:, k * 512 + 256 : k * 512 + 512]
        pieces.append(w_real * s_real - w_imag * s_imag)
        pieces.append(w_real * s_imag + w_imag * s_real)
    acc = jnp.zeros((8, 128), f32)
    spot = iota((256, 128), 1)
    source = iota((256, 128), 0) % 16
    for n in range(8):
        pick = jnp.where(spot == source + 16 * n, 1.0, 0.0).astype(f32)
        acc = acc + dot(pieces[n], pick, precision=highest)
    acc = acc * (1.0 / (NZ * NX * NY))
    for step in range(32):
        out_ref[pl.ds(step * 8, 8), :] = acc


def scatter_groups_kernel(phase_ref, in_ref, out_ref, mid_ref):
    quarter = iota((16, 128), 0) % 4
    zero = jnp.zeros((16, 128), f32)
    for q in range(4):
        mid_ref[pl.ds(q, 64, stride=4), :] = in_ref[pl.ds(q * 64, 64), :]
    for kx in range(MODES):
        tile = swap_blocks(mid_ref[pl.ds(kx * 16, 16), :])
        turned = times_j(tile)
        cos = phase_ref[kx]
        sin = phase_ref[16 + kx]
        real = tile * cos + turned * sin
        imag = turned * cos - tile * sin
        for g in range(4):
            turn = (quarter * g) % 4
            out_ref[g, pl.ds(kx * 16, 16), :] = jnp.where(
                turn == 0, real, jnp.where(turn == 1, imag, jnp.where(turn == 2, -real, -imag))
            )


def gelu(values):
    half = values * 0.5
    return half + half * lax.erf(values * np.float32(math.sqrt(0.5)))


ZB = 4


def point_kernel(
    modes_ref, hi_ref, lo_ref, ytab_ref, occ_ref, emb_ref, pw_ref, pb_ref, w1_ref, b1_ref, w2_ref,
    b2_ref, out_ref, planes_ref, table_ref, wide1_ref, wide2_ref, bias1_ref, bias2_ref,
):
    @pl.when(pl.program_id(0) == 0)
    def _():
        hi = hi_ref[...]
        lo = lo_ref[...]
        for g in range(4):
            tile = modes_ref[g]
            both = jnp.concatenate([tile, times_j(tile)], axis=0)
            part_hi, part_lo = to_parts(both)
            full = dot(hi, part_hi) + dot(hi, part_lo) + dot(lo, part_hi)
            planes_ref[:, pl.ds(g * 128, 128)] = full.astype(bf16).astype(f32)
        table = dot(pw_ref[...], emb_ref[...], ((0,), (1,)), highest)
        spread = jnp.where(
            iota((NCLASS, 128), 0) == iota((NCLASS, 128), 1), 1.0, 0.0
        ).astype(f32)
        eye = iota((16, 16), 0) == iota((16, 16), 1)
        bias = jnp.sum(jnp.where(eye, pb_ref[...], 0.0), axis=1, keepdims=True)
        table_ref[...] = dot(table, spread, precision=highest) + bias
        r1 = jnp.where(iota((512, 64), 0) % 64 == iota((512, 64), 1), 1.0, 0.0)
        r2 = jnp.where(iota((16, 128), 1) % 16 == iota((16, 128), 0), 1.0, 0.0).astype(bf16)
        a1 = dot(r1.astype(bf16), w1_ref[...], ((1,), (1,))).astype(bf16)
        full1 = dot(a1, r2)
        same1 = iota((512, 128), 0) // 64 == iota((512, 128), 1) // 16
        wide1_ref[...] = jnp.where(same1, full1, 0.0).astype(bf16)
        col1 = jnp.sum(r1 * b1_ref[...], axis=1, keepdims=True)
        bias1_ref[...] = jnp.broadcast_to(col1, (512, 128))
        r3 = jnp.where(iota((128, 16), 0) // 8 == iota((128, 16), 1), 1.0, 0.0)
        r4 = jnp.where(iota((64, 512), 1) % 64 == iota((64, 512), 0), 1.0, 0.0).astype(bf16)
        a2 = dot(r3.astype(bf16), w2_ref[...], ((1,), (1,))).astype(bf16)
        full2 = dot(a2, r4)
        same2 = iota((128, 512), 0) % 8 == iota((128, 512), 1) // 64
        wide2_ref[...] = jnp.where(same2, full2, 0.0).astype(bf16)
        col2 = jnp.sum(r3 * b2_ref[...], axis=1, keepdims=True)
        bias2_ref[...] = jnp.broadcast_to(col2, (128, 128))

    own = iota((16, 512), 0) == iota((16, 512), 1) % 16
    table = table_ref[...]
    bias1 = jnp.concatenate([bias1_ref[...]] * 2, axis=1)
    bias2 = jnp.concatenate([bias2_ref[...]] * 2, axis=1)
    for zi in range(ZB):
        base = pl.multiple_of((pl.program_id(0) * ZB + zi) * 8, 8)
        left = []
        point = []
        rows = planes_ref[pl.ds(base, 8), :]
        labels = occ_ref[pl.ds(base, 8), :]
        for x in range(LX):
            row = jnp.broadcast_to(rows[x : x + 1], (16, 512))
            left.append(jnp.where(own, row, 0.0).astype(bf16))
            for half in range(2):
                label = jnp.broadcast_to(
                    labels[x : x + 1, half * 128 : (half + 1) * 128], (16, 128)
                )
                point.append(jnp.take_along_axis(table, label, axis=1))
        left = jnp.concatenate(left, axis=0)
        pointwise = jnp.concatenate(
            [jnp.concatenate(point[0::2], axis=0), jnp.concatenate(point[1::2], axis=0)], axis=1
        )
        spatial = dot(left, ytab_ref[...])
        activated = gelu(spatial + pointwise).astype(bf16)
        hidden = gelu(dot(wide1_ref[...], activated) + bias1).astype(bf16)
        encoded = dot(wide2_ref[...], hidden) + bias2
        out_ref[:, zi] = encoded.reshape(16, 8, 256).astype(bf16)


def vmem():
    return pl.BlockSpec(memory_space=pltpu.VMEM)


def smem():
    return pl.BlockSpec(memory_space=pltpu.SMEM)


def shards(
    occupancy,
    embedding,
    spectral_weight,
    point_weight,
    point_bias,
    expand_weight,
    expand_bias,
    reduce_weight,
    reduce_bias,
):
    ytab = y_tables()
    hi, lo = split(plane_tables())
    labels = occupancy.reshape(ROWS, NY)
    phases = lax.dynamic_slice_in_dim(jnp.asarray(pen_phases()), lax.axis_index("pen"), 1, 0)[0]
    partial = pl.pallas_call(
        forward_kernel,
        out_shape=jax.ShapeDtypeStruct((4, 256, 128), f32),
        in_specs=[vmem()] * 4,
        out_specs=vmem(),
        scratch_shapes=[pltpu.VMEM((4, 512, 128), f32)],
        name="forward",
    )(labels, jnp.asarray(ytab), jnp.asarray(hi), jnp.asarray(lo))
    partial = lax.all_to_all(partial, "grp", 0, 0, tiled=True)
    chunks = pl.pallas_call(
        gather_groups_kernel,
        out_shape=jax.ShapeDtypeStruct((256, 128), f32),
        in_specs=[smem(), vmem()],
        out_specs=vmem(),
        scratch_shapes=[pltpu.VMEM((256, 128), f32)],
        name="gather_groups",
    )(phases, partial)
    chunks = lax.all_to_all(chunks.reshape(64, 4, 128), "pen", 0, 0, tiled=True)
    rep = (np.arange(2048)[None, :] // 16 == np.arange(128)[:, None]).astype(ml_dtypes.bfloat16)
    mixed = pl.pallas_call(
        mix_kernel,
        out_shape=jax.ShapeDtypeStruct((256, 128), f32),
        in_specs=[vmem()] * 4,
        out_specs=vmem(),
        name="mix",
    )(chunks.reshape(256, 128), spectral_weight.reshape(4, 2048), embedding, jnp.asarray(rep))
    mixed = lax.all_to_all(mixed.reshape(64, 4, 128), "pen", 0, 0, tiled=True)
    modes = pl.pallas_call(
        scatter_groups_kernel,
        out_shape=jax.ShapeDtypeStruct((4, 256, 128), f32),
        in_specs=[smem(), vmem()],
        out_specs=vmem(),
        scratch_shapes=[pltpu.VMEM((256, 128), f32)],
        name="scatter_groups",
    )(phases, mixed.reshape(256, 128))
    modes = lax.all_to_all(modes, "grp", 0, 0, tiled=True)
    whole = lambda *shape: pl.BlockSpec(shape, lambda i: (0,) * len(shape))
    return pl.pallas_call(
        point_kernel,
        out_shape=jax.ShapeDtypeStruct((CH, LZ, LX, NY), bf16),
        grid=(LZ // ZB,),
        in_specs=[
            whole(4, 256, 128),
            whole(512, 512),
            whole(512, 512),
            whole(512, 256),
            whole(512, 256),
            whole(NCLASS, CH),
            whole(CH, CH),
            whole(1, CH),
            whole(CH, HIDDEN),
            whole(1, HIDDEN),
            whole(HIDDEN, CH),
            whole(1, CH),
        ],
        out_specs=pl.BlockSpec((CH, ZB, LX, NY), lambda i: (0, i, 0, 0)),
        scratch_shapes=[
            pltpu.VMEM((512, 512), f32),
            pltpu.VMEM((16, 128), f32),
            pltpu.VMEM((512, 128), bf16),
            pltpu.VMEM((128, 512), bf16),
            pltpu.VMEM((512, 128), f32),
            pltpu.VMEM((128, 128), f32),
        ],
        name="point",
    )(
        modes,
        jnp.asarray(hi.T.copy()),
        jnp.asarray(lo.T.copy()),
        jnp.asarray(np.repeat(ytab, 16, axis=0)),
        labels,
        embedding,
        point_weight,
        point_bias.reshape(1, CH),
        expand_weight,
        expand_bias.reshape(1, HIDDEN),
        reduce_weight,
        reduce_bias.reshape(1, CH),
    )


def solution(mesh):
    return jax.shard_map(
        shards,
        mesh=mesh,
        in_specs=(
            P("grp", "pen", None),
            P(),
            P(("grp", "pen"), None, None, None, None),
            P(),
            P(),
            P(),
            P(),
            P(),
            P(),
        ),
        out_specs=P(None, "grp", "pen", None),
        check_vma=False,
    )
```

profile of v0, /device:TPU:1, one launch (start us, length us, event | category | flops | bytes accessed | tf_op | source)
XLA Modules:
  0.0 118.6 jit_solution(5662002155002550244)
XLA Ops:
  0.0 0.0 copy-start.3
  0.0 0.0 copy-start.4
  0.0 5.4 %forward.1 = f32[4,256,128]{2,1,0:T(8,128)} custom-call(s32[512,256]{1,0:T(8,128)} %bitcast.12, bf16[32,256]{1,0:T(8,128)(2,1)} %constant.25.clone.ytab_ref, bf16[512,512]{1,0:T(8,128)(2,1)} %constant.26.clone.hi_ref, bf16[512,512]{1,0:T(8,128)(2,1)} %constant.27.clone.lo_ref), custom_call_target="tpu_custom_call" | custom-call | tf_op jit(solution)/shard_map/forward/pallas_call | solution.py:287
  5.4 4.8 %all-to-all-start = ((f32[4,256,128]{2,1,0:T(8,128)}), f32[4,256,128]{2,1,0:T(8,128)S(1)}, u32[]{:S(2)}, u32[]{:S(2)}) async-start(f32[4,256,128]{2,1,0:T(8,128)} %forward.1), calls=%async_computation | async-start | bytes 1048576 | tf_op jit(solution)/shard_map/all_to_all | solution.py:295
  10.2 1.2 %dynamic-slice_bitcast_fusion.phase_ref = f32[32]{0:T(128)} fusion(f32[64,32]{1,0:T(8,128)} %constant.24.clone, s32[]{:T(128)S(6)} %select_n.3), kind=kLoop, calls=%fused_computation | loop fusion | bytes 260 | tf_op jit(solution)/shard_map/squeeze | solution.py:286
  11.4 6.2 %all-to-all-done.in_ref = f32[4,256,128]{2,1,0:T(8,128)S(1)} async-done(((f32[4,256,128]{2,1,0:T(8,128)}), f32[4,256,128]{2,1,0:T(8,128)S(1)}, u32[]{:S(2)}, u32[]{:S(2)}) %all-to-all-start) | async-done | bytes 524320 | tf_op jit(solution)/shard_map/all_to_all | solution.py:295
  17.6 0.0 copy-start.1
  17.6 0.8 copy-done.1
  18.4 2.5 %gather_groups.1 = f32[256,128]{1,0:T(8,128)} custom-call(f32[32]{0:T(128)} %dynamic-slice_bitcast_fusion.phase_ref, f32[4,256,128]{2,1,0:T(8,128)} %copy-done.1), custom_call_target="tpu_custom_call" | custom-call | tf_op jit(solution)/shard_map/gather_groups/pallas_call | solution.py:296
  20.9 14.7 %all-to-all-start.1 = ((f32[64,4,128]{2,1,0:T(4,128)}), f32[64,4,128]{2,1,0:T(4,128)S(1)}, u32[]{:S(2)}, u32[]{:S(2)}) async-start(f32[64,4,128]{2,1,0:T(4,128)} %bitcast.16), calls=%async_computation.1 | async-start | bytes 262144 | tf_op jit(solution)/shard_map/all_to_all | solution.py:304
  35.7 0.0 copy-done.3
  35.7 0.8 reshape.30.weight_ref
  36.4 9.6 %all-to-all-done.1 = f32[64,4,128]{2,1,0:T(4,128)S(1)} async-done(((f32[64,4,128]{2,1,0:T(4,128)}), f32[64,4,128]{2,1,0:T(4,128)S(1)}, u32[]{:S(2)}, u32[]{:S(2)}) %all-to-all-start.1) | async-done | bytes 131104 | tf_op jit(solution)/shard_map/all_to_all | solution.py:304
  46.0 0.0 copy-start.2
  46.0 0.7 copy-done.2
  46.7 3.5 %mix.1 = f32[256,128]{1,0:T(8,128)} custom-call(f32[256,128]{1,0:T(8,128)} %bitcast.14, f32[4,2048]{1,0:T(4,128)} %reshape.30.weight_ref, f32[12,16]{1,0:T(8,128)} %emb_ref.3, bf16[128,2048]{1,0:T(8,128)(2,1)} %constant.28.clone.rep_ref), custom_call_target="tpu_custom_call" | custom-call | tf_op jit(solution)/shard_map/mix/pallas_call | solution.py:306
  50.2 15.7 %all_to_all.20 = f32[64,4,128]{2,1,0:T(4,128)} all-to-all(f32[64,4,128]{2,1,0:T(4,128)} %bitcast.15), channel_id=1, replica_groups=mesh['grp'=4,'pen'=64] {'pen'}, dimensions={0} | all-to-all | bytes 262144 | tf_op jit(solution)/shard_map/all_to_all | solution.py:313
  65.8 2.6 %scatter_groups.1 = f32[4,256,128]{2,1,0:T(8,128)} custom-call(f32[32]{0:T(128)} %dynamic-slice_bitcast_fusion.phase_ref, f32[256,128]{1,0:T(8,128)} %bitcast.17), custom_call_target="tpu_custom_call" | custom-call | tf_op jit(solution)/shard_map/scatter_groups/pallas_call | solution.py:314
  68.5 3.5 %all-to-all-start.3 = ((f32[4,256,128]{2,1,0:T(8,128)}), f32[4,256,128]{2,1,0:T(8,128)S(1)}, u32[]{:S(2)}, u32[]{:S(2)}) async-start(f32[4,256,128]{2,1,0:T(8,128)} %scatter_groups.1), calls=%async_computation.3 | async-start | bytes 1048576 | tf_op jit(solution)/shard_map/all_to_all | solution.py:322
  71.9 0.0 copy-done.4
  71.9 0.7 copy.18.w2_ref
  72.6 8.5 %all-to-all-done.3.modes_ref = f32[4,256,128]{2,1,0:T(8,128)S(1)} async-done(((f32[4,256,128]{2,1,0:T(8,128)}), f32[4,256,128]{2,1,0:T(8,128)S(1)}, u32[]{:S(2)}, u32[]{:S(2)}) %all-to-all-start.3) | async-done | bytes 524320 | tf_op jit(solution)/shard_map/all_to_all | solution.py:322
  81.1 0.0 copy-start
  81.1 0.8 copy-done
  81.9 36.7 %point.1 = bf16[16,64,8,256]{3,2,1,0:T(8,128)(2,1)} custom-call(f32[4,256,128]{2,1,0:T(8,128)} %copy-done, bf16[512,512]{1,0:T(8,128)(2,1)} %constant.29.clone.hi_ref, bf16[512,512]{1,0:T(8,128)(2,1)} %constant.30.clone.lo_ref, bf16[512,256]{1,0:T(8,128)(2,1)} %constant.31.clone.ytab_ref, s32[512,256]{1,0:T(8,128)} %bitcast.13, f32[12,16]{1,0:T(8,128)} %emb_ref.3, ...), custom_call_target="tpu_custom_call" | custom-call | tf_op jit(solution)/shard_map/point/pallas_call | solution.py:324
Async XLA Ops:
  0.0 35.7 %copy-start.3 = (f32[1,16,2,16,16]{4,3,2,1,0:T(8,128)S(1)}, f32[1,16,2,16,16]{4,3,2,1,0:T(8,128)}, u32[]{:S(2)}) copy-start(f32[1,16,2,16,16]{4,3,2,1,0:T(8,128)} %param.19) | copy-start | bytes 98308
  0.0 71.9 %copy-start.4 = (bf16[64,16]{0,1:T(8,128)(2,1)S(1)}, bf16[64,16]{0,1:T(8,128)(2,1)}, u32[]{:S(2)}) copy-start(bf16[64,16]{0,1:T(8,128)(2,1)} %param.24) | copy-start | bytes 6148
  5.4 12.2 %all-to-all-start = ((f32[4,256,128]{2,1,0:T(8,128)}), f32[4,256,128]{2,1,0:T(8,128)S(1)}, u32[]{:S(2)}, u32[]{:S(2)}) async-start(f32[4,256,128]{2,1,0:T(8,128)} %forward.1), calls=%async_computation | async-start | bytes 1048576 | tf_op jit(solution)/shard_map/all_to_all | solution.py:295
  17.6 0.8 copy-start.1
  20.9 25.1 %all-to-all-start.1 = ((f32[64,4,128]{2,1,0:T(4,128)}), f32[64,4,128]{2,1,0:T(4,128)S(1)}, u32[]{:S(2)}, u32[]{:S(2)}) async-start(f32[64,4,128]{2,1,0:T(4,128)} %bitcast.16), calls=%async_computation.1 | async-start | bytes 262144 | tf_op jit(solution)/shard_map/all_to_all | solution.py:304
  46.0 0.7 copy-start.2
  68.5 12.6 %all-to-all-start.3 = ((f32[4,256,128]{2,1,0:T(8,128)}), f32[4,256,128]{2,1,0:T(8,128)S(1)}, u32[]{:S(2)}, u32[]{:S(2)}) async-start(f32[4,256,128]{2,1,0:T(8,128)} %scatter_groups.1), calls=%async_computation.3 | async-start | bytes 1048576 | tf_op jit(solution)/shard_map/all_to_all | solution.py:322
  81.1 0.8 copy-start
where the time goes:
time: 119 us
  Pallas kernels  50.8 us (43%)
  waiting for transfers between devices  24.2 us (20%)
  starting transfers between devices  23 us (19%)
  blocking collectives  15.7 us (13%)
  local copies, waits for them, and re-layouts  4.92 us (4%)
    pallas_call x1, Pallas kernels, shards(): pl.pallas_call(point_kernel, out_shape=jax.ShapeDtypeStruct((CH, LZ, LX,...  36.7 us
    all_to_all x1, blocking collectives, shards(): mixed = lax.all_to_all(mixed.reshape(64, 4, 128), 'pen', 0, 0, tiled=True)  15.7 us
    all_to_all x1, starting transfers between devices, shards(): chunks = lax.all_to_all(chunks.reshape(64, 4, 128), 'pen', 0, 0, tiled=True)  14.7 us
    all_to_all x1, waiting for transfers between devices, shards(): chunks = lax.all_to_all(chunks.reshape(64, 4, 128), 'pen', 0, 0, tiled=True)  9.58 us
    all_to_all x1, waiting for transfers between devices, shards(): modes = lax.all_to_all(modes, 'grp', 0, 0, tiled=True)  8.46 us
    all_to_all x1, waiting for transfers between devices, shards(): partial = lax.all_to_all(partial, 'grp', 0, 0, tiled=True)  6.17 us
    pallas_call x1, Pallas kernels, shards(): pl.pallas_call(forward_kernel, out_shape=jax.ShapeDtypeStruct((4, 256, 12...  5.38 us
    all_to_all x1, starting transfers between devices, shards(): partial = lax.all_to_all(partial, 'grp', 0, 0, tiled=True)  4.84 us
  transfers between devices with their start and end apart: 3, of which 3 were waited for; matrix products, arithmetic and copies ran while one was open for 2% of the time, Pallas kernels for 0%

commit v1 on v0

v1 whole, which is shorter than its diff:
```python
import functools
import math

import jax
import jax.numpy as jnp
import ml_dtypes
import numpy as np
from jax import lax
from jax.experimental import pallas as pl
from jax.experimental.pallas import tpu as pltpu
from jax.sharding import PartitionSpec as P

NZ = 256
NX = 512
NY = 256
CH = 16
MODES = 16
NCLASS = 12
HIDDEN = 64
LZ = 64
LX = 8
ROWS = LZ * LX

highest = lax.Precision.HIGHEST
f32 = jnp.float32
bf16 = jnp.bfloat16
FREQ = np.where(np.arange(MODES) < 8, np.arange(MODES), np.arange(MODES) - MODES)


def split(values):
    hi = values.astype(ml_dtypes.bfloat16)
    lo = (values - hi.astype(np.float64)).astype(ml_dtypes.bfloat16)
    return hi, lo


def y_tables():
    product = np.remainder(FREQ[:, None] * np.arange(NY)[None, :], NY)
    angles = product.astype(np.float32) * np.float32(2.0 * math.pi / NY)
    cos = np.cos(angles).astype(ml_dtypes.bfloat16)
    sin = np.sin(angles).astype(ml_dtypes.bfloat16)
    return np.stack([cos, -sin], axis=1).reshape(2 * MODES, NY)


def z_tables():
    angles = 2.0 * np.pi * np.remainder(FREQ[None, :] * np.arange(LZ)[:, None], NZ) / NZ
    table = np.zeros((LZ, LX, 2, LX, MODES))
    for x in range(LX):
        table[:, x, 0, x] = np.cos(angles)
        table[:, x, 1, x] = np.sin(angles)
    return table.reshape(ROWS, 2 * LX * MODES)


def x_tables():
    angles = 2.0 * np.pi * np.remainder(FREQ[None, :] * np.arange(LX)[:, None], NX) / NX
    table = np.zeros((2, LX, MODES, MODES, MODES))
    for kz in range(MODES):
        table[0, :, kz, :, kz] = np.cos(angles)
        table[1, :, kz, :, kz] = np.sin(angles)
    return table.reshape(2, LX * MODES, MODES * MODES)


def y_lanes(ytab):
    table = ytab.reshape(2, 2, 4, 2, NY)
    table = np.moveaxis(table, (0, 1, 2, 3), (0, 3, 1, 2))
    return np.repeat(table.reshape(2 * MODES, NY), 8, axis=0)


def pen_phases():
    turn = np.remainder(np.arange(64)[:, None] * FREQ[None, :], 64)
    angles = 2.0 * np.pi * turn / 64
    return np.concatenate([np.cos(angles), np.sin(angles)], axis=1).astype(np.float32)


def iota(shape, axis):
    return lax.broadcasted_iota(jnp.int32, shape, axis)


def times_j(tile):
    imag_lane = (iota(tile.shape, 1) // 16) % 2 == 1
    return jnp.where(imag_lane, pltpu.roll(tile, 16, 1), -pltpu.roll(tile, 112, 1))


def swap_blocks(tile):
    row = iota(tile.shape, 0) % 4
    block = iota(tile.shape, 1) // 32
    out = tile
    for step in (-3, -2, -1, 1, 2, 3):
        moved = pltpu.roll(pltpu.roll(tile, (-step) % 16, 0), (32 * step) % 128, 1)
        out = jnp.where(block - row == step, moved, out)
    return out


def to_parts(values):
    hi = values.astype(bf16)
    lo = (values - hi.astype(f32)).astype(bf16)
    return hi, lo


def dot(left, right, dims=((1,), (0,)), precision=None):
    return lax.dot_general(
        left, right, (dims, ((), ())), precision=precision, preferred_element_type=f32
    )


def three(hi, lo, right):
    right_hi, right_lo = to_parts(right)
    return dot(hi, right_hi) + dot(hi, right_lo) + dot(lo, right_hi)


def forward_kernel(occ_ref, ytab_ref, hi_ref, lo_ref, out_ref, rows_ref):
    rows_ref[...] = jnp.zeros_like(rows_ref)
    labels = occ_ref[...]
    for label in range(NCLASS):
        hot = jnp.where(labels == label, 1.0, 0.0).astype(bf16)
        part = dot(ytab_ref[...], hot, ((1,), (1,)))
        for quarter in range(4):
            rows_ref[quarter, pl.ds(label, 32, stride=16), :] = part[
                :, quarter * 128 : (quarter + 1) * 128
            ]
    for group in range(4):
        block = [rows_ref[quarter, pl.ds(group * 128, 128), :] for quarter in range(4)]
        block_hi, block_lo = to_parts(jnp.concatenate(block, axis=1))
        nt = ((1,), (1,))
        full = (
            dot(hi_ref[...], block_hi, nt)
            + dot(hi_ref[...], block_lo, nt)
            + dot(lo_ref[...], block_hi, nt)
        )
        out_ref[group] = full[:128] - times_j(full[128:])


def gather_groups_kernel(phase_ref, hi_ref, lo_ref, in_ref, out_ref, mid_ref):
    spot = lax.axis_index("pen") * 32
    quarter = iota((128, 128), 0) % 4
    tiles = [in_ref[g] for g in range(4)]
    real = tiles[0]
    imag = jnp.zeros((128, 128), f32)
    for g in range(1, 4):
        turn = (quarter * g) % 4
        real = real + jnp.where(turn == 0, tiles[g], jnp.where(turn == 2, -tiles[g], 0.0))
        imag = imag + jnp.where(turn == 3, tiles[g], jnp.where(turn == 1, -tiles[g], 0.0))
    real = real + times_j(imag)
    both = three(hi_ref[...], lo_ref[...], jnp.concatenate([real, -times_j(real)], axis=0))
    turned = times_j(both)
    for kx in range(MODES):
        cos = phase_ref[spot + kx]
        sin = phase_ref[spot + 16 + kx]
        tile = both[kx * 16 : kx * 16 + 16] * cos - turned[kx * 16 : kx * 16 + 16] * sin
        mid_ref[pl.ds(kx * 16, 16), :] = swap_blocks(tile)
    for q in range(4):
        out_ref[pl.ds(q * 64, 64), :] = mid_ref[pl.ds(q, 64, stride=4), :]


def mix_kernel(in_ref, weight_ref, emb_ref, rep_ref, out_ref):
    total = in_ref[0:8, :]
    for step in range(1, 32):
        total = total + in_ref[pl.ds(step * 8, 8), :]
    total = total + pltpu.roll(total, 4, 0)
    left = jnp.where(iota((128, NCLASS), 0) % 16 == iota((128, NCLASS), 1), 1.0, 0.0).astype(f32)
    right = jnp.where(iota((16, 128), 1) % 16 == iota((16, 128), 0), 1.0, 0.0).astype(f32)
    wide = dot(dot(left, emb_ref[...], precision=highest), right, precision=highest)
    wide = jnp.where(iota((128, 128), 0) // 16 == iota((128, 128), 1) // 16, wide, 0.0)
    lifted = dot(total, wide, precision=highest)
    first = lifted.astype(bf16)
    rest = lifted - first.astype(f32)
    second = rest.astype(bf16)
    third = (rest - second.astype(f32)).astype(bf16)
    rep = rep_ref[...]
    spread = dot(first, rep) + dot(second, rep) + dot(third, rep)
    weight = jnp.concatenate([weight_ref[...], weight_ref[...]], axis=0)
    pieces = []
    for k in range(4):
        s_real = spread[:, k * 512 : k * 512 + 256]
        s_imag = spread[:, k * 512 + 256 : k * 512 + 512]
        w_real = weight[:, k * 512 : k * 512 + 256]
        w_imag = weight[:, k * 512 + 256 : k * 512 + 512]
        pieces.append(w_real * s_real - w_imag * s_imag)
        pieces.append(w_real * s_imag + w_imag * s_real)
    acc = jnp.zeros((8, 128), f32)
    spot = iota((256, 128), 1)
    source = iota((256, 128), 0) % 16
    for n in range(8):
        pick = jnp.where(spot == source + 16 * n, 1.0, 0.0).astype(f32)
        acc = acc + dot(pieces[n], pick, precision=highest)
    acc = acc * (1.0 / (NZ * NX * NY))
    for step in range(32):
        out_ref[pl.ds(step * 8, 8), :] = acc


def scatter_groups_kernel(phase_ref, hi_ref, lo_ref, in_ref, out_ref, mid_ref):
    spot = lax.axis_index("pen") * 32
    for q in range(4):
        mid_ref[pl.ds(q, 64, stride=4), :] = in_ref[pl.ds(q * 64, 64), :]
    real = []
    imag = []
    for kx in range(MODES):
        tile = swap_blocks(mid_ref[pl.ds(kx * 16, 16), :])
        turned = times_j(tile)
        cos = phase_ref[spot + kx]
        sin = phase_ref[spot + 16 + kx]
        real.append(tile * cos + turned * sin)
        imag.append(turned * cos - tile * sin)
    real = three(hi_ref[...], lo_ref[...], jnp.concatenate(real + imag, axis=0))
    imag = times_j(real)
    quarter = iota((128, 128), 0) % 4
    for g in range(4):
        turn = (quarter * g) % 4
        out_ref[g] = jnp.where(
            turn == 0, real, jnp.where(turn == 1, imag, jnp.where(turn == 2, -real, -imag))
        )


def twice_gelu(values):
    return values + values * lax.erf(values * np.float32(math.sqrt(0.5)))


ZB = 4


def point_kernel(
    modes_ref, hi_ref, lo_ref, ytab_ref, occ_ref, emb_ref, pw_ref, pb_ref, w1_ref, b1_ref, w2_ref,
    b2_ref, out_ref, planes_ref, table_ref, wide1_ref, wide2_ref, bias2_ref, label_ref,
):
    @pl.when(pl.program_id(0) == 0)
    def _():
        for half in range(2):
            label_ref[half] = occ_ref[:, half * 128 : (half + 1) * 128]
        hi = hi_ref[...]
        lo = lo_ref[...]
        high_lane = (iota((128, 128), 1) // 8) % 2 == 1
        for pair in range(2):
            even = modes_ref[2 * pair]
            odd = modes_ref[2 * pair + 1]
            for c_hi in range(2):
                if c_hi == 0:
                    tile = jnp.where(high_lane, pltpu.roll(odd, 8, 1), even)
                else:
                    tile = jnp.where(high_lane, odd, pltpu.roll(even, 120, 1))
                full = three(hi, lo, jnp.concatenate([tile, times_j(tile)], axis=0))
                planes_ref[c_hi * 2 + pair] = full.astype(bf16).astype(f32)
        table = dot(pw_ref[...], emb_ref[...], ((0,), (1,)), highest)
        spread = jnp.where(
            iota((NCLASS, 128), 0) == iota((NCLASS, 128), 1), 1.0, 0.0
        ).astype(f32)
        eye = iota((16, 16), 0) == iota((16, 16), 1)
        bias = jnp.sum(jnp.where(eye, pb_ref[...], 0.0), axis=1, keepdims=True)
        table_ref[...] = dot(table, spread, precision=highest) + bias
        r1 = jnp.where(iota((512, 64), 0) % 64 == iota((512, 64), 1), 1.0, 0.0)
        r2 = jnp.where(iota((16, 128), 1) % 16 == iota((16, 128), 0), 0.5, 0.0).astype(bf16)
        a1 = dot(r1.astype(bf16), w1_ref[...], ((1,), (1,))).astype(bf16)
        full1 = dot(a1, r2)
        same1 = iota((512, 128), 0) // 64 == iota((512, 128), 1) // 16
        wide1_ref[:, 0:128] = jnp.where(same1, full1, 0.0).astype(bf16)
        col1 = jnp.sum(r1 * b1_ref[...], axis=1, keepdims=True)
        first = col1.astype(bf16).astype(f32)
        second = (col1 - first).astype(bf16).astype(f32)
        third = col1 - first - second
        lane = iota((512, 128), 1)
        wide1_ref[:, 128:256] = jnp.where(
            lane == 0, first, jnp.where(lane == 1, second, jnp.where(lane == 2, third, 0.0))
        ).astype(bf16)
        r3 = jnp.where(iota((128, 16), 0) // 8 == iota((128, 16), 1), 1.0, 0.0)
        r4 = jnp.where(iota((64, 512), 1) % 64 == iota((64, 512), 0), 0.5, 0.0).astype(bf16)
        a2 = dot(r3.astype(bf16), w2_ref[...]).astype(bf16)
        full2 = dot(a2, r4)
        same2 = iota((128, 512), 0) % 8 == iota((128, 512), 1) // 64
        wide2_ref[...] = jnp.where(same2, full2, 0.0).astype(bf16)
        col2 = jnp.sum(r3 * b2_ref[...], axis=1, keepdims=True)
        bias2_ref[...] = jnp.broadcast_to(col2, (128, 128))

    own = jnp.where(iota((16, 256), 0) % 8 == iota((16, 256), 1) % 8, 1.0, 0.0).astype(bf16)
    low = table_ref[0:8, :]
    high = table_ref[8:16, :]
    ones = jnp.ones((16, 256), bf16)
    bias2 = jnp.concatenate([bias2_ref[...]] * 2, axis=1)
    left = []
    for zi in range(ZB):
        base = pl.multiple_of((pl.program_id(0) * ZB + zi) * 8, 8)
        for x in range(LX):
            rows = [planes_ref[t, pl.ds(base + x, 8, stride=0), :] for t in range(4)]
            block = jnp.concatenate(
                [jnp.concatenate(rows[0:2], axis=1), jnp.concatenate(rows[2:4], axis=1)], axis=0
            )
            left.append(block.astype(bf16) * own)
    spatial = dot(jnp.concatenate(left, axis=0), ytab_ref[...])
    for zi in range(ZB):
        base = pl.multiple_of((pl.program_id(0) * ZB + zi) * 8, 8)
        point = []
        for x in range(LX):
            halves = []
            for half in range(2):
                label = label_ref[half, pl.ds(base + x, 8, stride=0), :]
                halves.append(
                    jnp.concatenate(
                        [
                            jnp.take_along_axis(low, label, axis=1),
                            jnp.take_along_axis(high, label, axis=1),
                        ],
                        axis=0,
                    )
                )
            point.append(jnp.concatenate(halves, axis=1))
        pointwise = jnp.concatenate(point, axis=0)
        activated = twice_gelu(spatial[zi * 128 : zi * 128 + 128] + pointwise).astype(bf16)
        hidden = dot(wide1_ref[:, 0:144], jnp.concatenate([activated, ones], axis=0))
        hidden = twice_gelu(hidden).astype(bf16)
        encoded = dot(wide2_ref[...], hidden) + bias2
        out_ref[:, zi] = encoded.reshape(16, 8, 256).astype(bf16)


def room(mib):
    return pltpu.CompilerParams(vmem_limit_bytes=mib * 1024 * 1024)


def vmem():
    return pl.BlockSpec(memory_space=pltpu.VMEM)


def smem():
    return pl.BlockSpec(memory_space=pltpu.SMEM)


def shards(
    occupancy,
    embedding,
    spectral_weight,
    point_weight,
    point_bias,
    expand_weight,
    expand_bias,
    reduce_weight,
    reduce_bias,
):
    ytab = y_tables()
    z_hi, z_lo = split(z_tables())
    x_hi, x_lo = split(x_tables())
    x_in = [jnp.asarray(t.transpose(2, 0, 1).reshape(256, 256)) for t in (x_hi, x_lo)]
    x_out = [jnp.asarray(t.transpose(1, 0, 2).reshape(128, 512)) for t in (x_hi, x_lo)]
    labels = occupancy.reshape(ROWS, NY)
    phases = jnp.asarray(pen_phases().reshape(-1))
    partial = pl.pallas_call(
        forward_kernel,
        out_shape=jax.ShapeDtypeStruct((4, 128, 128), f32),
        in_specs=[vmem()] * 4,
        out_specs=vmem(),
        scratch_shapes=[pltpu.VMEM((4, 512, 128), f32)],
        compiler_params=room(16),
        name="forward",
    )(labels, jnp.asarray(ytab), jnp.asarray(z_hi.T.copy()), jnp.asarray(z_lo.T.copy()))
    weight = spectral_weight.reshape(4, 2048)
    partial, weight = lax.optimization_barrier((partial, weight))
    partial = lax.all_to_all(partial, "grp", 0, 0, tiled=True)
    chunks = pl.pallas_call(
        gather_groups_kernel,
        out_shape=jax.ShapeDtypeStruct((256, 128), f32),
        in_specs=[smem()] + [vmem()] * 3,
        out_specs=vmem(),
        scratch_shapes=[pltpu.VMEM((256, 128), f32)],
        compiler_params=room(8),
        name="gather_groups",
    )(phases, *x_in, partial)
    chunks = lax.all_to_all(chunks.reshape(64, 4, 128), "pen", 0, 0, tiled=True)
    rep = (np.arange(2048)[None, :] // 16 == np.arange(128)[:, None]).astype(ml_dtypes.bfloat16)
    mixed = pl.pallas_call(
        mix_kernel,
        out_shape=jax.ShapeDtypeStruct((256, 128), f32),
        in_specs=[vmem()] * 4,
        out_specs=vmem(),
        compiler_params=room(8),
        name="mix",
    )(chunks.reshape(256, 128), weight, embedding, jnp.asarray(rep))
    mixed = lax.all_to_all(mixed.reshape(64, 4, 128), "pen", 0, 0, tiled=True)
    modes = pl.pallas_call(
        scatter_groups_kernel,
        out_shape=jax.ShapeDtypeStruct((4, 128, 128), f32),
        in_specs=[smem()] + [vmem()] * 3,
        out_specs=vmem(),
        scratch_shapes=[pltpu.VMEM((256, 128), f32)],
        compiler_params=room(8),
        name="scatter_groups",
    )(phases, *x_out, mixed.reshape(256, 128))
    modes = lax.all_to_all(modes, "grp", 0, 0, tiled=True)
    whole = lambda *shape: pl.BlockSpec(shape, lambda i: (0,) * len(shape))
    return pl.pallas_call(
        point_kernel,
        out_shape=jax.ShapeDtypeStruct((CH, LZ, LX, NY), bf16),
        grid=(LZ // ZB,),
        in_specs=[
            whole(4, 128, 128),
            whole(512, 256),
            whole(512, 256),
            whole(256, 256),
            whole(512, 256),
            whole(NCLASS, CH),
            whole(CH, CH),
            whole(1, CH),
            whole(CH, HIDDEN),
            whole(1, HIDDEN),
            whole(CH, HIDDEN),
            whole(1, CH),
        ],
        out_specs=pl.BlockSpec((CH, ZB, LX, NY), lambda i: (0, i, 0, 0)),
        scratch_shapes=[
            pltpu.VMEM((4, 512, 128), f32),
            pltpu.VMEM((16, 128), f32),
            pltpu.VMEM((512, 256), bf16),
            pltpu.VMEM((128, 512), bf16),
            pltpu.VMEM((128, 128), f32),
            pltpu.VMEM((2, 512, 128), jnp.int32),
        ],
        compiler_params=room(28),
        name="point",
    )(
        modes,
        jnp.asarray(z_hi),
        jnp.asarray(z_lo),
        jnp.asarray(y_lanes(ytab)),
        labels,
        embedding,
        point_weight,
        point_bias.reshape(1, CH),
        expand_weight,
        expand_bias.reshape(1, HIDDEN),
        reduce_weight.T,
        reduce_bias.reshape(1, CH),
    )


def solution(mesh):
    return jax.shard_map(
        shards,
        mesh=mesh,
        in_specs=(
            P("grp", "pen", None),
            P(),
            P(("grp", "pen"), None, None, None, None),
            P(),
            P(),
            P(),
            P(),
            P(),
            P(),
        ),
        out_specs=P(None, "grp", "pen", None),
        check_vma=False,
    )
```

time: 119 us -> 100 us (0.84)
  blocking collectives: 15.7 us -> 57.9 us
  waiting for transfers between devices: 24.2 us -> 0 us
  starting transfers between devices: 23 us -> 0 us
  Pallas kernels: 50.8 us -> 29.9 us
  local copies, waits for them, and re-layouts: 4.92 us -> 11.7 us
    all_to_all x0 -> x3, blocking collectives: none -> 42.9 us  [the longest x1 23.9 us: shards(): chunks = lax.all_to_all(chunks.reshape(64, 4, 128), 'pen', 0, 0, tiled=True)]
    all_to_all x3 -> x0, waiting for transfers between devices: 24.2 us -> none  [the longest x1 9.58 us: shards(): chunks = lax.all_to_all(chunks.reshape(64, 4, 128), 'pen', 0, 0, tiled=True)]
    all_to_all x3 -> x0, starting transfers between devices: 23 us -> none  [the longest x1 14.7 us: shards(): chunks = lax.all_to_all(chunks.reshape(64, 4, 128), 'pen', 0, 0, tiled=True)]
    pallas_call x1, Pallas kernels: 36.7 us -> 23.1 us  [shards(): pl.pallas_call(point_kernel, out_shape=jax.ShapeDtypeStruct((CH, LZ, LX,...]
    unnamed x11 -> x46, local copies, waits for them, and re-layouts: 2.94 us -> 10.4 us
    pallas_call x1, Pallas kernels: 5.38 us -> 2.33 us  [shards(): pl.pallas_call(forward_kernel, out_shape=jax.ShapeDtypeStruct((4, 128, 12...]
    pallas_call x1, Pallas kernels: 3.49 us -> 1.69 us  [shards(): pl.pallas_call(mix_kernel, out_shape=jax.ShapeDtypeStruct((256, 128), f32...]
    pallas_call x1, Pallas kernels: 2.63 us -> 1.35 us  [shards(): pl.pallas_call(scatter_groups_kernel, out_shape=jax.ShapeDtypeStruct((4,...]
  transfers between devices with their start and end apart: 3 -> 0, of which waited for: 3 -> 0; matrix products, arithmetic and copies ran while one was open for 2% -> 0% of each run, Pallas kernels for 0% -> 0%
where the time goes in v1:
time: 100 us; the launch traced here: 99.6 us
  blocking collectives  57.9 us (58%)
  Pallas kernels  29.9 us (30%)
  local copies, waits for them, and re-layouts  11.7 us (12%)
    all_to_all x1, blocking collectives, shards(): chunks = lax.all_to_all(chunks.reshape(64, 4, 128), 'pen', 0, 0, tiled=True)  23.9 us
    pallas_call x1, Pallas kernels, shards(): pl.pallas_call(point_kernel, out_shape=jax.ShapeDtypeStruct((CH, LZ, LX,...  23.1 us
    all_to_all x1, blocking collectives, shards(): mixed = lax.all_to_all(mixed.reshape(64, 4, 128), 'pen', 0, 0, tiled=True)  15 us
    unnamed x46, local copies, waits for them, and re-layouts  10.4 us
    all_to_all x1, blocking collectives, shards(): partial = lax.all_to_all(partial, 'grp', 0, 0, tiled=True)  10.2 us
    all_to_all x1, blocking collectives, shards(): modes = lax.all_to_all(modes, 'grp', 0, 0, tiled=True)  8.78 us
    pallas_call x1, Pallas kernels, shards(): pl.pallas_call(forward_kernel, out_shape=jax.ShapeDtypeStruct((4, 128, 12...  2.33 us

profile of v1, /device:TPU:1, one launch (start us, length us, event | category | flops | bytes accessed | tf_op | source)
XLA Modules:
  0.0 99.6 jit_solution(5827285828637912458)
XLA Ops:
  0.0 0.0 copy-start.3
  0.0 0.0 copy-start.13
  0.0 0.0 copy-start.22
  0.0 0.0 copy-start.19
  0.0 0.0 copy-start.21
  0.0 0.0 copy-start.18
  0.0 0.0 copy-start.20
  0.0 0.0 copy-start.17
  0.1 1.2 %reshape.28.weight_ref = f32[4,2048]{1,0:T(4,128)S(1)} reshape(f32[1,16,2,16,16]{4,3,2,1,0:T(8,128)} %param.23) | data formatting | bytes 65536 | tf_op jit(solution)/shard_map/reshape | solution.py:350
  1.3 0.0 copy-start
  1.3 1.0 %copy-done = s32[64,8,256]{2,1,0:T(8,128)S(1)} copy-done((s32[64,8,256]{2,1,0:T(8,128)S(1)}, s32[64,8,256]{2,1,0:T(8,128)}, u32[]{:S(2)}) %copy-start) | copy-done | bytes 524312
  2.3 0.0 copy-start.5
  2.3 0.9 copy-done.5
  3.3 0.0 copy-start.6
  3.3 0.9 copy-done.6
  4.2 0.0 copy-start.16
  4.2 0.7 copy-done.16
  5.0 0.0 copy-start.1
  5.0 0.0 copy-start.4
  5.0 0.0 copy-start.7
  5.0 2.3 %forward.1 = f32[4,128,128]{2,1,0:T(8,128)S(1)} custom-call(s32[512,256]{1,0:T(8,128)S(1)} %bitcast.11, bf16[32,256]{1,0:T(8,128)(2,1)S(1)} %copy-done.16, bf16[256,512]{1,0:T(8,128)(2,1)S(1)} %copy-done.6, bf16[256,512]{1,0:T(8,128)(2,1)S(1)} %copy-done.5), custom_call_target="tpu_custom_call" | custom-call | tf_op jit(solution)/shard_map/forward/pallas_call | solution.py:341
  7.3 10.2 %all_to_all.20.in_ref = f32[4,128,128]{2,1,0:T(8,128)S(1)} all-to-all(f32[4,128,128]{2,1,0:T(8,128)S(1)} %forward.1), channel_id=1, replica_groups=mesh['grp'=4,'pen'=64] {'grp'}, dimensions={0} | all-to-all | bytes 524288 | tf_op jit(solution)/shard_map/all_to_all | solution.py:352
  17.5 0.0 copy-start.10
  17.5 0.9 copy-done.10
  18.4 0.0 copy-start.11
  18.4 0.9 copy-done.11
  19.3 0.0 copy-start.14
  19.3 0.7 copy-done.14
  20.0 1.4 %gather_groups.1 = f32[256,128]{1,0:T(8,128)S(1)} custom-call(f32[2048]{0:T(1024)S(1)} %copy-done.14, bf16[256,256]{1,0:T(8,128)(2,1)S(1)} %copy-done.11, bf16[256,256]{1,0:T(8,128)(2,1)S(1)} %copy-done.10, f32[4,128,128]{2,1,0:T(8,128)S(1)} %all_to_all.20.in_ref), custom_call_target="tpu_custom_call" | custom-call | tf_op jit(solution)/shard_map/gather_groups/pallas_call | solution.py:353
  21.5 23.9 %all_to_all.21 = f32[64,4,128]{2,1,0:T(4,128)S(1)} all-to-all(f32[64,4,128]{2,1,0:T(4,128)S(1)} %bitcast.16), channel_id=1, replica_groups=mesh['grp'=4,'pen'=64] {'pen'}, dimensions={0} | all-to-all | bytes 262144 | tf_op jit(solution)/shard_map/all_to_all | solution.py:362
  45.3 0.0 copy-start.2
  45.3 1.0 %copy-done.2 = bf16[128,2048]{1,0:T(8,128)(2,1)S(1)} copy-done((bf16[128,2048]{1,0:T(8,128)(2,1)S(1)}, bf16[128,2048]{1,0:T(8,128)(2,1)}, u32[]{:S(2)}) %copy-start.2) | copy-done | bytes 524312
  46.4 0.0 copy-start.12
  46.4 0.7 copy-done.12
  47.1 1.7 %mix.1 = f32[256,128]{1,0:T(8,128)S(1)} custom-call(f32[256,128]{1,0:T(8,128)S(1)} %bitcast.13, f32[4,2048]{1,0:T(4,128)S(1)} %reshape.28.weight_ref, f32[12,16]{1,0:T(8,128)S(1)} %copy-done.12, bf16[128,2048]{1,0:T(8,128)(2,1)S(1)} %copy-done.2), custom_call_target="tpu_custom_call" | custom-call | tf_op jit(solution)/shard_map/mix/pallas_call | solution.py:364
  48.8 15.0 %all_to_all.22 = f32[64,4,128]{2,1,0:T(4,128)S(1)} all-to-all(f32[64,4,128]{2,1,0:T(4,128)S(1)} %bitcast.14), channel_id=1, replica_groups=mesh['grp'=4,'pen'=64] {'pen'}, dimensions={0} | all-to-all | bytes 262144 | tf_op jit(solution)/shard_map/all_to_all | solution.py:372
  63.8 0.0 copy-start.8
  63.8 0.9 copy-done.8
  64.7 0.0 copy-start.9
  64.7 0.9 copy-done.9
  65.6 0.0 copy-start.15
  65.6 0.7 copy-done.15
  66.3 1.4 %scatter_groups.1 = f32[4,128,128]{2,1,0:T(8,128)S(1)} custom-call(f32[2048]{0:T(1024)S(1)} %copy-done.15, bf16[128,512]{1,0:T(8,128)(2,1)S(1)} %copy-done.9, bf16[128,512]{1,0:T(8,128)(2,1)S(1)} %copy-done.8, f32[256,128]{1,0:T(8,128)S(1)} %bitcast.15), custom_call_target="tpu_custom_call" | custom-call | tf_op jit(solution)/shard_map/scatter_groups/pallas_call | solution.py:373
  67.7 8.8 %all_to_all.23.modes_ref = f32[4,128,128]{2,1,0:T(8,128)S(1)} all-to-all(f32[4,128,128]{2,1,0:T(8,128)S(1)} %scatter_groups.1), channel_id=1, replica_groups=mesh['grp'=4,'pen'=64] {'grp'}, dimensions={0} | all-to-all | bytes 524288 | tf_op jit(solution)/shard_map/all_to_all | solution.py:382
  76.5 0.0 copy-done.3
  76.5 0.0 copy-done.13
  76.5 0.0 copy-done.22
  76.5 0.0 copy-done.19
  76.5 0.0 copy-done.21
  76.5 0.0 copy-done.18
  76.5 0.0 copy-done.20
  76.5 0.0 copy-done.17
  76.5 0.0 copy-done.1
  76.5 0.0 copy-done.4
  76.6 0.0 copy-done.7
  76.6 23.1 %point.1 = bf16[16,64,8,256]{3,2,1,0:T(8,128)(2,1)} custom-call(f32[4,128,128]{2,1,0:T(8,128)S(1)} %all_to_all.23.modes_ref, bf16[512,256]{1,0:T(8,128)(2,1)S(1)} %copy-done.4, bf16[512,256]{1,0:T(8,128)(2,1)S(1)} %copy-done.3, bf16[256,256]{1,0:T(8,128)(2,1)S(1)} %copy-done.7, s32[512,256]{1,0:T(8,128)S(1)} %bitcast.12, f32[12,16]{1,0:T(8,128)S(1)} %copy-done.13, ...), custom_call_target="tpu_custom_call" | custom-call | tf_op jit(solution)/shard_map/point/pallas_call | solution.py:384
Async XLA Ops:
  0.0 76.5 %copy-start.3 = (bf16[512,256]{1,0:T(8,128)(2,1)S(1)}, bf16[512,256]{1,0:T(8,128)(2,1)}, u32[]{:S(2)}) copy-start(bf16[512,256]{1,0:T(8,128)(2,1)} %constant.34.clone.lo_ref) | copy-start | bytes 786436
  0.0 76.5 %copy-start.13 = (f32[12,16]{1,0:T(8,128)S(1)}, f32[12,16]{1,0:T(8,128)}, u32[]{:S(2)}) copy-start(f32[12,16]{1,0:T(8,128)} %emb_ref.3) | copy-start | bytes 2308
  0.0 76.5 %copy-start.22 = (f32[16]{0:T(128)S(1)}, f32[16]{0:T(128)}, u32[]{:S(2)}) copy-start(f32[16]{0:T(128)} %param.29) | copy-start | bytes 196
  0.0 76.5 %copy-start.19 = (bf16[64,16]{0,1:T(8,128)(2,1)S(1)}, bf16[64,16]{0,1:T(8,128)(2,1)}, u32[]{:S(2)}) copy-start(bf16[64,16]{0,1:T(8,128)(2,1)} %param.28) | copy-start | bytes 6148
  0.0 76.5 %copy-start.21 = (f32[64]{0:T(128)S(1)}, f32[64]{0:T(128)}, u32[]{:S(2)}) copy-start(f32[64]{0:T(128)} %param.27) | copy-start | bytes 772
  0.0 76.5 %copy-start.18 = (bf16[16,64]{1,0:T(8,128)(2,1)S(1)}, bf16[16,64]{1,0:T(8,128)(2,1)}, u32[]{:S(2)}) copy-start(bf16[16,64]{1,0:T(8,128)(2,1)} %w1_ref.1) | copy-start | bytes 6148
  0.0 76.5 %copy-start.20 = (f32[16]{0:T(128)S(1)}, f32[16]{0:T(128)}, u32[]{:S(2)}) copy-start(f32[16]{0:T(128)} %param.25) | copy-start | bytes 196
  0.0 76.5 %copy-start.17 = (f32[16,16]{1,0:T(8,128)S(1)}, f32[16,16]{1,0:T(8,128)}, u32[]{:S(2)}) copy-start(f32[16,16]{1,0:T(8,128)} %pw_ref.1) | copy-start | bytes 3076
  1.3 1.0 %copy-start = (s32[64,8,256]{2,1,0:T(8,128)S(1)}, s32[64,8,256]{2,1,0:T(8,128)}, u32[]{:S(2)}) copy-start(s32[64,8,256]{2,1,0:T(8,128)} %param.21) | copy-start | bytes 1572868
  2.3 0.9 copy-start.5
  3.3 0.9 copy-start.6
  4.2 0.7 copy-start.16
  5.0 71.6 %copy-start.1 = (s32[64,8,256]{2,1,0:T(8,128)S(1)}, s32[64,8,256]{2,1,0:T(8,128)}, u32[]{:S(2)}) copy-start(s32[64,8,256]{2,1,0:T(8,128)} %param.21) | copy-start | bytes 1572868
  5.0 71.6 %copy-start.4 = (bf16[512,256]{1,0:T(8,128)(2,1)S(1)}, bf16[512,256]{1,0:T(8,128)(2,1)}, u32[]{:S(2)}) copy-start(bf16[512,256]{1,0:T(8,128)(2,1)} %constant.33.clone.hi_ref) | copy-start | bytes 786436
  5.0 71.6 %copy-start.7 = (bf16[256,256]{1,0:T(8,128)(2,1)S(1)}, bf16[256,256]{1,0:T(8,128)(2,1)}, u32[]{:S(2)}) copy-start(bf16[256,256]{1,0:T(8,128)(2,1)} %constant.35.clone.ytab_ref) | copy-start | bytes 393220
  17.5 0.9 copy-start.10
  18.4 0.9 copy-start.11
  19.3 0.7 copy-start.14
  45.3 1.0 %copy-start.2 = (bf16[128,2048]{1,0:T(8,128)(2,1)S(1)}, bf16[128,2048]{1,0:T(8,128)(2,1)}, u32[]{:S(2)}) copy-start(bf16[128,2048]{1,0:T(8,128)(2,1)} %constant.32.clone.rep_ref) | copy-start | bytes 1572868
  46.4 0.7 copy-start.12
  63.8 0.9 copy-start.8
  64.7 0.9 copy-start.9
  65.6 0.7 copy-start.15

commit v2 on v1

v2 whole, which is shorter than its diff:
```python
import functools
import math

import jax
import jax.numpy as jnp
import ml_dtypes
import numpy as np
from jax import lax
from jax.experimental import pallas as pl
from jax.experimental.pallas import tpu as pltpu
from jax.sharding import PartitionSpec as P

NZ = 256
NX = 512
NY = 256
CH = 16
MODES = 16
NCLASS = 12
HIDDEN = 64
LZ = 64
LX = 8
ROWS = LZ * LX

highest = lax.Precision.HIGHEST
f32 = jnp.float32
bf16 = jnp.bfloat16
FREQ = np.where(np.arange(MODES) < 8, np.arange(MODES), np.arange(MODES) - MODES)


def split(values):
    hi = values.astype(ml_dtypes.bfloat16)
    lo = (values - hi.astype(np.float64)).astype(ml_dtypes.bfloat16)
    return hi, lo


def y_tables():
    product = np.remainder(FREQ[:, None] * np.arange(NY)[None, :], NY)
    angles = product.astype(np.float32) * np.float32(2.0 * math.pi / NY)
    cos = np.cos(angles).astype(ml_dtypes.bfloat16)
    sin = np.sin(angles).astype(ml_dtypes.bfloat16)
    return np.stack([cos, -sin], axis=1).reshape(2 * MODES, NY)


def z_tables():
    angles = 2.0 * np.pi * np.remainder(FREQ[None, :] * np.arange(LZ)[:, None], NZ) / NZ
    table = np.zeros((LZ, LX, 2, LX, MODES))
    for x in range(LX):
        table[:, x, 0, x] = np.cos(angles)
        table[:, x, 1, x] = np.sin(angles)
    return table.reshape(ROWS, 2 * LX * MODES)


def x_tables():
    angles = 2.0 * np.pi * np.remainder(FREQ[None, :] * np.arange(LX)[:, None], NX) / NX
    table = np.zeros((2, LX, MODES, MODES, MODES))
    for kz in range(MODES):
        table[0, :, kz, :, kz] = np.cos(angles)
        table[1, :, kz, :, kz] = np.sin(angles)
    table = table.reshape(2, LX * MODES, MODES, 4, 4)
    return table.transpose(0, 1, 4, 3, 2).reshape(2, LX * MODES, MODES * MODES)


def y_lanes(ytab):
    table = ytab.reshape(2, 2, 4, 2, NY)
    table = np.moveaxis(table, (0, 1, 2, 3), (0, 3, 1, 2))
    return np.repeat(table.reshape(2 * MODES, NY), 8, axis=0)


def pen_phases():
    turn = np.remainder(np.arange(64)[:, None] * FREQ[None, :], 64)
    angles = 2.0 * np.pi * turn / 64
    table = np.zeros((64, 128), np.float32)
    table[:, 0:16] = np.cos(angles)
    table[:, 16:32] = np.sin(angles)
    return table


def iota(shape, axis):
    return lax.broadcasted_iota(jnp.int32, shape, axis)


def times_j(tile):
    imag_lane = (iota(tile.shape, 1) // 16) % 2 == 1
    return jnp.where(imag_lane, pltpu.roll(tile, 16, 1), -pltpu.roll(tile, 112, 1))


def exchange(tiles):
    block = iota(tiles[0].shape, 1) // 32
    out = []
    for i in range(4):
        best = tiles[i]
        for j in range(4):
            if j != i:
                best = jnp.where(block == j, pltpu.roll(tiles[j], 32 * (j - i) % 128, 1), best)
        out.append(best)
    return out


def quarter_signs(shape):
    quarter = iota(shape, 0) % 4
    cos = jnp.where(quarter == 0, 1.0, jnp.where(quarter == 2, -1.0, 0.0))
    sin = jnp.where(quarter == 1, 1.0, jnp.where(quarter == 3, -1.0, 0.0))
    flip = jnp.where(quarter % 2 == 0, 1.0, -1.0)
    return cos, sin, flip


def to_parts(values):
    hi = values.astype(bf16)
    lo = (values - hi.astype(f32)).astype(bf16)
    return hi, lo


def dot(left, right, dims=((1,), (0,)), precision=None):
    return lax.dot_general(
        left, right, (dims, ((), ())), precision=precision, preferred_element_type=f32
    )


def three(hi, lo, right):
    right_hi, right_lo = to_parts(right)
    return dot(hi, right_hi) + dot(hi, right_lo) + dot(lo, right_hi)


def forward_kernel(
    occ, ytab, zt_hi, zt_lo, xi_hi, xi_lo, xo_hi, xo_lo, z_hi, z_lo, ylane, phase, emb, weight,
    pw, pb, w1, b1, w2, b2,
    out_ref, wide_ref, rep_ref, xi_hi_out, xi_lo_out, xo_hi_out, xo_lo_out, z_hi_out, z_lo_out,
    ylane_out, label_ref, phase_out, table_ref, wide1_ref, wide2_ref, bias2_ref,
    occ_v, ytab_v, zt_hi_v, zt_lo_v, phase_v, emb_v, weight_v, pw_v, pb_v, w1_v, b1_v, w2_v, b2_v,
    small_ref, rows_ref, sems,
):
    pairs = [
        (occ, occ_v), (ytab, ytab_v), (zt_hi, zt_hi_v), (zt_lo, zt_lo_v), (emb, emb_v),
        (weight, weight_v), (pw, pw_v), (pb, pb_v), (w1, w1_v), (b1, b1_v), (w2, w2_v), (b2, b2_v),
        (phase, phase_v), (xi_hi, xi_hi_out), (xi_lo, xi_lo_out), (xo_hi, xo_hi_out),
        (xo_lo, xo_lo_out), (z_hi, z_hi_out), (z_lo, z_lo_out), (ylane, ylane_out),
    ]
    copies = [pltpu.make_async_copy(a, b, sems.at[i]) for i, (a, b) in enumerate(pairs)]
    for copy in copies:
        copy.start()
    rows_ref[...] = jnp.zeros_like(rows_ref)
    copies[0].wait()
    copies[1].wait()
    for half in range(2):
        piece = occ_v[:, half * 128 : (half + 1) * 128]
        label_ref[half] = piece
        small_ref[:, half * 128 : (half + 1) * 128] = piece.astype(f32).astype(bf16)
    for label in range(NCLASS):
        same = small_ref[...] == jnp.array(label, bf16)
        hot = jnp.where(same, jnp.array(1.0, bf16), jnp.array(0.0, bf16))
        part = dot(ytab_v[...], hot, ((1,), (1,)))
        for quarter in range(4):
            rows_ref[quarter, pl.ds(label, 32, stride=16), :] = part[
                :, quarter * 128 : (quarter + 1) * 128
            ]
    for copy in copies[2:]:
        copy.wait()
    nt = ((1,), (1,))
    for pair in range(2):
        block = [rows_ref[quarter, pl.ds(pair * 256, 256), :] for quarter in range(4)]
        block_hi, block_lo = to_parts(jnp.concatenate(block, axis=1))
        full = (
            dot(zt_hi_v[...], block_hi, nt)
            + dot(zt_hi_v[...], block_lo, nt)
            + dot(zt_lo_v[...], block_hi, nt)
        )
        for half in range(2):
            tile = full[:, half * 128 : (half + 1) * 128]
            out_ref[pair * 2 + half] = tile[:128] - times_j(tile[128:])

    left = jnp.where(iota((128, NCLASS), 0) % 16 == iota((128, NCLASS), 1), 1.0, 0.0).astype(f32)
    right = jnp.where(iota((16, 128), 1) % 16 == iota((16, 128), 0), 1.0, 0.0).astype(f32)
    lifted = dot(left, emb_v[...], precision=highest)
    wide = dot(right, lifted, ((0,), (1,)), highest)
    wide_ref[...] = jnp.where(
        iota((128, 128), 0) // 16 == iota((128, 128), 1) // 16, wide, 0.0
    )
    rep_ref[...] = jnp.concatenate([weight_v[...]] * 8, axis=1)
    row = phase_v[pl.ds(lax.axis_index("pen"), 16, stride=0), :]
    for half in range(2):
        pick = iota((16, 128), 1) == iota((16, 128), 0) + 16 * half
        column = jnp.sum(jnp.where(pick, row, 0.0), axis=1, keepdims=True)
        phase_out[half] = jnp.broadcast_to(column, (16, 128))

    table = dot(pw_v[...], emb_v[...], ((0,), (1,)), highest)
    spread = jnp.where(
        iota((NCLASS, 128), 0) == iota((NCLASS, 128), 1), 1.0, 0.0
    ).astype(f32)
    eye = iota((16, 16), 0) == iota((16, 16), 1)
    bias = jnp.sum(jnp.where(eye, pb_v[...], 0.0), axis=1, keepdims=True)
    table_ref[...] = dot(table, spread, precision=highest) + bias
    r1 = jnp.where(iota((64, 64), 0) == iota((64, 64), 1), 1.0, 0.0)
    r2 = jnp.where(iota((16, 128), 1) % 16 == iota((16, 128), 0), 0.5, 0.0).astype(bf16)
    full1 = dot(dot(r1.astype(bf16), w1_v[...], ((1,), (1,))).astype(bf16), r2)
    col1 = jnp.broadcast_to(jnp.sum(r1 * b1_v[...], axis=1, keepdims=True), (64, 128))
    first = col1.astype(bf16).astype(f32)
    second = (col1 - first).astype(bf16).astype(f32)
    third = col1 - first - second
    lane = iota((64, 128), 1)
    extra = jnp.where(
        lane == 0, first, jnp.where(lane == 1, second, jnp.where(lane == 2, third, 0.0))
    ).astype(bf16)
    for x in range(LX):
        wide1_ref[x * 64 : x * 64 + 64, 0:128] = jnp.where(lane // 16 == x, full1, 0.0).astype(bf16)
        wide1_ref[x * 64 : x * 64 + 64, 128:256] = extra
    r3 = jnp.where(iota((128, 16), 0) // 8 == iota((128, 16), 1), 1.0, 0.0)
    r4 = jnp.where(iota((64, 128), 1) % 64 == iota((64, 128), 0), 0.5, 0.0).astype(bf16)
    full2 = dot(dot(r3.astype(bf16), w2_v[...]).astype(bf16), r4)
    x_row = iota((128, 128), 0) % 8
    x_lane = iota((128, 128), 1) // 64
    for tile in range(4):
        wide2_ref[:, tile * 128 : tile * 128 + 128] = jnp.where(
            x_row == x_lane + 2 * tile, full2, 0.0
        ).astype(bf16)
    col2 = jnp.sum(r3 * b2_v[...], axis=1, keepdims=True)
    bias2_ref[...] = jnp.broadcast_to(col2, (128, 128))


def gather_groups_kernel(phase_ref, hi_ref, lo_ref, in_ref, out_ref):
    cos, sin, flip = quarter_signs((128, 128))
    real = in_ref[0] + flip * in_ref[2] + cos * (in_ref[1] + in_ref[3])
    imag = sin * (in_ref[3] - in_ref[1])
    real = real + times_j(imag)
    both = three(hi_ref[...], lo_ref[...], jnp.concatenate([real, -times_j(real)], axis=0))
    turned = times_j(both)
    for kz_hi in range(4):
        tiles = []
        for kz_lo in range(4):
            rows = slice((kz_lo * 4 + kz_hi) * 16, (kz_lo * 4 + kz_hi) * 16 + 16)
            tiles.append(both[rows] * phase_ref[0] - turned[rows] * phase_ref[1])
        for q, tile in enumerate(exchange(tiles)):
            out_ref[pl.ds(q * 64 + kz_hi, 16, stride=4), :] = tile


def mix_kernel(in_ref, weight_ref, wide_ref, out_ref):
    parts = [in_ref[pl.ds(step * 8, 8), :] for step in range(32)]
    while len(parts) > 1:
        parts = [a + b for a, b in zip(parts[0::2], parts[1::2])]
    total = parts[0] + pltpu.roll(parts[0], 4, 0)
    columns = dot(wide_ref[...], total, ((1,), (1,)), highest)
    row = iota((128, 128), 0)
    lane = iota((128, 128), 1)
    near = row // 32 == lane // 32
    row_imag = (row // 16) % 2 == 1
    lane_imag = (lane // 16) % 2 == 1
    flipped = jnp.concatenate(
        [columns[(n ^ 1) * 16 : (n ^ 1) * 16 + 16] for n in range(8)], axis=0
    )
    signed = jnp.where(row_imag[:, 0:8], -columns, columns)
    out = []
    for kz_hi in range(4):
        same = jnp.broadcast_to(signed[:, kz_hi : kz_hi + 1], (128, 128))
        other = jnp.broadcast_to(flipped[:, kz_hi : kz_hi + 1], (128, 128))
        factor = jnp.where(near, jnp.where(lane_imag, other, same), 0.0)
        product = factor * weight_ref[pl.ds(kz_hi * 128, 128), :]
        out.append(jnp.sum(product, axis=0, keepdims=True))
    tile = jnp.concatenate(out + out, axis=0) * (1.0 / (NZ * NX * NY))
    for step in range(32):
        out_ref[pl.ds(step * 8, 8), :] = tile


def scatter_groups_kernel(phase_ref, hi_ref, lo_ref, in_ref, out_ref):
    real = [None] * 16
    imag = [None] * 16
    for kz_hi in range(4):
        tiles = [in_ref[pl.ds(q * 64 + kz_hi, 16, stride=4), :] for q in range(4)]
        for kz_lo, tile in enumerate(exchange(tiles)):
            turned = times_j(tile)
            real[kz_lo * 4 + kz_hi] = tile * phase_ref[0] + turned * phase_ref[1]
            imag[kz_lo * 4 + kz_hi] = turned * phase_ref[0] - tile * phase_ref[1]
    real = three(hi_ref[...], lo_ref[...], jnp.concatenate(real + imag, axis=0))
    imag = times_j(real)
    cos, sin, flip = quarter_signs((128, 128))
    out_ref[0] = real
    out_ref[1] = cos * real + sin * imag
    out_ref[2] = flip * real
    out_ref[3] = cos * real - sin * imag


def twice_gelu(values):
    return values + values * lax.erf(values * np.float32(math.sqrt(0.5)))


ZB = 4
STEPS = LZ // ZB


def point_kernel(
    modes_ref, hi_ref, lo_ref, ytab_ref, label_ref, table_ref, wide1_ref, wide2_ref, bias2_ref,
    out_ref, planes_ref, pre_ref,
):
    step = pl.program_id(0)

    @pl.when(step == 0)
    def _():
        high_lane = (iota((128, 128), 1) // 8) % 2 == 1
        pair_tiles = []
        for c_hi in range(2):
            tiles = []
            for pair in range(2):
                even = modes_ref[2 * pair]
                odd = modes_ref[2 * pair + 1]
                if c_hi == 0:
                    tile = jnp.where(high_lane, pltpu.roll(odd, 8, 1), even)
                else:
                    tile = jnp.where(high_lane, odd, pltpu.roll(even, 120, 1))
                tiles.append(jnp.concatenate([tile, times_j(tile)], axis=0))
            full = three(hi_ref[...], lo_ref[...], jnp.concatenate(tiles, axis=1))
            full = full.astype(bf16).astype(f32)
            planes_ref[c_hi * 2] = full[:, 0:128]
            planes_ref[c_hi * 2 + 1] = full[:, 128:256]

    def finish(zi):
        hidden = twice_gelu(pre_ref[zi]).astype(bf16)
        bias2 = jnp.concatenate([bias2_ref[...]] * 2, axis=1)
        encoded = dot(wide2_ref[...], hidden) + bias2
        out_ref[:, zi] = encoded.reshape(16, 8, 256).astype(bf16)

    def begin():
        own = jnp.where(iota((16, 256), 0) % 8 == iota((16, 256), 1) % 8, 1.0, 0.0).astype(bf16)
        left = []
        for zi in range(ZB):
            base = pl.multiple_of((step * ZB + zi) * 8, 8)
            for x in range(LX):
                rows = [planes_ref[t, pl.ds(base + x, 8, stride=0), :] for t in range(4)]
                block = jnp.concatenate(
                    [jnp.concatenate(rows[0:2], axis=1), jnp.concatenate(rows[2:4], axis=1)],
                    axis=0,
                )
                left.append(block.astype(bf16) * own)
        return dot(jnp.concatenate(left, axis=0), ytab_ref[...])

    def expand(spatial, zi):
        low = table_ref[0:8, :]
        high = table_ref[8:16, :]
        ones = jnp.ones((16, 256), bf16)
        base = pl.multiple_of((step * ZB + zi) * 8, 8)
        point = []
        for x in range(LX):
            halves = []
            for half in range(2):
                label = label_ref[half, pl.ds(base + x, 8, stride=0), :]
                halves.append(
                    jnp.concatenate(
                        [
                            jnp.take_along_axis(low, label, axis=1),
                            jnp.take_along_axis(high, label, axis=1),
                        ],
                        axis=0,
                    )
                )
            point.append(jnp.concatenate(halves, axis=1))
        pointwise = jnp.concatenate(point, axis=0)
        activated = twice_gelu(spatial[zi * 128 : zi * 128 + 128] + pointwise).astype(bf16)
        pre_ref[zi] = dot(wide1_ref[:, 0:144], jnp.concatenate([activated, ones], axis=0))

    @pl.when(step == 0)
    def _():
        spatial = begin()
        for zi in range(ZB):
            expand(spatial, zi)

    @pl.when(jnp.logical_and(step > 0, step < STEPS))
    def _():
        spatial = begin()
        for zi in range(ZB):
            finish(zi)
            expand(spatial, zi)

    @pl.when(step == STEPS)
    def _():
        for zi in range(ZB):
            finish(zi)


def room(mib):
    return pltpu.CompilerParams(vmem_limit_bytes=mib * 1024 * 1024)


def vmem():
    return pl.BlockSpec(memory_space=pltpu.VMEM)


def shards(
    occupancy,
    embedding,
    spectral_weight,
    point_weight,
    point_bias,
    expand_weight,
    expand_bias,
    reduce_weight,
    reduce_bias,
):
    ytab = y_tables()
    z_hi, z_lo = split(z_tables())
    x_hi, x_lo = split(x_tables())
    constants = [
        ytab,
        z_hi.T.copy(),
        z_lo.T.copy(),
        x_hi.transpose(2, 0, 1).reshape(256, 256),
        x_lo.transpose(2, 0, 1).reshape(256, 256),
        x_hi.transpose(1, 0, 2).reshape(128, 512),
        x_lo.transpose(1, 0, 2).reshape(128, 512),
        z_hi,
        z_lo,
        y_lanes(ytab),
        pen_phases(),
    ]
    shape = jax.ShapeDtypeStruct
    made = pl.pallas_call(
        forward_kernel,
        out_shape=[
            shape((4, 128, 128), f32),
            shape((128, 128), f32),
            shape((512, 128), f32),
            shape((256, 256), bf16),
            shape((256, 256), bf16),
            shape((128, 512), bf16),
            shape((128, 512), bf16),
            shape((512, 256), bf16),
            shape((512, 256), bf16),
            shape((256, 256), bf16),
            shape((2, 512, 128), jnp.int32),
            shape((2, 16, 128), f32),
            shape((16, 128), f32),
            shape((512, 256), bf16),
            shape((128, 512), bf16),
            shape((128, 128), f32),
        ],
        in_specs=[pl.BlockSpec(memory_space=pltpu.HBM)] * 20,
        out_specs=[vmem()] * 16,
        scratch_shapes=[
            pltpu.VMEM((ROWS, NY), jnp.int32),
            pltpu.VMEM((32, 256), bf16),
            pltpu.VMEM((256, 512), bf16),
            pltpu.VMEM((256, 512), bf16),
            pltpu.VMEM((64, 128), f32),
            pltpu.VMEM((NCLASS, CH), f32),
            pltpu.VMEM((512, 16), f32),
            pltpu.VMEM((CH, CH), f32),
            pltpu.VMEM((1, CH), f32),
            pltpu.VMEM((CH, HIDDEN), bf16),
            pltpu.VMEM((1, HIDDEN), f32),
            pltpu.VMEM((CH, HIDDEN), bf16),
            pltpu.VMEM((1, CH), f32),
            pltpu.VMEM((ROWS, NY), bf16),
            pltpu.VMEM((4, 512, 128), f32),
            pltpu.SemaphoreType.DMA((20,)),
        ],
        compiler_params=room(16),
        name="forward",
    )(
        occupancy.reshape(ROWS, NY),
        *[jnp.asarray(c) for c in constants],
        embedding,
        spectral_weight.reshape(512, 16),
        point_weight,
        point_bias.reshape(1, CH),
        expand_weight,
        expand_bias.reshape(1, HIDDEN),
        reduce_weight.T,
        reduce_bias.reshape(1, CH),
    )
    partial, wide, weight, xi_hi, xi_lo, xo_hi, xo_lo = made[:7]
    z_hi, z_lo, ylane, labels, phases, table, wide1, wide2, bias2 = made[7:]
    partial = lax.all_to_all(partial, "grp", 0, 0, tiled=True)
    chunks = pl.pallas_call(
        gather_groups_kernel,
        out_shape=shape((256, 128), f32),
        in_specs=[vmem()] * 4,
        out_specs=vmem(),
        compiler_params=room(8),
        name="gather_groups",
    )(phases, xi_hi, xi_lo, partial)
    chunks = lax.all_to_all(chunks.reshape(64, 4, 128), "pen", 0, 0, tiled=True)
    mixed = pl.pallas_call(
        mix_kernel,
        out_shape=shape((256, 128), f32),
        in_specs=[vmem()] * 3,
        out_specs=vmem(),
        compiler_params=room(8),
        name="mix",
    )(chunks.reshape(256, 128), weight, wide)
    mixed = lax.all_to_all(mixed.reshape(64, 4, 128), "pen", 0, 0, tiled=True)
    modes = pl.pallas_call(
        scatter_groups_kernel,
        out_shape=shape((4, 128, 128), f32),
        in_specs=[vmem()] * 4,
        out_specs=vmem(),
        compiler_params=room(8),
        name="scatter_groups",
    )(phases, xo_hi, xo_lo, mixed.reshape(256, 128))
    modes = lax.all_to_all(modes, "grp", 0, 0, tiled=True)
    return pl.pallas_call(
        point_kernel,
        out_shape=shape((CH, LZ, LX, NY), bf16),
        grid=(STEPS + 1,),
        in_specs=[vmem()] * 9,
        out_specs=pl.BlockSpec((CH, ZB, LX, NY), lambda i: (0, jnp.maximum(i - 1, 0), 0, 0)),
        scratch_shapes=[
            pltpu.VMEM((4, 512, 128), f32),
            pltpu.VMEM((ZB, 512, 256), f32),
        ],
        compiler_params=room(24),
        name="point",
    )(modes, z_hi, z_lo, ylane, labels, table, wide1, wide2, bias2)


def solution(mesh):
    return jax.shard_map(
        shards,
        mesh=mesh,
        in_specs=(
            P("grp", "pen", None),
            P(),
            P(("grp", "pen"), None, None, None, None),
            P(),
            P(),
            P(),
            P(),
            P(),
            P(),
        ),
        out_specs=P(None, "grp", "pen", None),
        check_vma=False,
    )
```

time: 100 us -> 97 us (0.970)
  Pallas kernels: 29.9 us -> 21.8 us
  local copies, waits for them, and re-layouts: 11.7 us -> 16.5 us
    pallas_call x5, Pallas kernels: 29.9 us -> 21.8 us  [the longest x1 16 us: shards(): pl.pallas_call(point_kernel, out_shape=shape((CH, LZ, LX, NY), bf16), gri...]
    unnamed x46 -> x40, local copies, waits for them, and re-layouts: 10.4 us -> 16.5 us
    reshape x1 -> x0, local copies, waits for them, and re-layouts: 1.24 us -> none  [shards(): weight = spectral_weight.reshape(4, 2048)]
where the time goes in v2:
time: 97 us; the launch traced here: 96.2 us
  blocking collectives  57.9 us (60%)
  Pallas kernels  21.8 us (22%)
  local copies, waits for them, and re-layouts  16.5 us (17%)
    all_to_all x1, blocking collectives, shards(): chunks = lax.all_to_all(chunks.reshape(64, 4, 128), 'pen', 0, 0, tiled=True)  23.9 us
    unnamed x40, local copies, waits for them, and re-layouts  16.5 us
    pallas_call x1, Pallas kernels, shards(): pl.pallas_call(point_kernel, out_shape=shape((CH, LZ, LX, NY), bf16), gri...  16 us
    all_to_all x1, blocking collectives, shards(): mixed = lax.all_to_all(mixed.reshape(64, 4, 128), 'pen', 0, 0, tiled=True)  15 us
    all_to_all x1, blocking collectives, shards(): partial = lax.all_to_all(partial, 'grp', 0, 0, tiled=True)  10.2 us
    all_to_all x1, blocking collectives, shards(): modes = lax.all_to_all(modes, 'grp', 0, 0, tiled=True)  8.78 us
    pallas_call x1, Pallas kernels, shards(): pl.pallas_call(forward_kernel, out_shape=[shape((4, 128, 128), f32), shap...  4.19 us

profile of v2, /device:TPU:1, one launch (start us, length us, event | category | flops | bytes accessed | tf_op | source)
XLA Modules:
  0.0 96.2 jit_solution(9185580657770846587)
XLA Ops:
  0.0 0.0 copy-start
  0.0 1.0 %copy-done = s32[64,8,256]{2,1,0:T(8,128)S(1)} copy-done((s32[64,8,256]{2,1,0:T(8,128)S(1)}, s32[64,8,256]{2,1,0:T(8,128)}, u32[]{:S(2)}) %copy-start) | copy-done | bytes 524312
  1.0 0.0 copy-start.1
  1.0 0.9 copy-done.1
  2.0 0.0 copy-start.2
  2.0 0.9 copy-done.2
  2.9 0.0 copy-start.3
  2.9 0.9 copy-done.3
  3.9 0.0 copy-start.4
  3.9 0.9 copy-done.4
  4.8 0.0 copy-start.5
  4.8 0.9 copy-done.5
  5.8 0.0 copy-start.6
  5.8 0.9 copy-done.6
  6.7 0.0 copy-start.7
  6.7 0.9 copy-done.7
  7.6 0.0 copy-start.8
  7.6 0.9 copy-done.8
  8.5 0.0 copy-start.9
  8.5 0.9 copy-done.9
  9.4 0.0 copy-start.10
  9.4 0.9 copy-done.10
  10.3 0.0 copy-start.11
  10.3 0.8 copy-done.11
  11.1 0.0 copy-start.12
  11.1 0.7 copy-done.12
  11.8 0.0 copy-start.13
  11.8 0.7 copy-done.13
  12.5 0.0 copy-start.14
  12.5 0.7 copy-done.14
  13.2 0.0 copy-start.15
  13.2 0.7 copy-done.15
  13.9 0.0 copy-start.16
  13.9 0.7 copy-done.16
  14.6 0.0 copy-start.17
  14.6 0.7 copy-done.17
  15.2 0.0 copy-start.18
  15.2 0.7 copy-done.18
  15.9 0.0 copy-start.19
  15.9 0.7 copy-done.19
  16.5 4.2 %forward.1 = (f32[4,128,128]{2,1,0:T(8,128)S(1)}, f32[128,128]{1,0:T(8,128)S(1)}, f32[512,128]{1,0:T(8,128)S(1)}, bf16[256,256]{1,0:T(8,128)(2,1)S(1)}, bf16[256...) custom-call(s32[512,256]{1,0:T(8,128)S(1)} %bitcast.14, ...), custom_call_target="tpu_custom_call" | custom-call | tf_op jit(solution)/shard_map/forward/pallas_call | solution.py:412
  20.7 10.2 %all_to_all.20.in_ref = f32[4,128,128]{2,1,0:T(8,128)S(1)} all-to-all(f32[4,128,128]{2,1,0:T(8,128)S(1)} %get-tuple-element.26), channel_id=1, replica_groups=mesh['grp'=4,'pen'=64] {'grp'}, dimensions={0} | all-to-all | bytes 524288 | tf_op jit(solution)/shard_map/all_to_all | solution.py:468
  30.9 0.6 gather_groups.1
  31.5 23.9 %all_to_all.21 = f32[64,4,128]{2,1,0:T(4,128)S(1)} all-to-all(f32[64,4,128]{2,1,0:T(4,128)S(1)} %bitcast.11), channel_id=1, replica_groups=mesh['grp'=4,'pen'=64] {'pen'}, dimensions={0} | all-to-all | bytes 262144 | tf_op jit(solution)/shard_map/all_to_all | solution.py:477
  55.4 0.4 mix.1
  55.9 15.0 %all_to_all.22 = f32[64,4,128]{2,1,0:T(4,128)S(1)} all-to-all(f32[64,4,128]{2,1,0:T(4,128)S(1)} %bitcast.13), channel_id=1, replica_groups=mesh['grp'=4,'pen'=64] {'pen'}, dimensions={0} | all-to-all | bytes 262144 | tf_op jit(solution)/shard_map/all_to_all | solution.py:486
  70.9 0.6 scatter_groups.1
  71.5 8.8 %all_to_all.23.modes_ref = f32[4,128,128]{2,1,0:T(8,128)S(1)} all-to-all(f32[4,128,128]{2,1,0:T(8,128)S(1)} %scatter_groups.1), channel_id=1, replica_groups=mesh['grp'=4,'pen'=64] {'grp'}, dimensions={0} | all-to-all | bytes 524288 | tf_op jit(solution)/shard_map/all_to_all | solution.py:495
  80.2 16.0 %point.1 = bf16[16,64,8,256]{3,2,1,0:T(8,128)(2,1)} custom-call(f32[4,128,128]{2,1,0:T(8,128)S(1)} %all_to_all.23.modes_ref, bf16[512,256]{1,0:T(8,128)(2,1)S(1)} %get-tuple-element.29.hi_ref, bf16[512,256]{1,0:T(8,128)(2,1)S(1)} %get-tuple-element.30.lo_ref, bf16[256,256]{1,0:T(8,128)(2,1)S(1)} %get-tuple-element.31.ytab_ref, ...), custom_call_target="tpu_custom_call" | custom-call | tf_op jit(solution)/shard_map/point/pallas_call | solution.py:496
Async XLA Ops:
  0.0 1.0 %copy-start = (s32[64,8,256]{2,1,0:T(8,128)S(1)}, s32[64,8,256]{2,1,0:T(8,128)}, u32[]{:S(2)}) copy-start(s32[64,8,256]{2,1,0:T(8,128)} %param.20) | copy-start | bytes 1572868
  1.0 0.9 copy-start.1
  2.0 0.9 copy-start.2
  2.9 0.9 copy-start.3
  3.9 0.9 copy-start.4
  4.8 0.9 copy-start.5
  5.8 0.9 copy-start.6
  6.7 0.9 copy-start.7
  7.6 0.9 copy-start.8
  8.5 0.9 copy-start.9
  9.4 0.9 copy-start.10
  10.3 0.8 copy-start.11
  11.1 0.7 copy-start.12
  11.8 0.7 copy-start.13
  12.5 0.7 copy-start.14
  13.2 0.7 copy-start.15
  13.9 0.7 copy-start.16
  14.6 0.7 copy-start.17
  15.2 0.7 copy-start.18
  15.9 0.7 copy-start.19

commit v3 on v2

--- a/solution.py
+++ b/solution.py
@@ -408,6 +408,18 @@
         y_lanes(ytab),
         pen_phases(),
     ]
+    sources = [
+        occupancy.reshape(ROWS, NY),
+        *[jnp.asarray(c) for c in constants],
+        embedding,
+        spectral_weight.reshape(512, 16),
+        point_weight,
+        point_bias.reshape(1, CH),
+        expand_weight,
+        expand_bias.reshape(1, HIDDEN),
+        reduce_weight.T,
+        reduce_bias.reshape(1, CH),
+    ]
     shape = jax.ShapeDtypeStruct
     made = pl.pallas_call(
         forward_kernel,
@@ -451,18 +463,7 @@
         ],
         compiler_params=room(16),
         name="forward",
-    )(
-        occupancy.reshape(ROWS, NY),
-        *[jnp.asarray(c) for c in constants],
-        embedding,
-        spectral_weight.reshape(512, 16),
-        point_weight,
-        point_bias.reshape(1, CH),
-        expand_weight,
-        expand_bias.reshape(1, HIDDEN),
-        reduce_weight.T,
-        reduce_bias.reshape(1, CH),
-    )
+    )(*[pltpu.with_memory_space_constraint(value, pltpu.HBM) for value in sources])
     partial, wide, weight, xi_hi, xi_lo, xo_hi, xo_lo = made[:7]
     z_hi, z_lo, ylane, labels, phases, table, wide1, wide2, bias2 = made[7:]
     partial = lax.all_to_all(partial, "grp", 0, 0, tiled=True)

time: 97 us -> 79.7 us (0.82)
  local copies, waits for them, and re-layouts: 16.5 us -> 0 us
    unnamed x40 -> x0, local copies, waits for them, and re-layouts: 16.5 us -> none
where the time goes in v3:
time: 79.7 us; the launch traced here: 79.5 us
  blocking collectives  57.9 us (73%)
  Pallas kernels  21.6 us (27%)
    all_to_all x1, blocking collectives, shards(): chunks = lax.all_to_all(chunks.reshape(64, 4, 128), 'pen', 0, 0, tiled=True)  23.9 us
    pallas_call x1, Pallas kernels, shards(): pl.pallas_call(point_kernel, out_shape=shape((CH, LZ, LX, NY), bf16), gri...  16 us
    all_to_all x1, blocking collectives, shards(): mixed = lax.all_to_all(mixed.reshape(64, 4, 128), 'pen', 0, 0, tiled=True)  15 us
    all_to_all x1, blocking collectives, shards(): partial = lax.all_to_all(partial, 'grp', 0, 0, tiled=True)  10.2 us
    all_to_all x1, blocking collectives, shards(): modes = lax.all_to_all(modes, 'grp', 0, 0, tiled=True)  8.78 us
    pallas_call x1, Pallas kernels, shards(): pl.pallas_call(forward_kernel, out_shape=[shape((4, 128, 128), f32), shap...  4 us

profile of v3, /device:TPU:1, one launch (start us, length us, event | category | flops | bytes accessed | tf_op | source)
XLA Modules:
  0.0 79.5 jit_solution(9250603642288805101)
XLA Ops:
  0.0 4.0 %forward.1 = (f32[4,128,128]{2,1,0:T(8,128)S(1)}, f32[128,128]{1,0:T(8,128)S(1)}, f32[512,128]{1,0:T(8,128)S(1)}, bf16[256,256]{1,0:T(8,128)(2,1)S(1)}, bf16[256...) custom-call(s32[512,256]{1,0:T(8,128)} %bitcast.14, ...), custom_call_target="tpu_custom_call" | custom-call | tf_op jit(solution)/shard_map/forward/pallas_call | solution.py:424
  4.0 10.2 %all_to_all.20.in_ref = f32[4,128,128]{2,1,0:T(8,128)S(1)} all-to-all(f32[4,128,128]{2,1,0:T(8,128)S(1)} %get-tuple-element.26), channel_id=1, replica_groups=mesh['grp'=4,'pen'=64] {'grp'}, dimensions={0} | all-to-all | bytes 524288 | tf_op jit(solution)/shard_map/all_to_all | solution.py:469
  14.2 0.6 gather_groups.1
  14.8 23.9 %all_to_all.21 = f32[64,4,128]{2,1,0:T(4,128)S(1)} all-to-all(f32[64,4,128]{2,1,0:T(4,128)S(1)} %bitcast.11), channel_id=1, replica_groups=mesh['grp'=4,'pen'=64] {'pen'}, dimensions={0} | all-to-all | bytes 262144 | tf_op jit(solution)/shard_map/all_to_all | solution.py:478
  38.7 0.4 mix.1
  39.1 15.0 %all_to_all.22 = f32[64,4,128]{2,1,0:T(4,128)S(1)} all-to-all(f32[64,4,128]{2,1,0:T(4,128)S(1)} %bitcast.13), channel_id=1, replica_groups=mesh['grp'=4,'pen'=64] {'pen'}, dimensions={0} | all-to-all | bytes 262144 | tf_op jit(solution)/shard_map/all_to_all | solution.py:487
  54.2 0.6 scatter_groups.1
  54.7 8.8 %all_to_all.23.modes_ref = f32[4,128,128]{2,1,0:T(8,128)S(1)} all-to-all(f32[4,128,128]{2,1,0:T(8,128)S(1)} %scatter_groups.1), channel_id=1, replica_groups=mesh['grp'=4,'pen'=64] {'grp'}, dimensions={0} | all-to-all | bytes 524288 | tf_op jit(solution)/shard_map/all_to_all | solution.py:496
  63.5 16.0 %point.1 = bf16[16,64,8,256]{3,2,1,0:T(8,128)(2,1)} custom-call(f32[4,128,128]{2,1,0:T(8,128)S(1)} %all_to_all.23.modes_ref, bf16[512,256]{1,0:T(8,128)(2,1)S(1)} %get-tuple-element.29.hi_ref, bf16[512,256]{1,0:T(8,128)(2,1)S(1)} %get-tuple-element.30.lo_ref, bf16[256,256]{1,0:T(8,128)(2,1)S(1)} %get-tuple-element.31.ytab_ref, ...), custom_call_target="tpu_custom_call" | custom-call | tf_op jit(solution)/shard_map/point/pallas_call | solution.py:497

commit v4 on v2

--- a/solution.py
+++ b/solution.py
@@ -122,29 +122,18 @@
 
 
 def forward_kernel(
-    occ, ytab, zt_hi, zt_lo, xi_hi, xi_lo, xo_hi, xo_lo, z_hi, z_lo, ylane, phase, emb, weight,
-    pw, pb, w1, b1, w2, b2,
-    out_ref, wide_ref, rep_ref, xi_hi_out, xi_lo_out, xo_hi_out, xo_lo_out, z_hi_out, z_lo_out,
-    ylane_out, label_ref, phase_out, table_ref, wide1_ref, wide2_ref, bias2_ref,
-    occ_v, ytab_v, zt_hi_v, zt_lo_v, phase_v, emb_v, weight_v, pw_v, pb_v, w1_v, b1_v, w2_v, b2_v,
-    small_ref, rows_ref, sems,
+    occ, ytab, zt_hi, zt_lo, out_ref, occ_v, ytab_v, zt_hi_v, zt_lo_v, small_ref, rows_ref, sems
 ):
-    pairs = [
-        (occ, occ_v), (ytab, ytab_v), (zt_hi, zt_hi_v), (zt_lo, zt_lo_v), (emb, emb_v),
-        (weight, weight_v), (pw, pw_v), (pb, pb_v), (w1, w1_v), (b1, b1_v), (w2, w2_v), (b2, b2_v),
-        (phase, phase_v), (xi_hi, xi_hi_out), (xi_lo, xi_lo_out), (xo_hi, xo_hi_out),
-        (xo_lo, xo_lo_out), (z_hi, z_hi_out), (z_lo, z_lo_out), (ylane, ylane_out),
-    ]
+    pairs = [(occ, occ_v), (ytab, ytab_v), (zt_hi, zt_hi_v), (zt_lo, zt_lo_v)]
     copies = [pltpu.make_async_copy(a, b, sems.at[i]) for i, (a, b) in enumerate(pairs)]
     for copy in copies:
         copy.start()
-    rows_ref[...] = jnp.zeros_like(rows_ref)
+    for label in range(NCLASS, 16):
+        for quarter in range(4):
+            rows_ref[quarter, pl.ds(label, 32, stride=16), :] = jnp.zeros((32, 128), f32)
     copies[0].wait()
     copies[1].wait()
-    for half in range(2):
-        piece = occ_v[:, half * 128 : (half + 1) * 128]
-        label_ref[half] = piece
-        small_ref[:, half * 128 : (half + 1) * 128] = piece.astype(f32).astype(bf16)
+    small_ref[...] = occ_v[...].astype(f32).astype(bf16)
     for label in range(NCLASS):
         same = small_ref[...] == jnp.array(label, bf16)
         hot = jnp.where(same, jnp.array(1.0, bf16), jnp.array(0.0, bf16))
@@ -153,8 +142,8 @@
             rows_ref[quarter, pl.ds(label, 32, stride=16), :] = part[
                 :, quarter * 128 : (quarter + 1) * 128
             ]
-    for copy in copies[2:]:
-        copy.wait()
+    copies[2].wait()
+    copies[3].wait()
     nt = ((1,), (1,))
     for pair in range(2):
         block = [rows_ref[quarter, pl.ds(pair * 256, 256), :] for quarter in range(4)]
@@ -168,6 +157,26 @@
             tile = full[:, half * 128 : (half + 1) * 128]
             out_ref[pair * 2 + half] = tile[:128] - times_j(tile[128:])
 
+
+def prepare_kernel(
+    occ, xi_hi, xi_lo, xo_hi, xo_lo, z_hi, z_lo, ylane, phase, emb, weight, pw, pb, w1, b1, w2, b2,
+    wide_ref, rep_ref, xi_hi_out, xi_lo_out, xo_hi_out, xo_lo_out, z_hi_out, z_lo_out,
+    ylane_out, label_ref, phase_out, table_ref, wide1_ref, wide2_ref, bias2_ref,
+    occ_v, phase_v, emb_v, weight_v, pw_v, pb_v, w1_v, b1_v, w2_v, b2_v, sems,
+):
+    pairs = [
+        (occ, occ_v), (emb, emb_v), (weight, weight_v), (pw, pw_v), (pb, pb_v), (w1, w1_v),
+        (b1, b1_v), (w2, w2_v), (b2, b2_v), (phase, phase_v), (xi_hi, xi_hi_out),
+        (xi_lo, xi_lo_out), (xo_hi, xo_hi_out), (xo_lo, xo_lo_out), (z_hi, z_hi_out),
+        (z_lo, z_lo_out), (ylane, ylane_out),
+    ]
+    copies = [pltpu.make_async_copy(a, b, sems.at[i]) for i, (a, b) in enumerate(pairs)]
+    for copy in copies:
+        copy.start()
+    for copy in copies:
+        copy.wait()
+    for half in range(2):
+        label_ref[half] = occ_v[:, half * 128 : (half + 1) * 128]
     left = jnp.where(iota((128, NCLASS), 0) % 16 == iota((128, NCLASS), 1), 1.0, 0.0).astype(f32)
     right = jnp.where(iota((16, 128), 1) % 16 == iota((16, 128), 0), 1.0, 0.0).astype(f32)
     lifted = dot(left, emb_v[...], precision=highest)
@@ -281,20 +290,36 @@
     return values + values * lax.erf(values * np.float32(math.sqrt(0.5)))
 
 
-ZB = 4
+def lookup(table, index):
+    numbers = lax.GatherDimensionNumbers(
+        offset_dims=(),
+        collapsed_slice_dims=(1,),
+        start_index_map=(1,),
+        operand_batching_dims=(0,),
+        start_indices_batching_dims=(0,),
+    )
+    return lax.gather(
+        table,
+        index[..., None],
+        numbers,
+        slice_sizes=(1, 1),
+        mode=lax.GatherScatterMode.PROMISE_IN_BOUNDS,
+    )
+
+
+ZB = 8
 STEPS = LZ // ZB
 
 
 def point_kernel(
     modes_ref, hi_ref, lo_ref, ytab_ref, label_ref, table_ref, wide1_ref, wide2_ref, bias2_ref,
-    out_ref, planes_ref, pre_ref,
+    out_ref, planes_ref, act_ref, pre_ref,
 ):
     step = pl.program_id(0)
 
     @pl.when(step == 0)
     def _():
         high_lane = (iota((128, 128), 1) // 8) % 2 == 1
-        pair_tiles = []
         for c_hi in range(2):
             tiles = []
             for pair in range(2):
@@ -310,67 +335,77 @@
             planes_ref[c_hi * 2] = full[:, 0:128]
             planes_ref[c_hi * 2 + 1] = full[:, 128:256]
 
-    def finish(zi):
-        hidden = twice_gelu(pre_ref[zi]).astype(bf16)
-        bias2 = jnp.concatenate([bias2_ref[...]] * 2, axis=1)
-        encoded = dot(wide2_ref[...], hidden) + bias2
-        out_ref[:, zi] = encoded.reshape(16, 8, 256).astype(bf16)
-
-    def begin():
+    def finish(sub):
+        slot = sub % 2
+        hidden = twice_gelu(pre_ref[slot]).astype(bf16)
+        bias2 = jnp.concatenate([bias2_ref[...]] * 4, axis=1)
+        encoded = (dot(wide2_ref[...], hidden) + bias2).astype(bf16)
+        for half in range(2):
+            tile = encoded[:, half * 256 : half * 256 + 256]
+            out_ref[:, sub * 2 + half] = tile.reshape(16, 8, 256)
+
+    def transform(pair):
         own = jnp.where(iota((16, 256), 0) % 8 == iota((16, 256), 1) % 8, 1.0, 0.0).astype(bf16)
         left = []
-        for zi in range(ZB):
-            base = pl.multiple_of((step * ZB + zi) * 8, 8)
-            for x in range(LX):
-                rows = [planes_ref[t, pl.ds(base + x, 8, stride=0), :] for t in range(4)]
-                block = jnp.concatenate(
-                    [jnp.concatenate(rows[0:2], axis=1), jnp.concatenate(rows[2:4], axis=1)],
+        for row in range(16):
+            base = pl.multiple_of(pair * 16, 16) + row
+            rows = [planes_ref[t, pl.ds(base, 8, stride=0), :] for t in range(4)]
+            block = jnp.concatenate(
+                [jnp.concatenate(rows[0:2], axis=1), jnp.concatenate(rows[2:4], axis=1)],
+                axis=0,
+            )
+            left.append(block.astype(bf16) * own)
+        return dot(jnp.concatenate(left, axis=0), ytab_ref[...])
+
+    def activate(spatial, pair, slot):
+        low = table_ref[0:8, :]
+        high = table_ref[8:16, :]
+        for row in range(16):
+            base = pl.multiple_of(pair * 16, 16) + row
+            for half in range(2):
+                label = label_ref[half, pl.ds(base, 8, stride=0), :]
+                point = jnp.concatenate(
+                    [
+                        lookup(low, label),
+                        lookup(high, label),
+                    ],
                     axis=0,
                 )
-                left.append(block.astype(bf16) * own)
-        return dot(jnp.concatenate(left, axis=0), ytab_ref[...])
-
-    def expand(spatial, zi):
-        low = table_ref[0:8, :]
-        high = table_ref[8:16, :]
-        ones = jnp.ones((16, 256), bf16)
-        base = pl.multiple_of((step * ZB + zi) * 8, 8)
-        point = []
-        for x in range(LX):
-            halves = []
-            for half in range(2):
-                label = label_ref[half, pl.ds(base + x, 8, stride=0), :]
-                halves.append(
-                    jnp.concatenate(
-                        [
-                            jnp.take_along_axis(low, label, axis=1),
-                            jnp.take_along_axis(high, label, axis=1),
-                        ],
-                        axis=0,
-                    )
-                )
-            point.append(jnp.concatenate(halves, axis=1))
-        pointwise = jnp.concatenate(point, axis=0)
-        activated = twice_gelu(spatial[zi * 128 : zi * 128 + 128] + pointwise).astype(bf16)
-        pre_ref[zi] = dot(wide1_ref[:, 0:144], jnp.concatenate([activated, ones], axis=0))
+                total = spatial[row * 16 : row * 16 + 16, half * 128 : half * 128 + 128] + point
+                lane = (row // 8) * 256 + half * 128
+                place = (row % 8) * 16
+                act_ref[slot, place : place + 16, lane : lane + 128] = twice_gelu(total).astype(bf16)
+
+    def expand(slot):
+        pre_ref[slot] = dot(wide1_ref[:, 0:144], act_ref[slot])
 
     @pl.when(step == 0)
     def _():
-        spatial = begin()
-        for zi in range(ZB):
-            expand(spatial, zi)
-
-    @pl.when(jnp.logical_and(step > 0, step < STEPS))
+        for slot in range(2):
+            act_ref[slot, 128:144] = jnp.ones((16, 512), bf16)
+            activate(transform(slot), slot, slot)
+        expand(0)
+
+    @pl.when(step < STEPS - 1)
     def _():
-        spatial = begin()
-        for zi in range(ZB):
-            finish(zi)
-            expand(spatial, zi)
-
-    @pl.when(step == STEPS)
+        for sub in range(ZB // 2):
+            pair = step * (ZB // 2) + sub + 2
+            spatial = transform(pair)
+            expand(1 - sub % 2)
+            finish(sub)
+            activate(spatial, pair, sub % 2)
+
+    @pl.when(step == STEPS - 1)
     def _():
-        for zi in range(ZB):
-            finish(zi)
+        for sub in range(ZB // 2):
+            pair = step * (ZB // 2) + sub + 2
+            if sub < ZB // 2 - 2:
+                spatial = transform(pair)
+            if sub < ZB // 2 - 1:
+                expand(1 - sub % 2)
+            finish(sub)
+            if sub < ZB // 2 - 2:
+                activate(spatial, pair, sub % 2)
 
 
 def room(mib):
@@ -379,6 +414,10 @@
 
 def vmem():
     return pl.BlockSpec(memory_space=pltpu.VMEM)
+
+
+def far(*values):
+    return [pltpu.with_memory_space_constraint(jnp.asarray(v), pltpu.HBM) for v in values]
 
 
 def shards(
@@ -395,24 +434,29 @@
     ytab = y_tables()
     z_hi, z_lo = split(z_tables())
     x_hi, x_lo = split(x_tables())
-    constants = [
-        ytab,
-        z_hi.T.copy(),
-        z_lo.T.copy(),
-        x_hi.transpose(2, 0, 1).reshape(256, 256),
-        x_lo.transpose(2, 0, 1).reshape(256, 256),
-        x_hi.transpose(1, 0, 2).reshape(128, 512),
-        x_lo.transpose(1, 0, 2).reshape(128, 512),
-        z_hi,
-        z_lo,
-        y_lanes(ytab),
-        pen_phases(),
-    ]
     shape = jax.ShapeDtypeStruct
+    labels = occupancy.reshape(ROWS, NY)
+    partial = pl.pallas_call(
+        forward_kernel,
+        out_shape=shape((4, 128, 128), f32),
+        in_specs=[pl.BlockSpec(memory_space=pltpu.HBM)] * 4,
+        out_specs=vmem(),
+        scratch_shapes=[
+            pltpu.VMEM((ROWS, NY), jnp.int32),
+            pltpu.VMEM((32, 256), bf16),
+            pltpu.VMEM((256, 512), bf16),
+            pltpu.VMEM((256, 512), bf16),
+            pltpu.VMEM((ROWS, NY), bf16),
+            pltpu.VMEM((4, 512, 128), f32),
+            pltpu.SemaphoreType.DMA((4,)),
+        ],
+        compiler_params=room(16),
+        cost_estimate=pl.CostEstimate(flops=400000000, bytes_accessed=1000000, transcendentals=0),
+        name="forward",
+    )(*far(labels, ytab, z_hi.T.copy(), z_lo.T.copy()))
     made = pl.pallas_call(
-        forward_kernel,
+        prepare_kernel,
         out_shape=[
-            shape((4, 128, 128), f32),
             shape((128, 128), f32),
             shape((512, 128), f32),
             shape((256, 256), bf16),
@@ -429,13 +473,10 @@
             shape((128, 512), bf16),
             shape((128, 128), f32),
         ],
-        in_specs=[pl.BlockSpec(memory_space=pltpu.HBM)] * 20,
-        out_specs=[vmem()] * 16,
+        in_specs=[pl.BlockSpec(memory_space=pltpu.HBM)] * 17,
+        out_specs=[vmem()] * 15,
         scratch_shapes=[
             pltpu.VMEM((ROWS, NY), jnp.int32),
-            pltpu.VMEM((32, 256), bf16),
-            pltpu.VMEM((256, 512), bf16),
-            pltpu.VMEM((256, 512), bf16),
             pltpu.VMEM((64, 128), f32),
             pltpu.VMEM((NCLASS, CH), f32),
             pltpu.VMEM((512, 16), f32),
@@ -445,26 +486,34 @@
             pltpu.VMEM((1, HIDDEN), f32),
             pltpu.VMEM((CH, HIDDEN), bf16),
             pltpu.VMEM((1, CH), f32),
-            pltpu.VMEM((ROWS, NY), bf16),
-            pltpu.VMEM((4, 512, 128), f32),
-            pltpu.SemaphoreType.DMA((20,)),
+            pltpu.SemaphoreType.DMA((17,)),
         ],
         compiler_params=room(16),
-        name="forward",
+        cost_estimate=pl.CostEstimate(flops=200000000, bytes_accessed=3000000, transcendentals=0),
+        name="prepare",
     )(
-        occupancy.reshape(ROWS, NY),
-        *[jnp.asarray(c) for c in constants],
-        embedding,
-        spectral_weight.reshape(512, 16),
-        point_weight,
-        point_bias.reshape(1, CH),
-        expand_weight,
-        expand_bias.reshape(1, HIDDEN),
-        reduce_weight.T,
-        reduce_bias.reshape(1, CH),
-    )
-    partial, wide, weight, xi_hi, xi_lo, xo_hi, xo_lo = made[:7]
-    z_hi, z_lo, ylane, labels, phases, table, wide1, wide2, bias2 = made[7:]
+        *far(
+            labels,
+            x_hi.transpose(2, 0, 1).reshape(256, 256),
+            x_lo.transpose(2, 0, 1).reshape(256, 256),
+            x_hi.transpose(1, 0, 2).reshape(128, 512),
+            x_lo.transpose(1, 0, 2).reshape(128, 512),
+            z_hi,
+            z_lo,
+            y_lanes(ytab),
+            pen_phases(),
+            embedding,
+            spectral_weight.reshape(512, 16),
+            point_weight,
+            point_bias.reshape(1, CH),
+            expand_weight,
+            expand_bias.reshape(1, HIDDEN),
+            reduce_weight.T,
+            reduce_bias.reshape(1, CH),
+        )
+    )
+    wide, weight, xi_hi, xi_lo, xo_hi, xo_lo = made[:6]
+    z_hi, z_lo, ylane, labels, phases, table, wide1, wide2, bias2 = made[6:]
     partial = lax.all_to_all(partial, "grp", 0, 0, tiled=True)
     chunks = pl.pallas_call(
         gather_groups_kernel,
@@ -496,12 +545,13 @@
     return pl.pallas_call(
         point_kernel,
         out_shape=shape((CH, LZ, LX, NY), bf16),
-        grid=(STEPS + 1,),
+        grid=(STEPS,),
         in_specs=[vmem()] * 9,
-        out_specs=pl.BlockSpec((CH, ZB, LX, NY), lambda i: (0, jnp.maximum(i - 1, 0), 0, 0)),
+        out_specs=pl.BlockSpec((CH, ZB, LX, NY), lambda i: (0, i, 0, 0)),
         scratch_shapes=[
             pltpu.VMEM((4, 512, 128), f32),
-            pltpu.VMEM((ZB, 512, 256), f32),
+            pltpu.VMEM((ZB // 2, 144, 512), bf16),
+            pltpu.VMEM((ZB // 2, 512, 512), f32),
         ],
         compiler_params=room(24),
         name="point",

time: 97 us -> 75.8 us (0.78)
  local copies, waits for them, and re-layouts: 16.5 us -> 0 us
  blocking collectives: 57.9 us -> 47.7 us
  starting transfers between devices: 0 us -> 4.85 us
  waiting for transfers between devices: 0 us -> 2.94 us
  Pallas kernels: 21.8 us -> 19.9 us
    unnamed x40 -> x0, local copies, waits for them, and re-layouts: 16.5 us -> none
    all_to_all x1 -> x0, blocking collectives: 10.2 us -> none  [shards(): partial = lax.all_to_all(partial, 'grp', 0, 0, tiled=True)]
    all_to_all x0 -> x1, starting transfers between devices: none -> 4.85 us  [shards(): partial = lax.all_to_all(partial, 'grp', 0, 0, tiled=True)]
    pallas_call x1, Pallas kernels: 16 us -> 11.8 us  [shards(): pl.pallas_call(point_kernel, out_shape=shape((CH, LZ, LX, NY), bf16), gri...]
    all_to_all x0 -> x1, waiting for transfers between devices: none -> 2.94 us  [shards(): partial = lax.all_to_all(partial, 'grp', 0, 0, tiled=True)]
    pallas_call x1 -> x2, Pallas kernels: 4.19 us -> 6.51 us  [the longest x1 3.92 us: shards(): pl.pallas_call(forward_kernel, out_shape=shape((4, 128, 128), f32), in_sp...]
  transfers between devices with their start and end apart: 0 -> 1, of which waited for: 0 -> 1; matrix products, arithmetic and copies ran while one was open for 0% -> 0% of each run, Pallas kernels for 0% -> 3%
where the time goes in v4:
time: 75.8 us; the launch traced here: 75.5 us
  blocking collectives  47.7 us (63%)
  Pallas kernels  19.9 us (26%)
  starting transfers between devices  4.85 us (6%)
  waiting for transfers between devices  2.94 us (4%)
    all_to_all x1, blocking collectives, shards(): chunks = lax.all_to_all(chunks.reshape(64, 4, 128), 'pen', 0, 0, tiled=True)  23.9 us
    all_to_all x1, blocking collectives, shards(): mixed = lax.all_to_all(mixed.reshape(64, 4, 128), 'pen', 0, 0, tiled=True)  15 us
    pallas_call x1, Pallas kernels, shards(): pl.pallas_call(point_kernel, out_shape=shape((CH, LZ, LX, NY), bf16), gri...  11.8 us
    all_to_all x1, blocking collectives, shards(): modes = lax.all_to_all(modes, 'grp', 0, 0, tiled=True)  8.78 us
    all_to_all x1, starting transfers between devices, shards(): partial = lax.all_to_all(partial, 'grp', 0, 0, tiled=True)  4.85 us
    pallas_call x1, Pallas kernels, shards(): pl.pallas_call(forward_kernel, out_shape=shape((4, 128, 128), f32), in_sp...  3.92 us
    all_to_all x1, waiting for transfers between devices, shards(): partial = lax.all_to_all(partial, 'grp', 0, 0, tiled=True)  2.94 us
    pallas_call x1, Pallas kernels, shards(): pl.pallas_call(prepare_kernel, out_shape=[shape((128, 128), f32), shape((...  2.59 us
  transfers between devices with their start and end apart: 1, of which 1 were waited for; matrix products, arithmetic and copies ran while one was open for 0% of the time, Pallas kernels for 3%

profile of v4, /device:TPU:1, one launch (start us, length us, event | category | flops | bytes accessed | tf_op | source)
XLA Modules:
  0.0 75.5 jit_solution(16020642299350397249)
XLA Ops:
  0.0 3.9 %forward.1 = f32[4,128,128]{2,1,0:T(8,128)} custom-call(s32[512,256]{1,0:T(8,128)} %bitcast.14, bf16[32,256]{1,0:T(8,128)(2,1)} %constant.22.clone.ytab, bf16[256,512]{1,0:T(8,128)(2,1)} %constant.23.clone.zt_hi, bf16[256,512]{1,0:T(8,128)(2,1)} %constant.24.clone.zt_lo), custom_call_target="tpu_custom_call" | custom-call | flops 400000000 | bytes 1000000 | tf_op jit(solution)/shard_map/forward/pallas_call | solution.py:439
  3.9 4.9 %all-to-all-start = ((f32[4,128,128]{2,1,0:T(8,128)}), f32[4,128,128]{2,1,0:T(8,128)S(1)}, u32[]{:S(2)}, u32[]{:S(2)}) async-start(f32[4,128,128]{2,1,0:T(8,128)} %forward.1), calls=%async_computation | async-start | bytes 524288 | tf_op jit(solution)/shard_map/all_to_all | solution.py:517
  8.8 2.6 %prepare.1 = (f32[128,128]{1,0:T(8,128)S(1)}, f32[512,128]{1,0:T(8,128)S(1)}, bf16[256,256]{1,0:T(8,128)(2,1)S(1)}, bf16[256,256]{1,0:T(8,128)(2,1)S(1)}, bf16[1...) custom-call(s32[512,256]{1,0:T(8,128)} %bitcast.15, ...), custom_call_target="tpu_custom_call" | custom-call | flops 200000000 | bytes 3000000 | tf_op jit(solution)/shard_map/prepare/pallas_call | solution.py:457
  11.4 2.9 %all-to-all-done.in_ref = f32[4,128,128]{2,1,0:T(8,128)S(1)} async-done(((f32[4,128,128]{2,1,0:T(8,128)}), f32[4,128,128]{2,1,0:T(8,128)S(1)}, u32[]{:S(2)}, u32[]{:S(2)}) %all-to-all-start) | async-done | bytes 262176 | tf_op jit(solution)/shard_map/all_to_all | solution.py:517
  14.3 0.6 gather_groups.1
  14.9 23.9 %all_to_all.20 = f32[64,4,128]{2,1,0:T(4,128)S(1)} all-to-all(f32[64,4,128]{2,1,0:T(4,128)S(1)} %bitcast.11), channel_id=1, replica_groups=mesh['grp'=4,'pen'=64] {'pen'}, dimensions={0} | all-to-all | bytes 262144 | tf_op jit(solution)/shard_map/all_to_all | solution.py:526
  38.8 0.4 mix.1
  39.3 15.0 %all_to_all.21 = f32[64,4,128]{2,1,0:T(4,128)S(1)} all-to-all(f32[64,4,128]{2,1,0:T(4,128)S(1)} %bitcast.13), channel_id=1, replica_groups=mesh['grp'=4,'pen'=64] {'pen'}, dimensions={0} | all-to-all | bytes 262144 | tf_op jit(solution)/shard_map/all_to_all | solution.py:535
  54.3 0.6 scatter_groups.1
  54.9 8.8 %all_to_all.22.modes_ref = f32[4,128,128]{2,1,0:T(8,128)S(1)} all-to-all(f32[4,128,128]{2,1,0:T(8,128)S(1)} %scatter_groups.1), channel_id=1, replica_groups=mesh['grp'=4,'pen'=64] {'grp'}, dimensions={0} | all-to-all | bytes 524288 | tf_op jit(solution)/shard_map/all_to_all | solution.py:544
  63.7 11.8 %point.1 = bf16[16,64,8,256]{3,2,1,0:T(8,128)(2,1)} custom-call(f32[4,128,128]{2,1,0:T(8,128)S(1)} %all_to_all.22.modes_ref, bf16[512,256]{1,0:T(8,128)(2,1)S(1)} %get-tuple-element.27.hi_ref, bf16[512,256]{1,0:T(8,128)(2,1)S(1)} %get-tuple-element.28.lo_ref, bf16[256,256]{1,0:T(8,128)(2,1)S(1)} %get-tuple-element.29.ytab_ref, ...), custom_call_target="tpu_custom_call" | custom-call | tf_op jit(solution)/shard_map/point/pallas_call | solution.py:545
Async XLA Ops:
  3.9 10.4 %all-to-all-start = ((f32[4,128,128]{2,1,0:T(8,128)}), f32[4,128,128]{2,1,0:T(8,128)S(1)}, u32[]{:S(2)}, u32[]{:S(2)}) async-start(f32[4,128,128]{2,1,0:T(8,128)} %forward.1), calls=%async_computation | async-start | bytes 524288 | tf_op jit(solution)/shard_map/all_to_all | solution.py:517

commit v5 on v4

--- a/solution.py
+++ b/solution.py
@@ -122,7 +122,8 @@
 
 
 def forward_kernel(
-    occ, ytab, zt_hi, zt_lo, out_ref, occ_v, ytab_v, zt_hi_v, zt_lo_v, small_ref, rows_ref, sems
+    occ, ytab, zt_hi, zt_lo, own_ref, one_ref, two_ref, three_ref,
+    occ_v, ytab_v, zt_hi_v, zt_lo_v, small_ref, rows_ref, tile_ref, sems,
 ):
     pairs = [(occ, occ_v), (ytab, ytab_v), (zt_hi, zt_hi_v), (zt_lo, zt_lo_v)]
     copies = [pltpu.make_async_copy(a, b, sems.at[i]) for i, (a, b) in enumerate(pairs)]
@@ -155,7 +156,10 @@
         )
         for half in range(2):
             tile = full[:, half * 128 : (half + 1) * 128]
-            out_ref[pair * 2 + half] = tile[:128] - times_j(tile[128:])
+            tile_ref[pair * 2 + half] = tile[:128] - times_j(tile[128:])
+    here = lax.axis_index("grp")
+    for k, ref in enumerate((own_ref, one_ref, two_ref, three_ref)):
+        ref[...] = tile_ref[(here + k) % 4]
 
 
 def prepare_kernel(
@@ -225,7 +229,10 @@
     bias2_ref[...] = jnp.broadcast_to(col2, (128, 128))
 
 
-def gather_groups_kernel(phase_ref, hi_ref, lo_ref, in_ref, out_ref):
+def gather_groups_kernel(phase_ref, hi_ref, lo_ref, own_ref, one_ref, two_ref, three_ref, out_ref, in_ref):
+    here = lax.axis_index("grp")
+    for k, ref in enumerate((own_ref, one_ref, two_ref, three_ref)):
+        in_ref[(here + 4 - k) % 4] = ref[...]
     cos, sin, flip = quarter_signs((128, 128))
     real = in_ref[0] + flip * in_ref[2] + cos * (in_ref[1] + in_ref[3])
     imag = sin * (in_ref[3] - in_ref[1])
@@ -268,7 +275,7 @@
         out_ref[pl.ds(step * 8, 8), :] = tile
 
 
-def scatter_groups_kernel(phase_ref, hi_ref, lo_ref, in_ref, out_ref):
+def scatter_groups_kernel(phase_ref, hi_ref, lo_ref, in_ref, own_ref, one_ref, two_ref, three_ref, out_ref):
     real = [None] * 16
     imag = [None] * 16
     for kz_hi in range(4):
@@ -284,6 +291,9 @@
     out_ref[1] = cos * real + sin * imag
     out_ref[2] = flip * real
     out_ref[3] = cos * real - sin * imag
+    here = lax.axis_index("grp")
+    for k, ref in enumerate((own_ref, one_ref, two_ref, three_ref)):
+        ref[...] = out_ref[(here + k) % 4]
 
 
 def twice_gelu(values):
@@ -307,18 +317,21 @@
     )
 
 
-ZB = 8
+ZB = 16
 STEPS = LZ // ZB
 
 
 def point_kernel(
-    modes_ref, hi_ref, lo_ref, ytab_ref, label_ref, table_ref, wide1_ref, wide2_ref, bias2_ref,
-    out_ref, planes_ref, act_ref, pre_ref,
+    own_ref, one_ref, two_ref, three_ref, hi_ref, lo_ref, ytab_ref, label_ref, table_ref, wide1_ref, wide2_ref, bias2_ref,
+    out_ref, planes_ref, act_ref, pre_ref, modes_ref,
 ):
     step = pl.program_id(0)
 
     @pl.when(step == 0)
     def _():
+        here = lax.axis_index("grp")
+        for k, ref in enumerate((own_ref, one_ref, two_ref, three_ref)):
+            modes_ref[(here + 4 - k) % 4] = ref[...]
         high_lane = (iota((128, 128), 1) // 8) % 2 == 1
         for c_hi in range(2):
             tiles = []
@@ -416,6 +429,13 @@
     return pl.BlockSpec(memory_space=pltpu.VMEM)
 
 
+def rotate(tiles):
+    moved = [tiles[0]]
+    for k in range(1, 4):
+        moved.append(lax.ppermute(tiles[k], "grp", [(i, (i + k) % 4) for i in range(4)]))
+    return moved
+
+
 def far(*values):
     return [pltpu.with_memory_space_constraint(jnp.asarray(v), pltpu.HBM) for v in values]
 
@@ -438,9 +458,9 @@
     labels = occupancy.reshape(ROWS, NY)
     partial = pl.pallas_call(
         forward_kernel,
-        out_shape=shape((4, 128, 128), f32),
+        out_shape=[shape((128, 128), f32)] * 4,
         in_specs=[pl.BlockSpec(memory_space=pltpu.HBM)] * 4,
-        out_specs=vmem(),
+        out_specs=[vmem()] * 4,
         scratch_shapes=[
             pltpu.VMEM((ROWS, NY), jnp.int32),
             pltpu.VMEM((32, 256), bf16),
@@ -448,6 +468,7 @@
             pltpu.VMEM((256, 512), bf16),
             pltpu.VMEM((ROWS, NY), bf16),
             pltpu.VMEM((4, 512, 128), f32),
+            pltpu.VMEM((4, 128, 128), f32),
             pltpu.SemaphoreType.DMA((4,)),
         ],
         compiler_params=room(16),
@@ -514,15 +535,16 @@
     )
     wide, weight, xi_hi, xi_lo, xo_hi, xo_lo = made[:6]
     z_hi, z_lo, ylane, labels, phases, table, wide1, wide2, bias2 = made[6:]
-    partial = lax.all_to_all(partial, "grp", 0, 0, tiled=True)
+    partial = rotate(partial)
     chunks = pl.pallas_call(
         gather_groups_kernel,
         out_shape=shape((256, 128), f32),
-        in_specs=[vmem()] * 4,
+        in_specs=[vmem()] * 7,
         out_specs=vmem(),
+        scratch_shapes=[pltpu.VMEM((4, 128, 128), f32)],
         compiler_params=room(8),
         name="gather_groups",
-    )(phases, xi_hi, xi_lo, partial)
+    )(phases, xi_hi, xi_lo, *partial)
     chunks = lax.all_to_all(chunks.reshape(64, 4, 128), "pen", 0, 0, tiled=True)
     mixed = pl.pallas_call(
         mix_kernel,
@@ -535,27 +557,29 @@
     mixed = lax.all_to_all(mixed.reshape(64, 4, 128), "pen", 0, 0, tiled=True)
     modes = pl.pallas_call(
         scatter_groups_kernel,
-        out_shape=shape((4, 128, 128), f32),
+        out_shape=[shape((128, 128), f32)] * 4,
         in_specs=[vmem()] * 4,
-        out_specs=vmem(),
+        out_specs=[vmem()] * 4,
+        scratch_shapes=[pltpu.VMEM((4, 128, 128), f32)],
         compiler_params=room(8),
         name="scatter_groups",
     )(phases, xo_hi, xo_lo, mixed.reshape(256, 128))
-    modes = lax.all_to_all(modes, "grp", 0, 0, tiled=True)
+    modes = rotate(modes)
     return pl.pallas_call(
         point_kernel,
         out_shape=shape((CH, LZ, LX, NY), bf16),
         grid=(STEPS,),
-        in_specs=[vmem()] * 9,
+        in_specs=[vmem()] * 12,
         out_specs=pl.BlockSpec((CH, ZB, LX, NY), lambda i: (0, i, 0, 0)),
         scratch_shapes=[
             pltpu.VMEM((4, 512, 128), f32),
-            pltpu.VMEM((ZB // 2, 144, 512), bf16),
-            pltpu.VMEM((ZB // 2, 512, 512), f32),
+            pltpu.VMEM((2, 144, 512), bf16),
+            pltpu.VMEM((2, 512, 512), f32),
+            pltpu.VMEM((4, 128, 128), f32),
         ],
         compiler_params=room(24),
         name="point",
-    )(modes, z_hi, z_lo, ylane, labels, table, wide1, wide2, bias2)
+    )(*modes, z_hi, z_lo, ylane, labels, table, wide1, wide2, bias2)
 
 
 def solution(mesh):

time: 75.8 us -> 71 us (0.937)
  blocking collectives: 47.7 us -> 38.6 us
  starting transfers between devices: 4.85 us -> 9.35 us
    ppermute x0 -> x6, starting transfers between devices: none -> 9.35 us  [rotate(): lax.ppermute(tiles[k], 'grp', [(i, (i + k) % 4) for i in range(4)])]
    all_to_all x1 -> x0, blocking collectives: 8.78 us -> none  [shards(): modes = lax.all_to_all(modes, 'grp', 0, 0, tiled=True)]
    all_to_all x1 -> x0, starting transfers between devices: 4.85 us -> none  [shards(): partial = lax.all_to_all(partial, 'grp', 0, 0, tiled=True)]
    ppermute x0 -> x6, waiting for transfers between devices: none -> 3.49 us  [rotate(): lax.ppermute(tiles[k], 'grp', [(i, (i + k) % 4) for i in range(4)])]
    all_to_all x1 -> x0, waiting for transfers between devices: 2.94 us -> none  [shards(): partial = lax.all_to_all(partial, 'grp', 0, 0, tiled=True)]
  transfers between devices with their start and end apart: 1 -> 6, of which waited for: 1 -> 3; matrix products, arithmetic and copies ran while one was open for 0% -> 0% of each run, Pallas kernels for 3% -> 4%
where the time goes in v5:
time: 71 us; the launch traced here: 70.8 us
  blocking collectives  38.6 us (54%)
  Pallas kernels  19.4 us (27%)
  starting transfers between devices  9.35 us (13%)
  waiting for transfers between devices  3.49 us (5%)
    all_to_all x1, blocking collectives, shards(): chunks = lax.all_to_all(chunks.reshape(64, 4, 128), 'pen', 0, 0, tiled=True)  23.5 us
    all_to_all x1, blocking collectives, shards(): mixed = lax.all_to_all(mixed.reshape(64, 4, 128), 'pen', 0, 0, tiled=True)  15 us
    pallas_call x1, Pallas kernels, shards(): pl.pallas_call(point_kernel, out_shape=shape((CH, LZ, LX, NY), bf16), gri...  11.9 us
    ppermute x6, starting transfers between devices, rotate(): lax.ppermute(tiles[k], 'grp', [(i, (i + k) % 4) for i in range(4)])  9.35 us
    ppermute x6, waiting for transfers between devices, rotate(): lax.ppermute(tiles[k], 'grp', [(i, (i + k) % 4) for i in range(4)])  3.49 us
    pallas_call x1, Pallas kernels, shards(): pl.pallas_call(forward_kernel, out_shape=[shape((128, 128), f32)] * 4, in...  3.24 us
    pallas_call x1, Pallas kernels, shards(): pl.pallas_call(prepare_kernel, out_shape=[shape((128, 128), f32), shape((...  2.59 us
  transfers between devices with their start and end apart: 6, of which 3 were waited for; matrix products, arithmetic and copies ran while one was open for 0% of the time, Pallas kernels for 4%

profile of v5, /device:TPU:1, one launch (start us, length us, event | category | flops | bytes accessed | tf_op | source)
XLA Modules:
  0.0 70.8 jit_solution(8181559591233589019)
XLA Ops:
  0.0 3.2 %forward.1 = (f32[128,128]{1,0:T(8,128)S(1)}, f32[128,128]{1,0:T(8,128)S(1)}, f32[128,128]{1,0:T(8,128)S(1)}, f32[128,128]{1,0:T(8,128)S(1)}) custom-call(s32[512,256]{1,0:T(8,128)} %bitcast.14, bf16[32,256]{1,0:T(8,128)(2,1)} %constant.22.clone.ytab, bf16[256,512]{1,0:T(8,128)(2,1)} %constant.23.clone.zt_hi, bf16[256,512]{1,0:T(8,128)(2,1)} %constant.24.clone.zt_lo), custom_call_target="tpu_custom_call" | custom-call | flops 400000000 | bytes 1000000 | tf_op jit(solution)/shard_map/forward/pallas_call | solution.py:459
  3.2 2.1 %collective-permute-start = (f32[128,128]{1,0:T(8,128)S(1)}, f32[128,128]{1,0:T(8,128)S(1)}, u32[]{:S(2)}, u32[]{:S(2)}) collective-permute-start(f32[128,128]{1,0:T(8,128)S(1)} %get-tuple-element.34), channel_id=1, source_target_pairs={{0,64},{64,128},{128,192},{192,0},{1,65},{65,129},{129,193},{193,1... | collective-permute-start | bytes 196616 | tf_op jit(solution)/shard_map/ppermute | solution.py:435
  5.4 2.4 %collective-permute-start.1 = (f32[128,128]{1,0:T(8,128)S(1)}, f32[128,128]{1,0:T(8,128)S(1)}, u32[]{:S(2)}, u32[]{:S(2)}) collective-permute-start(f32[128,128]{1,0:T(8,128)S(1)} %get-tuple-element.35), channel_id=1, source_target_pairs={{0,128},{64,192},{128,0},{192,64},{1,129},{65,193},{129,1},{193,65... | collective-permute-start | bytes 196616 | tf_op jit(solution)/shard_map/ppermute | solution.py:435
  7.8 1.2 %collective-permute-start.2 = (f32[128,128]{1,0:T(8,128)S(1)}, f32[128,128]{1,0:T(8,128)S(1)}, u32[]{:S(2)}, u32[]{:S(2)}) collective-permute-start(f32[128,128]{1,0:T(8,128)S(1)} %get-tuple-element.36), channel_id=1, source_target_pairs={{0,192},{64,0},{128,64},{192,128},{1,193},{65,1},{129,65},{193,129... | collective-permute-start | bytes 196616 | tf_op jit(solution)/shard_map/ppermute | solution.py:435
  9.0 2.6 %prepare.1 = (f32[128,128]{1,0:T(8,128)S(1)}, f32[512,128]{1,0:T(8,128)S(1)}, bf16[256,256]{1,0:T(8,128)(2,1)S(1)}, bf16[256,256]{1,0:T(8,128)(2,1)S(1)}, bf16[1...) custom-call(s32[512,256]{1,0:T(8,128)} %bitcast.15, ...), custom_call_target="tpu_custom_call" | custom-call | flops 200000000 | bytes 3000000 | tf_op jit(solution)/shard_map/prepare/pallas_call | solution.py:478
  11.6 0.0 collective-permute-done.one_ref
  11.6 0.0 collective-permute-done.1.two_ref
  11.6 0.0 collective-permute-done.2.three_ref
  11.6 0.6 gather_groups.1
  12.2 23.5 %all_to_all.10 = f32[64,4,128]{2,1,0:T(4,128)S(1)} all-to-all(f32[64,4,128]{2,1,0:T(4,128)S(1)} %bitcast.11), channel_id=1, replica_groups=mesh['grp'=4,'pen'=64] {'pen'}, dimensions={0} | all-to-all | bytes 262144 | tf_op jit(solution)/shard_map/all_to_all | solution.py:548
  35.8 0.4 mix.1
  36.2 15.0 %all_to_all.11 = f32[64,4,128]{2,1,0:T(4,128)S(1)} all-to-all(f32[64,4,128]{2,1,0:T(4,128)S(1)} %bitcast.13), channel_id=1, replica_groups=mesh['grp'=4,'pen'=64] {'pen'}, dimensions={0} | all-to-all | bytes 262144 | tf_op jit(solution)/shard_map/all_to_all | solution.py:557
  51.2 0.6 scatter_groups.1
  51.8 0.4 collective-permute-start.3
  52.2 3.3 %collective-permute-start.4 = (f32[128,128]{1,0:T(8,128)S(1)}, f32[128,128]{1,0:T(8,128)S(1)}, u32[]{:S(2)}, u32[]{:S(2)}) collective-permute-start(f32[128,128]{1,0:T(8,128)S(1)} %get-tuple-element.41), channel_id=1, source_target_pairs={{0,128},{64,192},{128,0},{192,64},{1,129},{65,193},{129,1},{193,65... | collective-permute-start | bytes 196616 | tf_op jit(solution)/shard_map/ppermute | solution.py:435
  55.4 0.0 collective-permute-start.5
  55.4 0.8 %collective-permute-done.3.one_ref = f32[128,128]{1,0:T(8,128)S(1)} collective-permute-done((f32[128,128]{1,0:T(8,128)S(1)}, f32[128,128]{1,0:T(8,128)S(1)}, u32[]{:S(2)}, u32[]{:S(2)}) %collective-permute-start.3) | collective-permute-done | bytes 65568 | tf_op jit(solution)/shard_map/ppermute | solution.py:435
  56.2 2.1 %collective-permute-done.4.two_ref = f32[128,128]{1,0:T(8,128)S(1)} collective-permute-done((f32[128,128]{1,0:T(8,128)S(1)}, f32[128,128]{1,0:T(8,128)S(1)}, u32[]{:S(2)}, u32[]{:S(2)}) %collective-permute-start.4) | collective-permute-done | bytes 65568 | tf_op jit(solution)/shard_map/ppermute | solution.py:435
  58.4 0.6 collective-permute-done.5.three_ref
  58.9 11.9 %point.1 = bf16[16,64,8,256]{3,2,1,0:T(8,128)(2,1)} custom-call(f32[128,128]{1,0:T(8,128)S(1)} %get-tuple-element.39.own_ref, f32[128,128]{1,0:T(8,128)S(1)} %collective-permute-done.3.one_ref, f32[128,128]{1,0:T(8,128)S(1)} %collective-permute-done.4.two_ref, f32[128,128]{1,0:T(8,128)S(1)} %collective-permute-done.5.three_ref, ...), custom_call_target="tpu_custom_call" | custom-call | tf_op jit(solution)/shard_map/point/pallas_call | solution.py:568
Async XLA Ops:
  3.2 8.3 %collective-permute-start = (f32[128,128]{1,0:T(8,128)S(1)}, f32[128,128]{1,0:T(8,128)S(1)}, u32[]{:S(2)}, u32[]{:S(2)}) collective-permute-start(f32[128,128]{1,0:T(8,128)S(1)} %get-tuple-element.34), channel_id=1, source_target_pairs={{0,64},{64,128},{128,192},{192,0},{1,65},{65,129},{129,193},{193,1... | collective-permute-start | bytes 196616 | tf_op jit(solution)/shard_map/ppermute | solution.py:435
  5.4 6.2 %collective-permute-start.1 = (f32[128,128]{1,0:T(8,128)S(1)}, f32[128,128]{1,0:T(8,128)S(1)}, u32[]{:S(2)}, u32[]{:S(2)}) collective-permute-start(f32[128,128]{1,0:T(8,128)S(1)} %get-tuple-element.35), channel_id=1, source_target_pairs={{0,128},{64,192},{128,0},{192,64},{1,129},{65,193},{129,1},{193,65... | collective-permute-start | bytes 196616 | tf_op jit(solution)/shard_map/ppermute | solution.py:435
  7.8 3.8 %collective-permute-start.2 = (f32[128,128]{1,0:T(8,128)S(1)}, f32[128,128]{1,0:T(8,128)S(1)}, u32[]{:S(2)}, u32[]{:S(2)}) collective-permute-start(f32[128,128]{1,0:T(8,128)S(1)} %get-tuple-element.36), channel_id=1, source_target_pairs={{0,192},{64,0},{128,64},{192,128},{1,193},{65,1},{129,65},{193,129... | collective-permute-start | bytes 196616 | tf_op jit(solution)/shard_map/ppermute | solution.py:435
  51.8 4.4 %collective-permute-start.3 = (f32[128,128]{1,0:T(8,128)S(1)}, f32[128,128]{1,0:T(8,128)S(1)}, u32[]{:S(2)}, u32[]{:S(2)}) collective-permute-start(f32[128,128]{1,0:T(8,128)S(1)} %get-tuple-element.40), channel_id=1, source_target_pairs={{0,64},{64,128},{128,192},{192,0},{1,65},{65,129},{129,193},{193,1... | collective-permute-start | bytes 196616 | tf_op jit(solution)/shard_map/ppermute | solution.py:435
  52.2 6.2 %collective-permute-start.4 = (f32[128,128]{1,0:T(8,128)S(1)}, f32[128,128]{1,0:T(8,128)S(1)}, u32[]{:S(2)}, u32[]{:S(2)}) collective-permute-start(f32[128,128]{1,0:T(8,128)S(1)} %get-tuple-element.41), channel_id=1, source_target_pairs={{0,128},{64,192},{128,0},{192,64},{1,129},{65,193},{129,1},{193,65... | collective-permute-start | bytes 196616 | tf_op jit(solution)/shard_map/ppermute | solution.py:435
  55.4 3.5 %collective-permute-start.5 = (f32[128,128]{1,0:T(8,128)S(1)}, f32[128,128]{1,0:T(8,128)S(1)}, u32[]{:S(2)}, u32[]{:S(2)}) collective-permute-start(f32[128,128]{1,0:T(8,128)S(1)} %get-tuple-element.42), channel_id=1, source_target_pairs={{0,192},{64,0},{128,64},{192,128},{1,193},{65,1},{129,65},{193,129... | collective-permute-start | bytes 196616 | tf_op jit(solution)/shard_map/ppermute | solution.py:435

commit v6 on v5

--- a/solution.py
+++ b/solution.py
@@ -122,19 +122,25 @@
 
 
 def forward_kernel(
-    occ, ytab, zt_hi, zt_lo, own_ref, one_ref, two_ref, three_ref,
-    occ_v, ytab_v, zt_hi_v, zt_lo_v, small_ref, rows_ref, tile_ref, sems,
+    occ, ytab, zt_hi, zt_lo, xi_hi, xi_lo, xo_hi, xo_lo, z_hi, z_lo, ylane, phase, emb, weight, pw,
+    pb, w1, b1, w2, b2, own_ref, one_ref, two_ref, three_ref, label_ref, *rest
 ):
-    pairs = [(occ, occ_v), (ytab, ytab_v), (zt_hi, zt_hi_v), (zt_lo, zt_lo_v)]
+    held, (ytab_v, zt_hi_v, zt_lo_v, small_ref, rows_ref, tile_ref, sems) = rest[:16], rest[16:]
+    pairs = [(occ.at[:, pl.ds(half * 128, 128)], label_ref.at[half]) for half in range(2)]
+    pairs += [(ytab, ytab_v), (zt_hi, zt_hi_v), (zt_lo, zt_lo_v)]
+    later = [xi_hi, xi_lo, emb, weight, pw, pb, w1, b1, w2, b2, phase]
+    later += [xo_hi, xo_lo, z_hi, z_lo, ylane]
+    pairs += list(zip(later, held))
     copies = [pltpu.make_async_copy(a, b, sems.at[i]) for i, (a, b) in enumerate(pairs)]
     for copy in copies:
         copy.start()
     for label in range(NCLASS, 16):
         for quarter in range(4):
             rows_ref[quarter, pl.ds(label, 32, stride=16), :] = jnp.zeros((32, 128), f32)
-    copies[0].wait()
-    copies[1].wait()
-    small_ref[...] = occ_v[...].astype(f32).astype(bf16)
+    for copy in copies[:3]:
+        copy.wait()
+    for half in range(2):
+        small_ref[:, half * 128 : (half + 1) * 128] = label_ref[half].astype(f32).astype(bf16)
     for label in range(NCLASS):
         same = small_ref[...] == jnp.array(label, bf16)
         hot = jnp.where(same, jnp.array(1.0, bf16), jnp.array(0.0, bf16))
@@ -143,8 +149,8 @@
             rows_ref[quarter, pl.ds(label, 32, stride=16), :] = part[
                 :, quarter * 128 : (quarter + 1) * 128
             ]
-    copies[2].wait()
-    copies[3].wait()
+    for copy in copies[3:]:
+        copy.wait()
     nt = ((1,), (1,))
     for pair in range(2):
         block = [rows_ref[quarter, pl.ds(pair * 256, 256), :] for quarter in range(4)]
@@ -163,24 +169,9 @@
 
 
 def prepare_kernel(
-    occ, xi_hi, xi_lo, xo_hi, xo_lo, z_hi, z_lo, ylane, phase, emb, weight, pw, pb, w1, b1, w2, b2,
-    wide_ref, rep_ref, xi_hi_out, xi_lo_out, xo_hi_out, xo_lo_out, z_hi_out, z_lo_out,
-    ylane_out, label_ref, phase_out, table_ref, wide1_ref, wide2_ref, bias2_ref,
-    occ_v, phase_v, emb_v, weight_v, pw_v, pb_v, w1_v, b1_v, w2_v, b2_v, sems,
+    emb_v, weight_v, pw_v, pb_v, w1_v, b1_v, w2_v, b2_v, phase_v,
+    wide_ref, rep_ref, phase_out, table_ref, wide1_ref, wide2_ref, bias2_ref,
 ):
-    pairs = [
-        (occ, occ_v), (emb, emb_v), (weight, weight_v), (pw, pw_v), (pb, pb_v), (w1, w1_v),
-        (b1, b1_v), (w2, w2_v), (b2, b2_v), (phase, phase_v), (xi_hi, xi_hi_out),
-        (xi_lo, xi_lo_out), (xo_hi, xo_hi_out), (xo_lo, xo_lo_out), (z_hi, z_hi_out),
-        (z_lo, z_lo_out), (ylane, ylane_out),
-    ]
-    copies = [pltpu.make_async_copy(a, b, sems.at[i]) for i, (a, b) in enumerate(pairs)]
-    for copy in copies:
-        copy.start()
-    for copy in copies:
-        copy.wait()
-    for half in range(2):
-        label_ref[half] = occ_v[:, half * 128 : (half + 1) * 128]
     left = jnp.where(iota((128, NCLASS), 0) % 16 == iota((128, NCLASS), 1), 1.0, 0.0).astype(f32)
     right = jnp.where(iota((16, 128), 1) % 16 == iota((16, 128), 0), 1.0, 0.0).astype(f32)
     lifted = dot(left, emb_v[...], precision=highest)
@@ -455,86 +446,84 @@
     z_hi, z_lo = split(z_tables())
     x_hi, x_lo = split(x_tables())
     shape = jax.ShapeDtypeStruct
-    labels = occupancy.reshape(ROWS, NY)
-    partial = pl.pallas_call(
+    sources = far(
+        occupancy.reshape(ROWS, NY),
+        ytab,
+        z_hi.T.copy(),
+        z_lo.T.copy(),
+        x_hi.transpose(2, 0, 1).reshape(256, 256),
+        x_lo.transpose(2, 0, 1).reshape(256, 256),
+        x_hi.transpose(1, 0, 2).reshape(128, 512),
+        x_lo.transpose(1, 0, 2).reshape(128, 512),
+        z_hi,
+        z_lo,
+        y_lanes(ytab),
+        pen_phases(),
+        embedding,
+        spectral_weight.reshape(512, 16),
+        point_weight,
+        point_bias.reshape(1, CH),
+        expand_weight,
+        expand_bias.reshape(1, HIDDEN),
+        reduce_weight.T,
+        reduce_bias.reshape(1, CH),
+    )
+    made = pl.pallas_call(
         forward_kernel,
-        out_shape=[shape((128, 128), f32)] * 4,
-        in_specs=[pl.BlockSpec(memory_space=pltpu.HBM)] * 4,
-        out_specs=[vmem()] * 4,
+        out_shape=[shape((128, 128), f32)] * 4
+        + [
+            shape((2, ROWS, 128), jnp.int32),
+            shape((256, 256), bf16),
+            shape((256, 256), bf16),
+            shape((NCLASS, CH), f32),
+            shape((512, 16), f32),
+            shape((CH, CH), f32),
+            shape((1, CH), f32),
+            shape((CH, HIDDEN), bf16),
+            shape((1, HIDDEN), f32),
+            shape((CH, HIDDEN), bf16),
+            shape((1, CH), f32),
+            shape((64, 128), f32),
+            shape((128, 512), bf16),
+            shape((128, 512), bf16),
+            shape((512, 256), bf16),
+            shape((512, 256), bf16),
+            shape((256, 256), bf16),
+        ],
+        in_specs=[pl.BlockSpec(memory_space=pltpu.HBM)] * 20,
+        out_specs=[vmem()] * 21,
         scratch_shapes=[
-            pltpu.VMEM((ROWS, NY), jnp.int32),
             pltpu.VMEM((32, 256), bf16),
             pltpu.VMEM((256, 512), bf16),
             pltpu.VMEM((256, 512), bf16),
             pltpu.VMEM((ROWS, NY), bf16),
             pltpu.VMEM((4, 512, 128), f32),
             pltpu.VMEM((4, 128, 128), f32),
-            pltpu.SemaphoreType.DMA((4,)),
+            pltpu.SemaphoreType.DMA((21,)),
         ],
         compiler_params=room(16),
-        cost_estimate=pl.CostEstimate(flops=400000000, bytes_accessed=1000000, transcendentals=0),
+        cost_estimate=pl.CostEstimate(flops=400000000, bytes_accessed=3000000, transcendentals=0),
         name="forward",
-    )(*far(labels, ytab, z_hi.T.copy(), z_lo.T.copy()))
-    made = pl.pallas_call(
+    )(*sources)
+    partial, (labels, xi_hi, xi_lo), small = made[:4], made[4:7], made[7:16]
+    xo_hi, xo_lo, z_hi, z_lo, ylane = made[16:]
+    wide, weight, phases, table, wide1, wide2, bias2 = pl.pallas_call(
         prepare_kernel,
         out_shape=[
             shape((128, 128), f32),
             shape((512, 128), f32),
-            shape((256, 256), bf16),
-            shape((256, 256), bf16),
-            shape((128, 512), bf16),
-            shape((128, 512), bf16),
-            shape((512, 256), bf16),
-            shape((512, 256), bf16),
-            shape((256, 256), bf16),
-            shape((2, 512, 128), jnp.int32),
             shape((2, 16, 128), f32),
             shape((16, 128), f32),
             shape((512, 256), bf16),
             shape((128, 512), bf16),
             shape((128, 128), f32),
         ],
-        in_specs=[pl.BlockSpec(memory_space=pltpu.HBM)] * 17,
-        out_specs=[vmem()] * 15,
-        scratch_shapes=[
-            pltpu.VMEM((ROWS, NY), jnp.int32),
-            pltpu.VMEM((64, 128), f32),
-            pltpu.VMEM((NCLASS, CH), f32),
-            pltpu.VMEM((512, 16), f32),
-            pltpu.VMEM((CH, CH), f32),
-            pltpu.VMEM((1, CH), f32),
-            pltpu.VMEM((CH, HIDDEN), bf16),
-            pltpu.VMEM((1, HIDDEN), f32),
-            pltpu.VMEM((CH, HIDDEN), bf16),
-            pltpu.VMEM((1, CH), f32),
-            pltpu.SemaphoreType.DMA((17,)),
-        ],
-        compiler_params=room(16),
-        cost_estimate=pl.CostEstimate(flops=200000000, bytes_accessed=3000000, transcendentals=0),
+        in_specs=[vmem()] * 9,
+        out_specs=[vmem()] * 7,
+        compiler_params=room(8),
+        cost_estimate=pl.CostEstimate(flops=200000000, bytes_accessed=1000000, transcendentals=0),
         name="prepare",
-    )(
-        *far(
-            labels,
-            x_hi.transpose(2, 0, 1).reshape(256, 256),
-            x_lo.transpose(2, 0, 1).reshape(256, 256),
-            x_hi.transpose(1, 0, 2).reshape(128, 512),
-            x_lo.transpose(1, 0, 2).reshape(128, 512),
-            z_hi,
-            z_lo,
-            y_lanes(ytab),
-            pen_phases(),
-            embedding,
-            spectral_weight.reshape(512, 16),
-            point_weight,
-            point_bias.reshape(1, CH),
-            expand_weight,
-            expand_bias.reshape(1, HIDDEN),
-            reduce_weight.T,
-            reduce_bias.reshape(1, CH),
-        )
-    )
-    wide, weight, xi_hi, xi_lo, xo_hi, xo_lo = made[:6]
-    z_hi, z_lo, ylane, labels, phases, table, wide1, wide2, bias2 = made[6:]
+    )(*small)
     partial = rotate(partial)
     chunks = pl.pallas_call(
         gather_groups_kernel,

time: 71 us -> 71.2 us (level)
  Pallas kernels: 19.4 us -> 17.8 us
  waiting for transfers between devices: 3.49 us -> 4.87 us
    pallas_call x1, Pallas kernels: 2.59 us -> 0.85 us  [shards(): pl.pallas_call(prepare_kernel, out_shape=[shape((128, 128), f32), shape((...]
    ppermute x6, waiting for transfers between devices: 3.49 us -> 4.87 us  [rotate(): lax.ppermute(tiles[k], 'grp', [(i, (i + k) % 4) for i in range(4)])]
  transfers between devices with their start and end apart: 6 -> 6, of which waited for: 3 -> 5; matrix products, arithmetic and copies ran while one was open for 0% -> 0% of each run, Pallas kernels for 4% -> 1%
where the time goes in v6:
time: 71.2 us; the launch traced here: 71 us
  blocking collectives  38.9 us (55%)
  Pallas kernels  17.8 us (25%)
  starting transfers between devices  9.35 us (13%)
  waiting for transfers between devices  4.87 us (7%)
    all_to_all x1, blocking collectives, shards(): chunks = lax.all_to_all(chunks.reshape(64, 4, 128), 'pen', 0, 0, tiled=True)  23.9 us
    all_to_all x1, blocking collectives, shards(): mixed = lax.all_to_all(mixed.reshape(64, 4, 128), 'pen', 0, 0, tiled=True)  15 us
    pallas_call x1, Pallas kernels, shards(): pl.pallas_call(point_kernel, out_shape=shape((CH, LZ, LX, NY), bf16), gri...  11.9 us
    ppermute x6, starting transfers between devices, rotate(): lax.ppermute(tiles[k], 'grp', [(i, (i + k) % 4) for i in range(4)])  9.35 us
    ppermute x6, waiting for transfers between devices, rotate(): lax.ppermute(tiles[k], 'grp', [(i, (i + k) % 4) for i in range(4)])  4.87 us
    pallas_call x1, Pallas kernels, shards(): pl.pallas_call(forward_kernel, out_shape=[shape((128, 128), f32)] * 4 + [...  3.42 us
  transfers between devices with their start and end apart: 6, of which 5 were waited for; matrix products, arithmetic and copies ran while one was open for 0% of the time, Pallas kernels for 1%

profile of v6, /device:TPU:1, one launch (start us, length us, event | category | flops | bytes accessed | tf_op | source)
XLA Modules:
  0.0 71.0 jit_solution(9595709126522267845)
XLA Ops:
  0.0 3.4 %forward.1 = (f32[128,128]{1,0:T(8,128)S(1)}, f32[128,128]{1,0:T(8,128)S(1)}, f32[128,128]{1,0:T(8,128)S(1)}, f32[128,128]{1,0:T(8,128)S(1)}, s32[2,512,128]{2,1...) custom-call(s32[512,256]{1,0:T(8,128)} %bitcast.14, ...), custom_call_target="tpu_custom_call" | custom-call | flops 400000000 | bytes 3000000 | tf_op jit(solution)/shard_map/forward/pallas_call | solution.py:471
  3.4 2.1 %collective-permute-start = (f32[128,128]{1,0:T(8,128)S(1)}, f32[128,128]{1,0:T(8,128)S(1)}, u32[]{:S(2)}, u32[]{:S(2)}) collective-permute-start(f32[128,128]{1,0:T(8,128)S(1)} %get-tuple-element.52), channel_id=1, source_target_pairs={{0,64},{64,128},{128,192},{192,0},{1,65},{65,129},{129,193},{193,1... | collective-permute-start | bytes 196616 | tf_op jit(solution)/shard_map/ppermute | solution.py:426
  5.5 2.5 %collective-permute-start.1 = (f32[128,128]{1,0:T(8,128)S(1)}, f32[128,128]{1,0:T(8,128)S(1)}, u32[]{:S(2)}, u32[]{:S(2)}) collective-permute-start(f32[128,128]{1,0:T(8,128)S(1)} %get-tuple-element.53), channel_id=1, source_target_pairs={{0,128},{64,192},{128,0},{192,64},{1,129},{65,193},{129,1},{193,65... | collective-permute-start | bytes 196616 | tf_op jit(solution)/shard_map/ppermute | solution.py:426
  8.0 1.2 %collective-permute-start.2 = (f32[128,128]{1,0:T(8,128)S(1)}, f32[128,128]{1,0:T(8,128)S(1)}, u32[]{:S(2)}, u32[]{:S(2)}) collective-permute-start(f32[128,128]{1,0:T(8,128)S(1)} %get-tuple-element.54), channel_id=1, source_target_pairs={{0,192},{64,0},{128,64},{192,128},{1,193},{65,1},{129,65},{193,129... | collective-permute-start | bytes 196616 | tf_op jit(solution)/shard_map/ppermute | solution.py:426
  9.2 0.9 %prepare.1 = (f32[128,128]{1,0:T(8,128)S(1)}, f32[512,128]{1,0:T(8,128)S(1)}, f32[2,16,128]{2,1,0:T(8,128)S(1)}, f32[16,128]{1,0:T(8,128)S(1)}, bf16[512,256]{1,...) custom-call(f32[12,16]{1,0:T(8,128)S(1)} %get-tuple-element.37.emb_v, ...), custom_call_target="tpu_custom_call" | custom-call | flops 200000000 | bytes 1000000 | tf_op jit(solution)/shard_map/prepare/pallas_call | solution.py:510
  10.0 0.0 collective-permute-done.one_ref
  10.0 0.6 collective-permute-done.1.two_ref
  10.6 0.8 %collective-permute-done.2.three_ref = f32[128,128]{1,0:T(8,128)S(1)} collective-permute-done((f32[128,128]{1,0:T(8,128)S(1)}, f32[128,128]{1,0:T(8,128)S(1)}, u32[]{:S(2)}, u32[]{:S(2)}) %collective-permute-start.2) | collective-permute-done | bytes 65568 | tf_op jit(solution)/shard_map/ppermute | solution.py:426
  11.4 0.6 gather_groups.1
  12.0 23.9 %all_to_all.10 = f32[64,4,128]{2,1,0:T(4,128)S(1)} all-to-all(f32[64,4,128]{2,1,0:T(4,128)S(1)} %bitcast.11), channel_id=1, replica_groups=mesh['grp'=4,'pen'=64] {'pen'}, dimensions={0} | all-to-all | bytes 262144 | tf_op jit(solution)/shard_map/all_to_all | solution.py:537
  35.9 0.4 mix.1
  36.4 15.0 %all_to_all.11 = f32[64,4,128]{2,1,0:T(4,128)S(1)} all-to-all(f32[64,4,128]{2,1,0:T(4,128)S(1)} %bitcast.13), channel_id=1, replica_groups=mesh['grp'=4,'pen'=64] {'pen'}, dimensions={0} | all-to-all | bytes 262144 | tf_op jit(solution)/shard_map/all_to_all | solution.py:546
  51.4 0.6 scatter_groups.1
  52.0 0.4 collective-permute-start.3
  52.4 3.3 %collective-permute-start.4 = (f32[128,128]{1,0:T(8,128)S(1)}, f32[128,128]{1,0:T(8,128)S(1)}, u32[]{:S(2)}, u32[]{:S(2)}) collective-permute-start(f32[128,128]{1,0:T(8,128)S(1)} %get-tuple-element.59), channel_id=1, source_target_pairs={{0,128},{64,192},{128,0},{192,64},{1,129},{65,193},{129,1},{193,65... | collective-permute-start | bytes 196616 | tf_op jit(solution)/shard_map/ppermute | solution.py:426
  55.6 0.0 collective-permute-start.5
  55.6 0.8 %collective-permute-done.3.one_ref = f32[128,128]{1,0:T(8,128)S(1)} collective-permute-done((f32[128,128]{1,0:T(8,128)S(1)}, f32[128,128]{1,0:T(8,128)S(1)}, u32[]{:S(2)}, u32[]{:S(2)}) %collective-permute-start.3) | collective-permute-done | bytes 65568 | tf_op jit(solution)/shard_map/ppermute | solution.py:426
  56.4 2.1 %collective-permute-done.4.two_ref = f32[128,128]{1,0:T(8,128)S(1)} collective-permute-done((f32[128,128]{1,0:T(8,128)S(1)}, f32[128,128]{1,0:T(8,128)S(1)}, u32[]{:S(2)}, u32[]{:S(2)}) %collective-permute-start.4) | collective-permute-done | bytes 65568 | tf_op jit(solution)/shard_map/ppermute | solution.py:426
  58.5 0.6 collective-permute-done.5.three_ref
  59.1 11.9 %point.1 = bf16[16,64,8,256]{3,2,1,0:T(8,128)(2,1)} custom-call(f32[128,128]{1,0:T(8,128)S(1)} %get-tuple-element.57.own_ref, f32[128,128]{1,0:T(8,128)S(1)} %collective-permute-done.3.one_ref, f32[128,128]{1,0:T(8,128)S(1)} %collective-permute-done.4.two_ref, f32[128,128]{1,0:T(8,128)S(1)} %collective-permute-done.5.three_ref, ...), custom_call_target="tpu_custom_call" | custom-call | tf_op jit(solution)/shard_map/point/pallas_call | solution.py:557
Async XLA Ops:
  3.4 6.6 %collective-permute-start = (f32[128,128]{1,0:T(8,128)S(1)}, f32[128,128]{1,0:T(8,128)S(1)}, u32[]{:S(2)}, u32[]{:S(2)}) collective-permute-start(f32[128,128]{1,0:T(8,128)S(1)} %get-tuple-element.52), channel_id=1, source_target_pairs={{0,64},{64,128},{128,192},{192,0},{1,65},{65,129},{129,193},{193,1... | collective-permute-start | bytes 196616 | tf_op jit(solution)/shard_map/ppermute | solution.py:426
  5.5 5.1 %collective-permute-start.1 = (f32[128,128]{1,0:T(8,128)S(1)}, f32[128,128]{1,0:T(8,128)S(1)}, u32[]{:S(2)}, u32[]{:S(2)}) collective-permute-start(f32[128,128]{1,0:T(8,128)S(1)} %get-tuple-element.53), channel_id=1, source_target_pairs={{0,128},{64,192},{128,0},{192,64},{1,129},{65,193},{129,1},{193,65... | collective-permute-start | bytes 196616 | tf_op jit(solution)/shard_map/ppermute | solution.py:426
  8.0 3.4 %collective-permute-start.2 = (f32[128,128]{1,0:T(8,128)S(1)}, f32[128,128]{1,0:T(8,128)S(1)}, u32[]{:S(2)}, u32[]{:S(2)}) collective-permute-start(f32[128,128]{1,0:T(8,128)S(1)} %get-tuple-element.54), channel_id=1, source_target_pairs={{0,192},{64,0},{128,64},{192,128},{1,193},{65,1},{129,65},{193,129... | collective-permute-start | bytes 196616 | tf_op jit(solution)/shard_map/ppermute | solution.py:426
  52.0 4.4 %collective-permute-start.3 = (f32[128,128]{1,0:T(8,128)S(1)}, f32[128,128]{1,0:T(8,128)S(1)}, u32[]{:S(2)}, u32[]{:S(2)}) collective-permute-start(f32[128,128]{1,0:T(8,128)S(1)} %get-tuple-element.58), channel_id=1, source_target_pairs={{0,64},{64,128},{128,192},{192,0},{1,65},{65,129},{129,193},{193,1... | collective-permute-start | bytes 196616 | tf_op jit(solution)/shard_map/ppermute | solution.py:426
  52.4 6.2 %collective-permute-start.4 = (f32[128,128]{1,0:T(8,128)S(1)}, f32[128,128]{1,0:T(8,128)S(1)}, u32[]{:S(2)}, u32[]{:S(2)}) collective-permute-start(f32[128,128]{1,0:T(8,128)S(1)} %get-tuple-element.59), channel_id=1, source_target_pairs={{0,128},{64,192},{128,0},{192,64},{1,129},{65,193},{129,1},{193,65... | collective-permute-start | bytes 196616 | tf_op jit(solution)/shard_map/ppermute | solution.py:426
  55.6 3.5 %collective-permute-start.5 = (f32[128,128]{1,0:T(8,128)S(1)}, f32[128,128]{1,0:T(8,128)S(1)}, u32[]{:S(2)}, u32[]{:S(2)}) collective-permute-start(f32[128,128]{1,0:T(8,128)S(1)} %get-tuple-element.60), channel_id=1, source_target_pairs={{0,192},{64,0},{128,64},{192,128},{1,193},{65,1},{129,65},{193,129... | collective-permute-start | bytes 196616 | tf_op jit(solution)/shard_map/ppermute | solution.py:426

commit v7 on v6

--- a/solution.py
+++ b/solution.py
@@ -20,6 +20,7 @@
 LZ = 64
 LX = 8
 ROWS = LZ * LX
+ORDER = (0, 2, 1, 3)
 
 highest = lax.Precision.HIGHEST
 f32 = jnp.float32
@@ -69,9 +70,9 @@
 def pen_phases():
     turn = np.remainder(np.arange(64)[:, None] * FREQ[None, :], 64)
     angles = 2.0 * np.pi * turn / 64
-    table = np.zeros((64, 128), np.float32)
-    table[:, 0:16] = np.cos(angles)
-    table[:, 16:32] = np.sin(angles)
+    table = np.zeros((80, 128), np.float32)
+    table[:64, 0:16] = np.cos(angles)
+    table[:64, 16:32] = np.sin(angles)
     return table
 
 
@@ -123,24 +124,26 @@
 
 def forward_kernel(
     occ, ytab, zt_hi, zt_lo, xi_hi, xi_lo, xo_hi, xo_lo, z_hi, z_lo, ylane, phase, emb, weight, pw,
-    pb, w1, b1, w2, b2, own_ref, one_ref, two_ref, three_ref, label_ref, *rest
+    pb, w1, b1, w2, b2, own_ref, first_ref, second_ref, third_ref, label_ref, *rest
 ):
     held, (ytab_v, zt_hi_v, zt_lo_v, small_ref, rows_ref, tile_ref, sems) = rest[:16], rest[16:]
-    pairs = [(occ.at[:, pl.ds(half * 128, 128)], label_ref.at[half]) for half in range(2)]
+    pairs = [(occ.at[:, pl.ds(half * 128, 128)], label_ref.at[half, pl.ds(0, ROWS)]) for half in range(2)]
     pairs += [(ytab, ytab_v), (zt_hi, zt_hi_v), (zt_lo, zt_lo_v)]
     later = [xi_hi, xi_lo, emb, weight, pw, pb, w1, b1, w2, b2, phase]
     later += [xo_hi, xo_lo, z_hi, z_lo, ylane]
     pairs += list(zip(later, held))
     copies = [pltpu.make_async_copy(a, b, sems.at[i]) for i, (a, b) in enumerate(pairs)]
-    for copy in copies:
+    for copy in copies[:5]:
         copy.start()
     for label in range(NCLASS, 16):
         for quarter in range(4):
             rows_ref[quarter, pl.ds(label, 32, stride=16), :] = jnp.zeros((32, 128), f32)
     for copy in copies[:3]:
         copy.wait()
+    for copy in copies[5:]:
+        copy.start()
     for half in range(2):
-        small_ref[:, half * 128 : (half + 1) * 128] = label_ref[half].astype(f32).astype(bf16)
+        small_ref[:, half * 128 : (half + 1) * 128] = label_ref[half, 0:ROWS].astype(f32).astype(bf16)
     for label in range(NCLASS):
         same = small_ref[...] == jnp.array(label, bf16)
         hot = jnp.where(same, jnp.array(1.0, bf16), jnp.array(0.0, bf16))
@@ -149,7 +152,7 @@
             rows_ref[quarter, pl.ds(label, 32, stride=16), :] = part[
                 :, quarter * 128 : (quarter + 1) * 128
             ]
-    for copy in copies[3:]:
+    for copy in copies[3:5]:
         copy.wait()
     nt = ((1,), (1,))
     for pair in range(2):
@@ -164,8 +167,10 @@
             tile = full[:, half * 128 : (half + 1) * 128]
             tile_ref[pair * 2 + half] = tile[:128] - times_j(tile[128:])
     here = lax.axis_index("grp")
-    for k, ref in enumerate((own_ref, one_ref, two_ref, three_ref)):
+    for k, ref in zip(ORDER, (own_ref, first_ref, second_ref, third_ref)):
         ref[...] = tile_ref[(here + k) % 4]
+    for copy in copies[5:]:
+        copy.wait()
 
 
 def prepare_kernel(
@@ -220,9 +225,9 @@
     bias2_ref[...] = jnp.broadcast_to(col2, (128, 128))
 
 
-def gather_groups_kernel(phase_ref, hi_ref, lo_ref, own_ref, one_ref, two_ref, three_ref, out_ref, in_ref):
+def gather_groups_kernel(phase_ref, hi_ref, lo_ref, own_ref, first_ref, second_ref, third_ref, out_ref, in_ref):
     here = lax.axis_index("grp")
-    for k, ref in enumerate((own_ref, one_ref, two_ref, three_ref)):
+    for k, ref in zip(ORDER, (own_ref, first_ref, second_ref, third_ref)):
         in_ref[(here + 4 - k) % 4] = ref[...]
     cos, sin, flip = quarter_signs((128, 128))
     real = in_ref[0] + flip * in_ref[2] + cos * (in_ref[1] + in_ref[3])
@@ -266,7 +271,7 @@
         out_ref[pl.ds(step * 8, 8), :] = tile
 
 
-def scatter_groups_kernel(phase_ref, hi_ref, lo_ref, in_ref, own_ref, one_ref, two_ref, three_ref, out_ref):
+def scatter_groups_kernel(phase_ref, hi_ref, lo_ref, in_ref, own_ref, first_ref, second_ref, third_ref, out_ref):
     real = [None] * 16
     imag = [None] * 16
     for kz_hi in range(4):
@@ -283,7 +288,7 @@
     out_ref[2] = flip * real
     out_ref[3] = cos * real - sin * imag
     here = lax.axis_index("grp")
-    for k, ref in enumerate((own_ref, one_ref, two_ref, three_ref)):
+    for k, ref in zip(ORDER, (own_ref, first_ref, second_ref, third_ref)):
         ref[...] = out_ref[(here + k) % 4]
 
 
@@ -313,31 +318,10 @@
 
 
 def point_kernel(
-    own_ref, one_ref, two_ref, three_ref, hi_ref, lo_ref, ytab_ref, label_ref, table_ref, wide1_ref, wide2_ref, bias2_ref,
+    own_ref, first_ref, second_ref, third_ref, hi_ref, lo_ref, ytab_ref, label_ref, table_ref, wide1_ref, wide2_ref, bias2_ref,
     out_ref, planes_ref, act_ref, pre_ref, modes_ref,
 ):
     step = pl.program_id(0)
-
-    @pl.when(step == 0)
-    def _():
-        here = lax.axis_index("grp")
-        for k, ref in enumerate((own_ref, one_ref, two_ref, three_ref)):
-            modes_ref[(here + 4 - k) % 4] = ref[...]
-        high_lane = (iota((128, 128), 1) // 8) % 2 == 1
-        for c_hi in range(2):
-            tiles = []
-            for pair in range(2):
-                even = modes_ref[2 * pair]
-                odd = modes_ref[2 * pair + 1]
-                if c_hi == 0:
-                    tile = jnp.where(high_lane, pltpu.roll(odd, 8, 1), even)
-                else:
-                    tile = jnp.where(high_lane, odd, pltpu.roll(even, 120, 1))
-                tiles.append(jnp.concatenate([tile, times_j(tile)], axis=0))
-            full = three(hi_ref[...], lo_ref[...], jnp.concatenate(tiles, axis=1))
-            full = full.astype(bf16).astype(f32)
-            planes_ref[c_hi * 2] = full[:, 0:128]
-            planes_ref[c_hi * 2 + 1] = full[:, 128:256]
 
     def finish(sub):
         slot = sub % 2
@@ -385,6 +369,24 @@
 
     @pl.when(step == 0)
     def _():
+        here = lax.axis_index("grp")
+        for k, ref in zip(ORDER, (own_ref, first_ref, second_ref, third_ref)):
+            modes_ref[(here + 4 - k) % 4] = ref[...]
+        high_lane = (iota((128, 128), 1) // 8) % 2 == 1
+        for c_hi in range(2):
+            tiles = []
+            for pair in range(2):
+                even = modes_ref[2 * pair]
+                odd = modes_ref[2 * pair + 1]
+                if c_hi == 0:
+                    tile = jnp.where(high_lane, pltpu.roll(odd, 8, 1), even)
+                else:
+                    tile = jnp.where(high_lane, odd, pltpu.roll(even, 120, 1))
+                tiles.append(jnp.concatenate([tile, times_j(tile)], axis=0))
+            full = three(hi_ref[...], lo_ref[...], jnp.concatenate(tiles, axis=1))
+            full = full.astype(bf16).astype(f32)
+            planes_ref[c_hi * 2, 0:ROWS] = full[:, 0:128]
+            planes_ref[c_hi * 2 + 1, 0:ROWS] = full[:, 128:256]
         for slot in range(2):
             act_ref[slot, 128:144] = jnp.ones((16, 512), bf16)
             activate(transform(slot), slot, slot)
@@ -422,8 +424,8 @@
 
 def rotate(tiles):
     moved = [tiles[0]]
-    for k in range(1, 4):
-        moved.append(lax.ppermute(tiles[k], "grp", [(i, (i + k) % 4) for i in range(4)]))
+    for k, tile in zip(ORDER[1:], tiles[1:]):
+        moved.append(lax.ppermute(tile, "grp", [(i, (i + k) % 4) for i in range(4)]))
     return moved
 
 
@@ -472,7 +474,7 @@
         forward_kernel,
         out_shape=[shape((128, 128), f32)] * 4
         + [
-            shape((2, ROWS, 128), jnp.int32),
+            shape((2, ROWS + 8, 128), jnp.int32),
             shape((256, 256), bf16),
             shape((256, 256), bf16),
             shape((NCLASS, CH), f32),
@@ -483,7 +485,7 @@
             shape((1, HIDDEN), f32),
             shape((CH, HIDDEN), bf16),
             shape((1, CH), f32),
-            shape((64, 128), f32),
+            shape((80, 128), f32),
             shape((128, 512), bf16),
             shape((128, 512), bf16),
             shape((512, 256), bf16),
@@ -561,7 +563,7 @@
         in_specs=[vmem()] * 12,
         out_specs=pl.BlockSpec((CH, ZB, LX, NY), lambda i: (0, i, 0, 0)),
         scratch_shapes=[
-            pltpu.VMEM((4, 512, 128), f32),
+            pltpu.VMEM((4, ROWS + 8, 128), f32),
             pltpu.VMEM((2, 144, 512), bf16),
             pltpu.VMEM((2, 512, 512), f32),
             pltpu.VMEM((4, 128, 128), f32),

time: 71.2 us -> 70.9 us (level)
  starting transfers between devices: 9.35 us -> 10.3 us
    ppermute x6, starting transfers between devices: 9.35 us -> 10.3 us  [rotate(): lax.ppermute(tile, 'grp', [(i, (i + k) % 4) for i in range(4)])]
  transfers between devices with their start and end apart: 6 -> 6, of which waited for: 5 -> 4; matrix products, arithmetic and copies ran while one was open for 0% -> 0% of each run, Pallas kernels for 1% -> 1%
where the time goes in v7:
time: 70.9 us; the launch traced here: 70.7 us
  blocking collectives  38.2 us (54%)
  Pallas kernels  17.5 us (25%)
  starting transfers between devices  10.3 us (15%)
  waiting for transfers between devices  4.68 us (7%)
    all_to_all x1, blocking collectives, shards(): chunks = lax.all_to_all(chunks.reshape(64, 4, 128), 'pen', 0, 0, tiled=True)  23.2 us
    all_to_all x1, blocking collectives, shards(): mixed = lax.all_to_all(mixed.reshape(64, 4, 128), 'pen', 0, 0, tiled=True)  15 us
    pallas_call x1, Pallas kernels, shards(): pl.pallas_call(point_kernel, out_shape=shape((CH, LZ, LX, NY), bf16), gri...  11.6 us
    ppermute x6, starting transfers between devices, rotate(): lax.ppermute(tile, 'grp', [(i, (i + k) % 4) for i in range(4)])  10.3 us
    ppermute x6, waiting for transfers between devices, rotate(): lax.ppermute(tile, 'grp', [(i, (i + k) % 4) for i in range(4)])  4.68 us
    pallas_call x1, Pallas kernels, shards(): pl.pallas_call(forward_kernel, out_shape=[shape((128, 128), f32)] * 4 + [...  3.45 us
  transfers between devices with their start and end apart: 6, of which 4 were waited for; matrix products, arithmetic and copies ran while one was open for 0% of the time, Pallas kernels for 1%

profile of v7, /device:TPU:1, one launch (start us, length us, event | category | flops | bytes accessed | tf_op | source)
XLA Modules:
  0.0 70.7 jit_solution(7138134022305776579)
XLA Ops:
  0.0 3.4 %forward.1 = (f32[128,128]{1,0:T(8,128)S(1)}, f32[128,128]{1,0:T(8,128)S(1)}, f32[128,128]{1,0:T(8,128)S(1)}, f32[128,128]{1,0:T(8,128)S(1)}, s32[2,520,128]{2,1...) custom-call(s32[512,256]{1,0:T(8,128)} %bitcast.14, ...), custom_call_target="tpu_custom_call" | custom-call | flops 400000000 | bytes 3000000 | tf_op jit(solution)/shard_map/forward/pallas_call | solution.py:473
  3.5 3.7 %collective-permute-start = (f32[128,128]{1,0:T(8,128)S(1)}, f32[128,128]{1,0:T(8,128)S(1)}, u32[]{:S(2)}, u32[]{:S(2)}) collective-permute-start(f32[128,128]{1,0:T(8,128)S(1)} %get-tuple-element.52), channel_id=1, source_target_pairs={{0,128},{64,192},{128,0},{192,64},{1,129},{65,193},{129,1},{193,65... | collective-permute-start | bytes 196616 | tf_op jit(solution)/shard_map/ppermute | solution.py:428
  7.1 0.3 collective-permute-start.1
  7.4 2.4 %collective-permute-start.2 = (f32[128,128]{1,0:T(8,128)S(1)}, f32[128,128]{1,0:T(8,128)S(1)}, u32[]{:S(2)}, u32[]{:S(2)}) collective-permute-start(f32[128,128]{1,0:T(8,128)S(1)} %get-tuple-element.54), channel_id=1, source_target_pairs={{0,192},{64,0},{128,64},{192,128},{1,193},{65,1},{129,65},{193,129... | collective-permute-start | bytes 196616 | tf_op jit(solution)/shard_map/ppermute | solution.py:428
  9.8 0.8 %prepare.1 = (f32[128,128]{1,0:T(8,128)S(1)}, f32[512,128]{1,0:T(8,128)S(1)}, f32[2,16,128]{2,1,0:T(8,128)S(1)}, f32[16,128]{1,0:T(8,128)S(1)}, bf16[512,256]{1,...) custom-call(f32[12,16]{1,0:T(8,128)S(1)} %get-tuple-element.37.emb_v, ...), custom_call_target="tpu_custom_call" | custom-call | flops 200000000 | bytes 1000000 | tf_op jit(solution)/shard_map/prepare/pallas_call | solution.py:512
  10.6 0.0 collective-permute-done.first_ref
  10.7 1.5 %collective-permute-done.1.second_ref = f32[128,128]{1,0:T(8,128)S(1)} collective-permute-done((f32[128,128]{1,0:T(8,128)S(1)}, f32[128,128]{1,0:T(8,128)S(1)}, u32[]{:S(2)}, u32[]{:S(2)}) %collective-permute-start.1) | collective-permute-done | bytes 65568 | tf_op jit(solution)/shard_map/ppermute | solution.py:428
  12.2 0.0 collective-permute-done.2.third_ref
  12.2 0.6 gather_groups.1
  12.8 23.2 %all_to_all.10 = f32[64,4,128]{2,1,0:T(4,128)S(1)} all-to-all(f32[64,4,128]{2,1,0:T(4,128)S(1)} %bitcast.11), channel_id=1, replica_groups=mesh['grp'=4,'pen'=64] {'pen'}, dimensions={0} | all-to-all | bytes 262144 | tf_op jit(solution)/shard_map/all_to_all | solution.py:539
  36.0 0.4 mix.1
  36.4 15.0 %all_to_all.11 = f32[64,4,128]{2,1,0:T(4,128)S(1)} all-to-all(f32[64,4,128]{2,1,0:T(4,128)S(1)} %bitcast.13), channel_id=1, replica_groups=mesh['grp'=4,'pen'=64] {'pen'}, dimensions={0} | all-to-all | bytes 262144 | tf_op jit(solution)/shard_map/all_to_all | solution.py:548
  51.5 0.6 scatter_groups.1
  52.0 1.3 %collective-permute-start.3 = (f32[128,128]{1,0:T(8,128)S(1)}, f32[128,128]{1,0:T(8,128)S(1)}, u32[]{:S(2)}, u32[]{:S(2)}) collective-permute-start(f32[128,128]{1,0:T(8,128)S(1)} %get-tuple-element.58), channel_id=1, source_target_pairs={{0,128},{64,192},{128,0},{192,64},{1,129},{65,193},{129,1},{193,65... | collective-permute-start | bytes 196616 | tf_op jit(solution)/shard_map/ppermute | solution.py:428
  53.3 2.3 %collective-permute-start.4 = (f32[128,128]{1,0:T(8,128)S(1)}, f32[128,128]{1,0:T(8,128)S(1)}, u32[]{:S(2)}, u32[]{:S(2)}) collective-permute-start(f32[128,128]{1,0:T(8,128)S(1)} %get-tuple-element.59), channel_id=1, source_target_pairs={{0,64},{64,128},{128,192},{192,0},{1,65},{65,129},{129,193},{193,1... | collective-permute-start | bytes 196616 | tf_op jit(solution)/shard_map/ppermute | solution.py:428
  55.7 0.3 collective-permute-start.5
  56.0 0.8 %collective-permute-done.3.first_ref = f32[128,128]{1,0:T(8,128)S(1)} collective-permute-done((f32[128,128]{1,0:T(8,128)S(1)}, f32[128,128]{1,0:T(8,128)S(1)}, u32[]{:S(2)}, u32[]{:S(2)}) %collective-permute-start.3) | collective-permute-done | bytes 65568 | tf_op jit(solution)/shard_map/ppermute | solution.py:428
  56.8 2.1 %collective-permute-done.4.second_ref = f32[128,128]{1,0:T(8,128)S(1)} collective-permute-done((f32[128,128]{1,0:T(8,128)S(1)}, f32[128,128]{1,0:T(8,128)S(1)}, u32[]{:S(2)}, u32[]{:S(2)}) %collective-permute-start.4) | collective-permute-done | bytes 65568 | tf_op jit(solution)/shard_map/ppermute | solution.py:428
  58.8 0.3 collective-permute-done.5.third_ref
  59.2 11.6 %point.1 = bf16[16,64,8,256]{3,2,1,0:T(8,128)(2,1)} custom-call(f32[128,128]{1,0:T(8,128)S(1)} %get-tuple-element.57.own_ref, f32[128,128]{1,0:T(8,128)S(1)} %collective-permute-done.3.first_ref, f32[128,128]{1,0:T(8,128)S(1)} %collective-permute-done.4.second_ref, f32[128,128]{1,0:T(8,128)S(1)} %collective-permute-done.5.third_ref, ...), custom_call_target="tpu_custom_call" | custom-call | tf_op jit(solution)/shard_map/point/pallas_call | solution.py:559
Async XLA Ops:
  3.5 7.2 %collective-permute-start = (f32[128,128]{1,0:T(8,128)S(1)}, f32[128,128]{1,0:T(8,128)S(1)}, u32[]{:S(2)}, u32[]{:S(2)}) collective-permute-start(f32[128,128]{1,0:T(8,128)S(1)} %get-tuple-element.52), channel_id=1, source_target_pairs={{0,128},{64,192},{128,0},{192,64},{1,129},{65,193},{129,1},{193,65... | collective-permute-start | bytes 196616 | tf_op jit(solution)/shard_map/ppermute | solution.py:428
  7.1 5.0 %collective-permute-start.1 = (f32[128,128]{1,0:T(8,128)S(1)}, f32[128,128]{1,0:T(8,128)S(1)}, u32[]{:S(2)}, u32[]{:S(2)}) collective-permute-start(f32[128,128]{1,0:T(8,128)S(1)} %get-tuple-element.53), channel_id=1, source_target_pairs={{0,64},{64,128},{128,192},{192,0},{1,65},{65,129},{129,193},{193,1... | collective-permute-start | bytes 196616 | tf_op jit(solution)/shard_map/ppermute | solution.py:428
  7.4 4.7 %collective-permute-start.2 = (f32[128,128]{1,0:T(8,128)S(1)}, f32[128,128]{1,0:T(8,128)S(1)}, u32[]{:S(2)}, u32[]{:S(2)}) collective-permute-start(f32[128,128]{1,0:T(8,128)S(1)} %get-tuple-element.54), channel_id=1, source_target_pairs={{0,192},{64,0},{128,64},{192,128},{1,193},{65,1},{129,65},{193,129... | collective-permute-start | bytes 196616 | tf_op jit(solution)/shard_map/ppermute | solution.py:428
  52.0 4.7 %collective-permute-start.3 = (f32[128,128]{1,0:T(8,128)S(1)}, f32[128,128]{1,0:T(8,128)S(1)}, u32[]{:S(2)}, u32[]{:S(2)}) collective-permute-start(f32[128,128]{1,0:T(8,128)S(1)} %get-tuple-element.58), channel_id=1, source_target_pairs={{0,128},{64,192},{128,0},{192,64},{1,129},{65,193},{129,1},{193,65... | collective-permute-start | bytes 196616 | tf_op jit(solution)/shard_map/ppermute | solution.py:428
  53.3 5.5 %collective-permute-start.4 = (f32[128,128]{1,0:T(8,128)S(1)}, f32[128,128]{1,0:T(8,128)S(1)}, u32[]{:S(2)}, u32[]{:S(2)}) collective-permute-start(f32[128,128]{1,0:T(8,128)S(1)} %get-tuple-element.59), channel_id=1, source_target_pairs={{0,64},{64,128},{128,192},{192,0},{1,65},{65,129},{129,193},{193,1... | collective-permute-start | bytes 196616 | tf_op jit(solution)/shard_map/ppermute | solution.py:428
  55.7 3.5 %collective-permute-start.5 = (f32[128,128]{1,0:T(8,128)S(1)}, f32[128,128]{1,0:T(8,128)S(1)}, u32[]{:S(2)}, u32[]{:S(2)}) collective-permute-start(f32[128,128]{1,0:T(8,128)S(1)} %get-tuple-element.60), channel_id=1, source_target_pairs={{0,192},{64,0},{128,64},{192,128},{1,193},{65,1},{129,65},{193,129... | collective-permute-start | bytes 196616 | tf_op jit(solution)/shard_map/ppermute | solution.py:428

commit v8 on v7

--- a/solution.py
+++ b/solution.py
@@ -332,10 +332,10 @@
             tile = encoded[:, half * 256 : half * 256 + 256]
             out_ref[:, sub * 2 + half] = tile.reshape(16, 8, 256)
 
-    def transform(pair):
+    def transform(pair, count):
         own = jnp.where(iota((16, 256), 0) % 8 == iota((16, 256), 1) % 8, 1.0, 0.0).astype(bf16)
         left = []
-        for row in range(16):
+        for row in range(count):
             base = pl.multiple_of(pair * 16, 16) + row
             rows = [planes_ref[t, pl.ds(base, 8, stride=0), :] for t in range(4)]
             block = jnp.concatenate(
@@ -387,16 +387,17 @@
             full = full.astype(bf16).astype(f32)
             planes_ref[c_hi * 2, 0:ROWS] = full[:, 0:128]
             planes_ref[c_hi * 2 + 1, 0:ROWS] = full[:, 128:256]
+        both = transform(0, 32)
         for slot in range(2):
             act_ref[slot, 128:144] = jnp.ones((16, 512), bf16)
-            activate(transform(slot), slot, slot)
+            activate(both[slot * 256 : slot * 256 + 256], slot, slot)
         expand(0)
 
     @pl.when(step < STEPS - 1)
     def _():
         for sub in range(ZB // 2):
             pair = step * (ZB // 2) + sub + 2
-            spatial = transform(pair)
+            spatial = transform(pair, 16)
             expand(1 - sub % 2)
             finish(sub)
             activate(spatial, pair, sub % 2)
@@ -406,7 +407,7 @@
         for sub in range(ZB // 2):
             pair = step * (ZB // 2) + sub + 2
             if sub < ZB // 2 - 2:
-                spatial = transform(pair)
+                spatial = transform(pair, 16)
             if sub < ZB // 2 - 1:
                 expand(1 - sub % 2)
             finish(sub)

time: 70.9 us -> 71 us (level)
  no operation moved by 1% of the time
where the time goes in v8:
time: 71 us; the launch traced here: 70.8 us
  blocking collectives  38.2 us (54%)
  Pallas kernels  17.5 us (25%)
  starting transfers between devices  10.3 us (15%)
  waiting for transfers between devices  4.68 us (7%)
    all_to_all x1, blocking collectives, shards(): chunks = lax.all_to_all(chunks.reshape(64, 4, 128), 'pen', 0, 0, tiled=True)  23.2 us
    all_to_all x1, blocking collectives, shards(): mixed = lax.all_to_all(mixed.reshape(64, 4, 128), 'pen', 0, 0, tiled=True)  15 us
    pallas_call x1, Pallas kernels, shards(): pl.pallas_call(point_kernel, out_shape=shape((CH, LZ, LX, NY), bf16), gri...  11.6 us
    ppermute x6, starting transfers between devices, rotate(): lax.ppermute(tile, 'grp', [(i, (i + k) % 4) for i in range(4)])  10.3 us
    ppermute x6, waiting for transfers between devices, rotate(): lax.ppermute(tile, 'grp', [(i, (i + k) % 4) for i in range(4)])  4.68 us
    pallas_call x1, Pallas kernels, shards(): pl.pallas_call(forward_kernel, out_shape=[shape((128, 128), f32)] * 4 + [...  3.45 us
  transfers between devices with their start and end apart: 6, of which 4 were waited for; matrix products, arithmetic and copies ran while one was open for 0% of the time, Pallas kernels for 1%

profile of v8, /device:TPU:1, one launch (start us, length us, event | category | flops | bytes accessed | tf_op | source)
XLA Modules:
  0.0 70.8 jit_solution(15001809090249738102)
XLA Ops:
  0.0 3.4 %forward.1 = (f32[128,128]{1,0:T(8,128)S(1)}, f32[128,128]{1,0:T(8,128)S(1)}, f32[128,128]{1,0:T(8,128)S(1)}, f32[128,128]{1,0:T(8,128)S(1)}, s32[2,520,128]{2,1...) custom-call(s32[512,256]{1,0:T(8,128)} %bitcast.14, ...), custom_call_target="tpu_custom_call" | custom-call | flops 400000000 | bytes 3000000 | tf_op jit(solution)/shard_map/forward/pallas_call | solution.py:474
  3.5 3.7 %collective-permute-start = (f32[128,128]{1,0:T(8,128)S(1)}, f32[128,128]{1,0:T(8,128)S(1)}, u32[]{:S(2)}, u32[]{:S(2)}) collective-permute-start(f32[128,128]{1,0:T(8,128)S(1)} %get-tuple-element.52), channel_id=1, source_target_pairs={{0,128},{64,192},{128,0},{192,64},{1,129},{65,193},{129,1},{193,65... | collective-permute-start | bytes 196616 | tf_op jit(solution)/shard_map/ppermute | solution.py:429
  7.1 0.3 collective-permute-start.1
  7.4 2.4 %collective-permute-start.2 = (f32[128,128]{1,0:T(8,128)S(1)}, f32[128,128]{1,0:T(8,128)S(1)}, u32[]{:S(2)}, u32[]{:S(2)}) collective-permute-start(f32[128,128]{1,0:T(8,128)S(1)} %get-tuple-element.54), channel_id=1, source_target_pairs={{0,192},{64,0},{128,64},{192,128},{1,193},{65,1},{129,65},{193,129... | collective-permute-start | bytes 196616 | tf_op jit(solution)/shard_map/ppermute | solution.py:429
  9.8 0.8 %prepare.1 = (f32[128,128]{1,0:T(8,128)S(1)}, f32[512,128]{1,0:T(8,128)S(1)}, f32[2,16,128]{2,1,0:T(8,128)S(1)}, f32[16,128]{1,0:T(8,128)S(1)}, bf16[512,256]{1,...) custom-call(f32[12,16]{1,0:T(8,128)S(1)} %get-tuple-element.37.emb_v, ...), custom_call_target="tpu_custom_call" | custom-call | flops 200000000 | bytes 1000000 | tf_op jit(solution)/shard_map/prepare/pallas_call | solution.py:513
  10.6 0.0 collective-permute-done.first_ref
  10.7 1.5 %collective-permute-done.1.second_ref = f32[128,128]{1,0:T(8,128)S(1)} collective-permute-done((f32[128,128]{1,0:T(8,128)S(1)}, f32[128,128]{1,0:T(8,128)S(1)}, u32[]{:S(2)}, u32[]{:S(2)}) %collective-permute-start.1) | collective-permute-done | bytes 65568 | tf_op jit(solution)/shard_map/ppermute | solution.py:429
  12.2 0.0 collective-permute-done.2.third_ref
  12.2 0.6 gather_groups.1
  12.8 23.2 %all_to_all.10 = f32[64,4,128]{2,1,0:T(4,128)S(1)} all-to-all(f32[64,4,128]{2,1,0:T(4,128)S(1)} %bitcast.11), channel_id=1, replica_groups=mesh['grp'=4,'pen'=64] {'pen'}, dimensions={0} | all-to-all | bytes 262144 | tf_op jit(solution)/shard_map/all_to_all | solution.py:540
  36.0 0.4 mix.1
  36.4 15.0 %all_to_all.11 = f32[64,4,128]{2,1,0:T(4,128)S(1)} all-to-all(f32[64,4,128]{2,1,0:T(4,128)S(1)} %bitcast.13), channel_id=1, replica_groups=mesh['grp'=4,'pen'=64] {'pen'}, dimensions={0} | all-to-all | bytes 262144 | tf_op jit(solution)/shard_map/all_to_all | solution.py:549
  51.5 0.6 scatter_groups.1
  52.0 1.3 %collective-permute-start.3 = (f32[128,128]{1,0:T(8,128)S(1)}, f32[128,128]{1,0:T(8,128)S(1)}, u32[]{:S(2)}, u32[]{:S(2)}) collective-permute-start(f32[128,128]{1,0:T(8,128)S(1)} %get-tuple-element.58), channel_id=1, source_target_pairs={{0,128},{64,192},{128,0},{192,64},{1,129},{65,193},{129,1},{193,65... | collective-permute-start | bytes 196616 | tf_op jit(solution)/shard_map/ppermute | solution.py:429
  53.3 2.3 %collective-permute-start.4 = (f32[128,128]{1,0:T(8,128)S(1)}, f32[128,128]{1,0:T(8,128)S(1)}, u32[]{:S(2)}, u32[]{:S(2)}) collective-permute-start(f32[128,128]{1,0:T(8,128)S(1)} %get-tuple-element.59), channel_id=1, source_target_pairs={{0,64},{64,128},{128,192},{192,0},{1,65},{65,129},{129,193},{193,1... | collective-permute-start | bytes 196616 | tf_op jit(solution)/shard_map/ppermute | solution.py:429
  55.7 0.3 collective-permute-start.5
  56.0 0.8 %collective-permute-done.3.first_ref = f32[128,128]{1,0:T(8,128)S(1)} collective-permute-done((f32[128,128]{1,0:T(8,128)S(1)}, f32[128,128]{1,0:T(8,128)S(1)}, u32[]{:S(2)}, u32[]{:S(2)}) %collective-permute-start.3) | collective-permute-done | bytes 65568 | tf_op jit(solution)/shard_map/ppermute | solution.py:429
  56.8 2.1 %collective-permute-done.4.second_ref = f32[128,128]{1,0:T(8,128)S(1)} collective-permute-done((f32[128,128]{1,0:T(8,128)S(1)}, f32[128,128]{1,0:T(8,128)S(1)}, u32[]{:S(2)}, u32[]{:S(2)}) %collective-permute-start.4) | collective-permute-done | bytes 65568 | tf_op jit(solution)/shard_map/ppermute | solution.py:429
  58.8 0.3 collective-permute-done.5.third_ref
  59.2 11.6 %point.1 = bf16[16,64,8,256]{3,2,1,0:T(8,128)(2,1)} custom-call(f32[128,128]{1,0:T(8,128)S(1)} %get-tuple-element.57.own_ref, f32[128,128]{1,0:T(8,128)S(1)} %collective-permute-done.3.first_ref, f32[128,128]{1,0:T(8,128)S(1)} %collective-permute-done.4.second_ref, f32[128,128]{1,0:T(8,128)S(1)} %collective-permute-done.5.third_ref, ...), custom_call_target="tpu_custom_call" | custom-call | tf_op jit(solution)/shard_map/point/pallas_call | solution.py:560
Async XLA Ops:
  3.5 7.2 %collective-permute-start = (f32[128,128]{1,0:T(8,128)S(1)}, f32[128,128]{1,0:T(8,128)S(1)}, u32[]{:S(2)}, u32[]{:S(2)}) collective-permute-start(f32[128,128]{1,0:T(8,128)S(1)} %get-tuple-element.52), channel_id=1, source_target_pairs={{0,128},{64,192},{128,0},{192,64},{1,129},{65,193},{129,1},{193,65... | collective-permute-start | bytes 196616 | tf_op jit(solution)/shard_map/ppermute | solution.py:429
  7.1 5.0 %collective-permute-start.1 = (f32[128,128]{1,0:T(8,128)S(1)}, f32[128,128]{1,0:T(8,128)S(1)}, u32[]{:S(2)}, u32[]{:S(2)}) collective-permute-start(f32[128,128]{1,0:T(8,128)S(1)} %get-tuple-element.53), channel_id=1, source_target_pairs={{0,64},{64,128},{128,192},{192,0},{1,65},{65,129},{129,193},{193,1... | collective-permute-start | bytes 196616 | tf_op jit(solution)/shard_map/ppermute | solution.py:429
  7.4 4.7 %collective-permute-start.2 = (f32[128,128]{1,0:T(8,128)S(1)}, f32[128,128]{1,0:T(8,128)S(1)}, u32[]{:S(2)}, u32[]{:S(2)}) collective-permute-start(f32[128,128]{1,0:T(8,128)S(1)} %get-tuple-element.54), channel_id=1, source_target_pairs={{0,192},{64,0},{128,64},{192,128},{1,193},{65,1},{129,65},{193,129... | collective-permute-start | bytes 196616 | tf_op jit(solution)/shard_map/ppermute | solution.py:429
  52.0 4.7 %collective-permute-start.3 = (f32[128,128]{1,0:T(8,128)S(1)}, f32[128,128]{1,0:T(8,128)S(1)}, u32[]{:S(2)}, u32[]{:S(2)}) collective-permute-start(f32[128,128]{1,0:T(8,128)S(1)} %get-tuple-element.58), channel_id=1, source_target_pairs={{0,128},{64,192},{128,0},{192,64},{1,129},{65,193},{129,1},{193,65... | collective-permute-start | bytes 196616 | tf_op jit(solution)/shard_map/ppermute | solution.py:429
  53.3 5.5 %collective-permute-start.4 = (f32[128,128]{1,0:T(8,128)S(1)}, f32[128,128]{1,0:T(8,128)S(1)}, u32[]{:S(2)}, u32[]{:S(2)}) collective-permute-start(f32[128,128]{1,0:T(8,128)S(1)} %get-tuple-element.59), channel_id=1, source_target_pairs={{0,64},{64,128},{128,192},{192,0},{1,65},{65,129},{129,193},{193,1... | collective-permute-start | bytes 196616 | tf_op jit(solution)/shard_map/ppermute | solution.py:429
  55.7 3.5 %collective-permute-start.5 = (f32[128,128]{1,0:T(8,128)S(1)}, f32[128,128]{1,0:T(8,128)S(1)}, u32[]{:S(2)}, u32[]{:S(2)}) collective-permute-start(f32[128,128]{1,0:T(8,128)S(1)} %get-tuple-element.60), channel_id=1, source_target_pairs={{0,192},{64,0},{128,64},{192,128},{1,193},{65,1},{129,65},{193,129... | collective-permute-start | bytes 196616 | tf_op jit(solution)/shard_map/ppermute | solution.py:429
